TPU v7x, 256 devices: a whole 4x4x8 slice. The times are simulated.
256 devices in a mesh: gz: 8 (over x, core), ma: 32 (over z, y).
Axes of the slice: x: 4, y: 4, z: 8, core: 2. Of those that a mesh axis runs over, the one named last changes fastest.
Arguments:
- forward: float32 [8, 2, 1024, 4096], P('gz', None, 'ma'), may hold values from -6 to 6
- cotangent: float32 [8, 2, 1024, 4096], P('gz', None, 'ma'), may hold values from -6 to 6
- mode_order: int32 [1024], replicated, may hold values from 0 to 1023, each once
- region: int32 [128, 128], replicated, may hold values from 0 to 7
- chi: float32 [8], replicated, may hold values from 0.5 to 2
- phase: float32 [1024, 4096], P('ma'), may hold values from -3.140625 to 3.140625
- loss: float32 [8, 1024], P('gz', 'ma'), may hold values from 0.5 to 1
Outputs:
- adjoint: float32 [8, 2, 1024, 4096], P('gz', None, 'ma')
Inputs may be any that keep to these rules, and one draw needn't show every extreme that they name: Each number appears once; stored mode m has order mode_order[m] // 32 along the first transverse coordinate and mode_order[m] % 32 along the second.
All inputs are finite; a program needn't handle non-finite values.
Results may differ from a plain program's by a relative error of at most 0.0003.
Values sent between devices are 32-bit elements; how exact they have to be, the bound alone decides.
No kernel may reach another device: no remote copies, remote signals or barrier semaphores. Data moves between devices by JAX's collectives and lax.ppermute only.
A program may use at most 128 MiB of HBM per device.

v0:
```python
import math

import jax
import jax.numpy as jnp
import numpy as np
from jax import lax
from jax.experimental import pallas as pl
from jax.experimental.pallas import tpu as pltpu
from jax.sharding import PartitionSpec as P

ORDER = 32
MODES = 1024
GRID = 128
REGIONS = 8
TIME = 4096
BLOCK = 128
OUTER = 32
ZL = 8
PER = 4
BF = jnp.bfloat16
F32 = jnp.float32


def hermite_table():
    step = 20.0 / GRID
    coords = (np.arange(GRID, dtype=np.float64) - (GRID - 1) / 2.0) * step
    columns = [np.exp(-0.5 * coords * coords) * math.pi ** (-0.25)]
    columns.append(math.sqrt(2.0) * coords * columns[0])
    for n in range(2, ORDER):
        columns.append(
            math.sqrt(2.0 / n) * coords * columns[n - 1]
            - math.sqrt((n - 1.0) / n) * columns[n - 2]
        )
    return np.stack(columns, axis=1) * math.sqrt(step)


def halves(array):
    head = array.astype(jnp.bfloat16)
    tail = (array - head.astype(np.float64)).astype(jnp.bfloat16)
    return head, tail


def split(value):
    head = value.astype(BF)
    return head, (value - head.astype(F32)).astype(BF)


def dot(a, b):
    return jnp.dot(a, b, preferred_element_type=F32)


def kerr_kernel(x_ref, place_ref, back_ref, fwd_ref, proj_ref, tt_ref, k_ref, o_ref,
                xs, fs, gs, rs, ks):
    def split_in(j, carry):
        rows = pl.ds(pl.multiple_of(j * 32, 32), 32)
        for f in range(4):
            head, tail = split(x_ref[j, f])
            xs[f, rows, 0:128] = head
            xs[f, rows, 128:256] = tail
        return carry

    lax.fori_loop(0, 32, split_in, 0, unroll=4)

    def place(f, carry):
        fs[f] = dot(place_ref[...], xs[f]).astype(BF)
        return carry

    lax.fori_loop(0, 4, place, 0)

    def first(p, carry):
        rows = pl.ds(pl.multiple_of(p * 32, 32), 32)
        out_rows = pl.ds(pl.multiple_of(p * 128, 128), 128)
        for pair in range(2):
            a, b = fs[2 * pair, rows, :], fs[2 * pair + 1, rows, :]
            head = jnp.concatenate([a[:, :128], b[:, :128]], axis=1)
            tail = jnp.concatenate([a[:, 128:], b[:, 128:]], axis=1)
            got = dot(fwd_ref[...], jnp.concatenate([head, tail, head], axis=0))
            gs[2 * pair, out_rows, :] = got[:, :128]
            gs[2 * pair + 1, out_rows, :] = got[:, 128:]
        return carry

    lax.fori_loop(0, 32, first, 0, unroll=2)

    def column(y, carry):
        fields = []
        for pair in range(2):
            got = [split(gs[2 * pair + c, pl.ds(y, 32, stride=128), :]) for c in range(2)]
            head = jnp.concatenate([got[0][0], got[1][0]], axis=1)
            tail = jnp.concatenate([got[0][1], got[1][1]], axis=1)
            fields.append(dot(fwd_ref[...], jnp.concatenate([head, tail, head], axis=0)))
        er, ei = fields[0][:, :128], fields[0][:, 128:]
        cr, ci = fields[1][:, :128], fields[1][:, 128:]
        rr, ii, ri = er * er, ei * ei, er * ei
        cross = ri + ri
        total = rr + ii
        gr = (total + (rr + rr)) * ci - cross * cr
        gi = cross * ci - (total + (ii + ii)) * cr
        gr_h, gr_l = split(gr)
        gi_h, gi_l = split(gi)
        right = jnp.concatenate(
            [jnp.concatenate([gr_h, gi_h], axis=1), jnp.concatenate([gr_l, gi_l], axis=1)], axis=0
        )
        t_h, t_l = split(tt_ref[...] * k_ref[pl.ds(y, 1), :])
        left = jnp.concatenate(
            [jnp.concatenate([t_h, t_h], axis=1), jnp.concatenate([t_l, jnp.zeros_like(t_l)], axis=1)],
            axis=0,
        )
        got = dot(left, right)
        got = got[:32] + got[32:]
        rows = pl.ds(pl.multiple_of(y * 32, 32), 32)
        rs[0, rows, :] = got[:, :128]
        rs[1, rows, :] = got[:, 128:]
        return carry

    lax.fori_loop(0, GRID, column, 0, unroll=2)

    def last(p, carry):
        got = [split(rs[c, pl.ds(p, 128, stride=32), :]) for c in range(2)]
        right = jnp.concatenate(
            [jnp.concatenate([got[0][i], got[1][i]], axis=1) for i in range(2)], axis=0
        )
        res = dot(proj_ref[...], right)
        res = res[:32] + res[32:]
        rows = pl.ds(pl.multiple_of(p * 32, 32), 32)
        for c in range(2):
            head, tail = split(res[:, c * 128:(c + 1) * 128])
            ks[c, rows, 0:128] = head
            ks[c, rows, 128:256] = tail
        return carry

    lax.fori_loop(0, 32, last, 0, unroll=2)

    def finish(j, carry):
        rows = pl.ds(pl.multiple_of(j * 256, 256), 256)
        for c in range(2):
            res = dot(back_ref[rows, :], ks[c])
            res = res[:, :128] + res[:, 128:]
            for i in range(8):
                value = res[i * 32:(i + 1) * 32] + x_ref[j * 8 + i, 2 + c]
                for g in range(8):
                    o_ref[g, j * 8 + i, c * 4:(c + 1) * 4, :] = value[g * 4:(g + 1) * 4]
        return carry

    lax.fori_loop(0, 4, finish, 0)


def kerr_call(received, place, back, fwd, proj, tt, k):
    vm = pl.BlockSpec(memory_space=pltpu.VMEM)
    return pl.pallas_call(
        kerr_kernel,
        name="kerr",
        out_shape=jax.ShapeDtypeStruct((ZL, 32, 8, 128), F32),
        in_specs=[vm] * 7,
        out_specs=vm,
        scratch_shapes=[
            pltpu.VMEM((4, MODES, 256), BF),
            pltpu.VMEM((4, MODES, 256), BF),
            pltpu.VMEM((4, ORDER * GRID, 128), F32),
            pltpu.VMEM((2, ORDER * GRID, 128), F32),
            pltpu.VMEM((2, MODES, 256), BF),
        ],
        compiler_params=pltpu.CompilerParams(vmem_limit_bytes=48 * 2**20),
        cost_estimate=pl.CostEstimate(flops=2 * 10**10, bytes_accessed=8 * 2**20, transcendentals=0),
    )(received, place, back, fwd, proj, tt, k)


def three(a_h, a_l, b_h, b_l):
    return dot(a_h, b_h) + (dot(a_h, b_l) + dot(a_l, b_h))


def spectral_kernel(s_ref, l_ref, ph_ref, w1_ref, w2_ref, w3_ref, w4_ref, tw_ref, o_ref, sc):
    for z in range(ZL - 1, -1, -1):
        if z == ZL - 1:
            sc[z] = s_ref[z]
        else:
            sc[z] = s_ref[z] + l_ref[z] * sc[z + 1]
    tw_r = jnp.concatenate([tw_ref[0]] * PER, axis=0)
    tw_i = jnp.concatenate([tw_ref[1]] * PER, axis=0)
    ph_r, ph_i = ph_ref[0], ph_ref[1]

    def pair(j, carry):
        z0 = 2 * j
        a = jnp.concatenate(
            [sc[z0].reshape(256, 128), sc[z0 + 1].reshape(256, 128)], axis=1
        )
        a_h, a_l = split(a)
        first = three(w1_ref[0], w1_ref[1], a_h, a_l)
        outs = []
        for i in range(2):
            re, im = first[:128, i * 128:(i + 1) * 128], first[128:, i * 128:(i + 1) * 128]
            seg = jnp.concatenate([re * tw_r - im * tw_i, re * tw_i + im * tw_r], axis=1)
            s_h, s_l = split(seg)
            spec = three(s_h, s_l, w2_ref[0], w2_ref[1])
            re, im = spec[:, :128], spec[:, 128:]
            spec = jnp.concatenate([re * ph_r - im * ph_i, re * ph_i + im * ph_r], axis=1)
            s_h, s_l = split(spec)
            seg = three(s_h, s_l, w3_ref[0], w3_ref[1])
            re, im = seg[:, :128], seg[:, 128:]
            outs.append(
                jnp.concatenate([re * tw_r + im * tw_i, im * tw_r - re * tw_i], axis=0)
            )
        b_h, b_l = split(jnp.concatenate(outs, axis=1))
        final = three(w4_ref[0], w4_ref[1], b_h, b_l)
        o_ref[z0] = final[:, :128]
        o_ref[z0 + 1] = final[:, 128:]
        return carry

    lax.fori_loop(0, ZL // 2, pair, 0)


def spectral_constants():
    a = np.arange(OUTER)
    ang1 = 2 * math.pi / OUTER * (np.outer(a, a) % OUTER)
    c1, s1 = np.cos(ang1), np.sin(ang1)
    eye = np.eye(PER)
    w1 = np.zeros((2, PER, OUTER, OUTER, 2, PER))
    blocks = {(0, 0): c1, (0, 1): s1, (1, 0): -s1, (1, 1): c1}
    for (co, ci), m in blocks.items():
        w1[co, :, :, :, ci, :] = np.einsum("mn,ka->mkan", eye, m)
    w1 = w1.reshape(256, 256)
    w4 = np.zeros((OUTER, 2, PER, 2, PER, OUTER))
    blocks = {(0, 0): c1, (0, 1): -s1, (1, 0): s1, (1, 1): c1}
    for (co, ci), m in blocks.items():
        w4[:, co, :, ci, :, :] = np.einsum("mn,ka->amnk", eye, m)
    w4 = w4.reshape(256, 256) / TIME
    b = np.arange(BLOCK)
    ang2 = 2 * math.pi / BLOCK * (np.outer(b, b) % BLOCK)
    c2, s2 = np.cos(ang2), np.sin(ang2)
    w2 = np.block([[c2, -s2], [s2, c2]])
    w3 = np.block([[c2, s2], [-s2, c2]])
    angt = 2 * math.pi / TIME * (np.outer(a, b) % TIME)
    tw = np.stack([np.cos(angt), -np.sin(angt)]).astype(np.float32)
    return [np.stack(halves(w)) for w in (w1, w2, w3, w4)] + [tw]


def spectral_call(source, factors, turn):
    w1, w2, w3, w4, tw = spectral_constants()
    vm = pl.BlockSpec(memory_space=pltpu.VMEM)
    return pl.pallas_call(
        spectral_kernel,
        name="spectral",
        out_shape=jax.ShapeDtypeStruct((ZL, 256, 128), F32),
        in_specs=[vm] * 8,
        out_specs=vm,
        scratch_shapes=[pltpu.VMEM((ZL, OUTER, 8, 128), F32)],
        compiler_params=pltpu.CompilerParams(vmem_limit_bytes=32 * 2**20),
        cost_estimate=pl.CostEstimate(flops=3 * 10**9, bytes_accessed=4 * 2**20, transcendentals=0),
    )(source, factors, turn, w1, w2, w3, w4, tw)


def gathered_loss(loss):
    size = lax.axis_size("gz")
    have = loss
    reach = 1
    while reach < size:
        route = [((i + reach) % size, i) for i in range(size)]
        have = jnp.concatenate([have, lax.ppermute(have, "gz", route)], axis=0)
        reach *= 2
    me = lax.axis_index("gz")
    return lax.dynamic_slice_in_dim(jnp.concatenate([have, have], axis=0), size - me, size, 0)


def kerr_constants(mode_order, region, chi):
    t = hermite_table()
    t_h, t_l = halves(t)
    fwd = np.concatenate([t_h, t_h, t_l], axis=1)
    proj = np.concatenate(
        [np.concatenate([t_h.T, t_h.T], axis=1), np.concatenate([t_l.T, np.zeros_like(t_l.T)], axis=1)],
        axis=0,
    )
    tt = np.ascontiguousarray(t.T).astype(np.float32)
    matches = (region[None, :, :] == jnp.arange(REGIONS, dtype=jnp.int32)[:, None, None]).astype(F32)
    k = 2.0 * jnp.sum(matches * chi[:, None, None], axis=0).T
    index = jnp.arange(MODES, dtype=jnp.int32)
    place = (index[:, None] == mode_order[None, :]).astype(BF)
    back = (mode_order[:, None] == index[None, :]).astype(BF)
    return place, back, fwd, proj, tt, k


def on_device(forward, cotangent, mode_order, region, chi, phase, loss):
    me = lax.axis_index("gz")
    both = jnp.concatenate([forward[0], cotangent[0]], axis=0)
    send = both.reshape(4, 32, 32, BLOCK).transpose(2, 0, 1, 3)
    received = lax.all_to_all(send, "ma", split_axis=0, concat_axis=0, tiled=True)
    constants = kerr_constants(mode_order, region, chi)
    source = kerr_call(received, *constants)
    source = source.reshape(256, 8, 128)
    gathered = lax.all_to_all(source, ("gz", "ma"), split_axis=0, concat_axis=0, tiled=True)
    factors = lax.dynamic_slice_in_dim(gathered_loss(loss), me * PER, PER, 1)
    factors = jnp.concatenate([factors, factors], axis=1)
    factors = jnp.broadcast_to(factors[:, None, :, None], (ZL, 1, 8, 128))
    angles = lax.dynamic_slice_in_dim(phase, me * PER, PER, 0)
    angles = angles.reshape(PER, BLOCK, OUTER).transpose(0, 2, 1).reshape(PER * OUTER, BLOCK)
    turn = jnp.stack([jnp.cos(angles), -jnp.sin(angles)])
    result = spectral_call(gathered.reshape(ZL, OUTER, 8, 128), factors, turn)
    result = lax.all_to_all(result, "gz", split_axis=0, concat_axis=0, tiled=True)
    result = result.reshape(8, OUTER, 2, PER, BLOCK).transpose(2, 0, 3, 1, 4)
    return result.reshape(1, 2, 32, TIME)


def solution(mesh):
    in_specs = (
        P("gz", None, "ma", None),
        P("gz", None, "ma", None),
        P(),
        P(),
        P(),
        P("ma", None),
        P("gz", "ma"),
    )
    return jax.shard_map(
        on_device, mesh=mesh, in_specs=in_specs, out_specs=P("gz", None, "ma", None), check_vma=False
    )
```

profile of v0, /device:TPU:1, one launch (start us, length us, event | category | flops | bytes accessed | tf_op | source)
XLA Modules:
  0.0 186.4 jit_solution(18009225767140270354)
XLA Ops:
  0.0 1.5 copy.31
  1.5 0.6 copy.25
  2.1 0.2 copy.30
  2.3 0.6 copy.24
  2.9 1.5 maximum_bitcast_fusion
  4.5 12.2 %all-to-all-start = ((f32[32,4,32,128]{3,2,1,0:T(8,128)}), f32[32,4,32,128]{3,2,1,0:T(8,128)S(1)}, u32[]{:S(2)}, u32[]{:S(2)}) async-start(f32[32,4,32,128]{3,2,1,0:T(8,128)} %maximum_bitcast_fusion), calls=%async_computation | async-start | bytes 4194304 | tf_op jit(solution)/shard_map/all_to_all | solution.py:284
  16.9 2.6 %fusion.1 = (bf16[1024,1024]{1,0:T(8,128)(2,1)}, bf16[1024,1024]{1,0:T(8,128)(2,1)}) fusion(s32[1024]{0:T(1024)S(1)} %copy-done.11), kind=kLoop, calls=%fused_computation.3 | loop fusion | flops 4194304 | bytes 4198400 | tf_op jit(solution)/shard_map/convert_element_type | solution.py:276
  19.6 45.5 %all-to-all-done.x_ref = f32[32,4,32,128]{3,2,1,0:T(8,128)S(1)} async-done(((f32[32,4,32,128]{3,2,1,0:T(8,128)}), f32[32,4,32,128]{3,2,1,0:T(8,128)S(1)}, u32[]{:S(2)}, u32[]{:S(2)}) %all-to-all-start) | async-done | bytes 2097184 | tf_op jit(solution)/shard_map/all_to_all | solution.py:284
  65.1 1.6 copy-done
  66.7 52.6 %kerr.1 = f32[8,32,8,128]{3,2,1,0:T(8,128)} custom-call(f32[32,4,32,128]{3,2,1,0:T(8,128)S(1)} %all-to-all-done.x_ref, bf16[1024,1024]{1,0:T(8,128)(2,1)S(1)} %copy-done, bf16[1024,1024]{1,0:T(8,128)(2,1)} %get-tuple-element.7.back_ref, bf16[128,96]{1,0:T(8,128)(2,1)S(1)} %copy-done.6, bf16[64,256]{1,0:T(8,128)(2,1)S(1)} %copy-done.7, ...), custom_call_target="tpu_custom_call" | custom-call | flops 20000000000 | bytes 8388608 | tf_op jit(solution)/shard_map/kerr/pallas_call | solution.py:149
  119.4 11.2 %all-to-all-start.1 = ((f32[256,8,128]{2,1,0:T(8,128)}), f32[256,8,128]{2,1,0:T(8,128)S(1)}, u32[]{:S(2)}, u32[]{:S(2)}) async-start(f32[256,8,128]{2,1,0:T(8,128)} %bitcast.2), calls=%async_computation.1 | async-start | bytes 2097152 | tf_op jit(solution)/shard_map/all_to_all | solution.py:288
  130.6 2.2 %collective-permute-start = (f32[1,32]{1,0:T(1,128)S(1)}, f32[1,32]{1,0:T(1,128)S(1)}, u32[]{:S(2)}, u32[]{:S(2)}) collective-permute-start(f32[1,32]{1,0:T(1,128)S(1)} %copy-done.12), channel_id=1, source_target_pairs={{32,0},{64,32},{96,64},{128,96},{160,128},{192,160},{224,192},{0,2... | collective-permute-start | bytes 392 | tf_op jit(solution)/shard_map/ppermute | solution.py:257
  132.8 1.4 dynamic-slice_cosine_fusion
  134.2 0.1 neg.20
  134.3 3.5 %collective-permute-start.1 = (f32[2,32]{1,0:T(2,128)S(1)}, f32[2,32]{1,0:T(2,128)S(1)}, u32[]{:S(2)}, u32[]{:S(2)}) collective-permute-start(f32[2,32]{1,0:T(2,128)S(1)} %pad_maximum_fusion.3), channel_id=1, source_target_pairs={{64,0},{96,32},{128,64},{160,96},{192,128},{224,160},{0,192},{32,2... | collective-permute-start | bytes 776 | tf_op jit(solution)/shard_map/ppermute | solution.py:257
  137.9 0.1 cos.20
  138.1 0.4 collective-permute-done.1
  138.5 1.8 collective-permute-start.2
  140.4 2.5 %collective-permute-done.2 = f32[4,32]{1,0:T(4,128)S(1)} collective-permute-done((f32[4,32]{1,0:T(4,128)S(1)}, f32[4,32]{1,0:T(4,128)S(1)}, u32[]{:S(2)}, u32[]{:S(2)}) %collective-permute-start.2) | collective-permute-done | bytes 544 | tf_op jit(solution)/shard_map/ppermute | solution.py:257
  143.1 18.8 %all-to-all-done.1 = f32[256,8,128]{2,1,0:T(8,128)S(1)} async-done(((f32[256,8,128]{2,1,0:T(8,128)}), f32[256,8,128]{2,1,0:T(8,128)S(1)}, u32[]{:S(2)}, u32[]{:S(2)}) %all-to-all-start.1) | async-done | bytes 1048608 | tf_op jit(solution)/shard_map/all_to_all | solution.py:288
  162.0 4.6 %spectral.1 = f32[8,256,128]{2,1,0:T(8,128)S(1)} custom-call(f32[8,32,8,128]{3,2,1,0:T(8,128)S(1)} %bitcast.25, f32[8,1,8,128]{3,2,1,0:T(8,128)S(1)} %broadcast_in_dim.2.l_ref, f32[2,128,128]{2,1,0:T(8,128)S(1)} %pad_maximum_fusion.ph_ref, bf16[2,256,256]{2,1,0:T(8,128)(2,1)S(1)} %copy-done.1, bf16[2,256,256]{2,1,0:T(8,128)(2,1)S(1)} %copy-done.2, ...), custom_call_target="tpu_custom_call" | custom-call | flops 3000000000 | bytes 4194304 | tf_op jit(solution)/shard_map/spectral/pallas_call | solution.py:239
  166.6 18.4 %all_to_all.15 = f32[8,256,128]{2,1,0:T(8,128)S(1)} all-to-all(f32[8,256,128]{2,1,0:T(8,128)S(1)} %spectral.1), channel_id=1, replica_groups=mesh['gz'=8,'ma'=32] {'gz'}, dimensions={0} | all-to-all | bytes 2097152 | tf_op jit(solution)/shard_map/all_to_all | solution.py:296
  185.0 0.2 copy.29
  185.2 1.2 reshape.58
  (40 shorter events, 0.8 us)
Async XLA Ops:
  0.0 2.1 %copy-start.9 = (f32[1,2,32,4096]{3,2,1,0:T(8,128)S(1)}, f32[1,2,32,4096]{3,2,1,0:T(8,128)}, u32[]{:S(2)}) copy-start(f32[1,2,32,4096]{3,2,1,0:T(8,128)} %param.15) | copy-start | bytes 3145732
  4.5 12.2 %copy-start.10 = (s32[128,128]{1,0:T(8,128)S(1)}, s32[128,128]{1,0:T(8,128)}, u32[]{:S(2)}) copy-start(s32[128,128]{1,0:T(8,128)} %param.18) | copy-start | bytes 196612
  4.5 12.2 %copy-start.13 = (f32[8]{0:T(128)S(1)}, f32[8]{0:T(128)}, u32[]{:S(2)}) copy-start(f32[8]{0:T(128)} %param.19) | copy-start | bytes 100
  4.5 12.4 %copy-start.11 = (s32[1024]{0:T(1024)S(1)}, s32[1024]{0:T(1024)}, u32[]{:S(2)}) copy-start(s32[1024]{0:T(1024)} %param.17) | copy-start | bytes 12292
  4.5 60.6 %all-to-all-start = ((f32[32,4,32,128]{3,2,1,0:T(8,128)}), f32[32,4,32,128]{3,2,1,0:T(8,128)S(1)}, u32[]{:S(2)}, u32[]{:S(2)}) async-start(f32[32,4,32,128]{3,2,1,0:T(8,128)} %maximum_bitcast_fusion), calls=%async_computation | async-start | bytes 4194304 | tf_op jit(solution)/shard_map/all_to_all | solution.py:284
  16.9 48.2 %copy-start.6 = (bf16[128,96]{1,0:T(8,128)(2,1)S(1)}, bf16[128,96]{1,0:T(8,128)(2,1)}, u32[]{:S(2)}) copy-start(bf16[128,96]{1,0:T(8,128)(2,1)} %constant.49.clone.fwd_ref) | copy-start | bytes 73732
  16.9 48.2 %copy-start.7 = (bf16[64,256]{1,0:T(8,128)(2,1)S(1)}, bf16[64,256]{1,0:T(8,128)(2,1)}, u32[]{:S(2)}) copy-start(bf16[64,256]{1,0:T(8,128)(2,1)} %constant.50.clone.proj_ref) | copy-start | bytes 98308
  16.9 48.2 %copy-start.8 = (f32[32,128]{1,0:T(8,128)S(1)}, f32[32,128]{1,0:T(8,128)}, u32[]{:S(2)}) copy-start(f32[32,128]{1,0:T(8,128)} %constant.51.clone.tt_ref) | copy-start | bytes 49156
  65.1 1.6 copy-start
  119.3 11.3 %copy-start.12 = (f32[1,32]{1,0:T(1,128)S(1)}, f32[1,32]{1,0:T(1,128)}, u32[]{:S(2)}) copy-start(f32[1,32]{1,0:T(1,128)} %param.21) | copy-start | bytes 388
  119.3 42.6 %copy-start.1 = (bf16[2,256,256]{2,1,0:T(8,128)(2,1)S(1)}, bf16[2,256,256]{2,1,0:T(8,128)(2,1)}, u32[]{:S(2)}) copy-start(bf16[2,256,256]{2,1,0:T(8,128)(2,1)} %constant.52.clone.w1_ref) | copy-start | bytes 786436
  119.3 42.6 %copy-start.2 = (bf16[2,256,256]{2,1,0:T(8,128)(2,1)S(1)}, bf16[2,256,256]{2,1,0:T(8,128)(2,1)}, u32[]{:S(2)}) copy-start(bf16[2,256,256]{2,1,0:T(8,128)(2,1)} %constant.53.clone.w2_ref) | copy-start | bytes 786436
  119.3 42.6 %copy-start.3 = (bf16[2,256,256]{2,1,0:T(8,128)(2,1)S(1)}, bf16[2,256,256]{2,1,0:T(8,128)(2,1)}, u32[]{:S(2)}) copy-start(bf16[2,256,256]{2,1,0:T(8,128)(2,1)} %constant.54.clone.w3_ref) | copy-start | bytes 786436
  119.4 42.6 %copy-start.4 = (bf16[2,256,256]{2,1,0:T(8,128)(2,1)S(1)}, bf16[2,256,256]{2,1,0:T(8,128)(2,1)}, u32[]{:S(2)}) copy-start(bf16[2,256,256]{2,1,0:T(8,128)(2,1)} %constant.55.clone.w4_ref) | copy-start | bytes 786436
  119.4 42.6 %copy-start.5 = (f32[2,32,128]{2,1,0:T(8,128)S(1)}, f32[2,32,128]{2,1,0:T(8,128)}, u32[]{:S(2)}) copy-start(f32[2,32,128]{2,1,0:T(8,128)} %constant.56.clone.tw_ref) | copy-start | bytes 98308
  119.4 42.5 %all-to-all-start.1 = ((f32[256,8,128]{2,1,0:T(8,128)}), f32[256,8,128]{2,1,0:T(8,128)S(1)}, u32[]{:S(2)}, u32[]{:S(2)}) async-start(f32[256,8,128]{2,1,0:T(8,128)} %bitcast.2), calls=%async_computation.1 | async-start | bytes 2097152 | tf_op jit(solution)/shard_map/all_to_all | solution.py:288
  130.6 3.7 %collective-permute-start = (f32[1,32]{1,0:T(1,128)S(1)}, f32[1,32]{1,0:T(1,128)S(1)}, u32[]{:S(2)}, u32[]{:S(2)}) collective-permute-start(f32[1,32]{1,0:T(1,128)S(1)} %copy-done.12), channel_id=1, source_target_pairs={{32,0},{64,32},{96,64},{128,96},{160,128},{192,160},{224,192},{0,2... | collective-permute-start | bytes 392 | tf_op jit(solution)/shard_map/ppermute | solution.py:257
  134.3 4.2 %collective-permute-start.1 = (f32[2,32]{1,0:T(2,128)S(1)}, f32[2,32]{1,0:T(2,128)S(1)}, u32[]{:S(2)}, u32[]{:S(2)}) collective-permute-start(f32[2,32]{1,0:T(2,128)S(1)} %pad_maximum_fusion.3), channel_id=1, source_target_pairs={{64,0},{96,32},{128,64},{160,96},{192,128},{224,160},{0,192},{32,2... | collective-permute-start | bytes 776 | tf_op jit(solution)/shard_map/ppermute | solution.py:257
  138.5 4.3 %collective-permute-start.2 = (f32[4,32]{1,0:T(4,128)S(1)}, f32[4,32]{1,0:T(4,128)S(1)}, u32[]{:S(2)}, u32[]{:S(2)}) collective-permute-start(f32[4,32]{1,0:T(4,128)S(1)} %pad_maximum_fusion.2), channel_id=1, source_target_pairs={{128,0},{160,32},{192,64},{224,96},{0,128},{32,160},{64,192},{96,2... | collective-permute-start | bytes 1544 | tf_op jit(solution)/shard_map/ppermute | solution.py:257
where the time goes:
time: 187 us; the launch traced here: 186 us
  waiting for transfers between devices  67.2 us (36%)
  Pallas kernels  57.3 us (31%)
  starting transfers between devices  30.8 us (16%)
  blocking collectives  18.4 us (10%)
  local copies, waits for them, and re-layouts  6.66 us (4%)
  other arithmetic  5.77 us (3%)
    pallas_call x1, Pallas kernels, kerr_call(): pl.pallas_call(kerr_kernel, name='kerr', out_shape=jax.ShapeDtypeStruct((...  52.6 us
    all_to_all x1, waiting for transfers between devices, on_device(): lax.all_to_all(send, 'ma', split_axis=0, concat_axis=0, tiled=True)  45.5 us
    all_to_all x1, waiting for transfers between devices, on_device(): lax.all_to_all(source, ('gz', 'ma'), split_axis=0, concat_axis=0, tiled=T...  18.8 us
    all_to_all x1, blocking collectives, on_device(): lax.all_to_all(result, 'gz', split_axis=0, concat_axis=0, tiled=True)  18.4 us
    all_to_all x1, starting transfers between devices, on_device(): lax.all_to_all(send, 'ma', split_axis=0, concat_axis=0, tiled=True)  12.2 us
    all_to_all x1, starting transfers between devices, on_device(): lax.all_to_all(source, ('gz', 'ma'), split_axis=0, concat_axis=0, tiled=T...  11.2 us
    ppermute x3, starting transfers between devices, gathered_loss(): have = jnp.concatenate([have, lax.ppermute(have, 'gz', route)], axis=0)  7.42 us
    pallas_call x1, Pallas kernels, spectral_call(): pl.pallas_call(spectral_kernel, name='spectral', out_shape=jax.ShapeDtype...  4.63 us
  transfers between devices with their start and end apart: 5, of which 4 were waited for; matrix products, arithmetic and copies ran while one was open for 3% of the time, Pallas kernels for 0%

commit v1 on v0

--- a/solution.py
+++ b/solution.py
@@ -49,7 +49,7 @@
     return jnp.dot(a, b, preferred_element_type=F32)
 
 
-def kerr_kernel(x_ref, place_ref, back_ref, fwd_ref, proj_ref, tt_ref, k_ref, o_ref,
+def kerr_kernel(x_ref, place_ref, back_ref, f2_ref, f3_ref, proj_ref, tt_ref, k_ref, o_ref,
                 xs, fs, gs, rs, ks):
     def split_in(j, carry):
         rows = pl.ds(pl.multiple_of(j * 32, 32), 32)
@@ -67,68 +67,82 @@
 
     lax.fori_loop(0, 4, place, 0)
 
-    def first(p, carry):
-        rows = pl.ds(pl.multiple_of(p * 32, 32), 32)
-        out_rows = pl.ds(pl.multiple_of(p * 128, 128), 128)
+    def first(k, carry):
         for pair in range(2):
-            a, b = fs[2 * pair, rows, :], fs[2 * pair + 1, rows, :]
-            head = jnp.concatenate([a[:, :128], b[:, :128]], axis=1)
-            tail = jnp.concatenate([a[:, 128:], b[:, 128:]], axis=1)
-            got = dot(fwd_ref[...], jnp.concatenate([head, tail, head], axis=0))
-            gs[2 * pair, out_rows, :] = got[:, :128]
-            gs[2 * pair + 1, out_rows, :] = got[:, 128:]
-        return carry
-
-    lax.fori_loop(0, 32, first, 0, unroll=2)
-
-    def column(y, carry):
+            got = []
+            for h in range(2):
+                rows = pl.ds(pl.multiple_of(k * 128 + h * 64, 64), 64)
+                a, b = fs[2 * pair, rows, :], fs[2 * pair + 1, rows, :]
+                head = jnp.concatenate([a[:, :128], b[:, :128]], axis=1)
+                tail = jnp.concatenate([a[:, 128:], b[:, 128:]], axis=1)
+                res = dot(f2_ref[...], jnp.concatenate([head, tail, head], axis=0))
+                got.append(res.reshape(32, 8, 256))
+            low = jnp.concatenate([got[0][:, :4], got[1][:, :4]], axis=1)
+            high = jnp.concatenate([got[0][:, 4:], got[1][:, 4:]], axis=1)
+            for c in range(2):
+                lanes = slice(c * 128, (c + 1) * 128)
+                gs[2 * pair + c, :, 0, k] = low[:, :, lanes]
+                gs[2 * pair + c, :, 1, k] = high[:, :, lanes]
+        return carry
+
+    lax.fori_loop(0, 8, first, 0)
+
+    def column(v, parity):
+        u = 2 * v + parity
         fields = []
         for pair in range(2):
-            got = [split(gs[2 * pair + c, pl.ds(y, 32, stride=128), :]) for c in range(2)]
+            got = [split(gs[2 * pair + c, v, parity].reshape(64, 128)) for c in range(2)]
             head = jnp.concatenate([got[0][0], got[1][0]], axis=1)
             tail = jnp.concatenate([got[0][1], got[1][1]], axis=1)
-            fields.append(dot(fwd_ref[...], jnp.concatenate([head, tail, head], axis=0)))
-        er, ei = fields[0][:, :128], fields[0][:, 128:]
-        cr, ci = fields[1][:, :128], fields[1][:, 128:]
-        rr, ii, ri = er * er, ei * ei, er * ei
-        cross = ri + ri
-        total = rr + ii
-        gr = (total + (rr + rr)) * ci - cross * cr
-        gi = cross * ci - (total + (ii + ii)) * cr
-        gr_h, gr_l = split(gr)
-        gi_h, gi_l = split(gi)
-        right = jnp.concatenate(
-            [jnp.concatenate([gr_h, gi_h], axis=1), jnp.concatenate([gr_l, gi_l], axis=1)], axis=0
-        )
-        t_h, t_l = split(tt_ref[...] * k_ref[pl.ds(y, 1), :])
-        left = jnp.concatenate(
-            [jnp.concatenate([t_h, t_h], axis=1), jnp.concatenate([t_l, jnp.zeros_like(t_l)], axis=1)],
-            axis=0,
-        )
-        got = dot(left, right)
-        got = got[:32] + got[32:]
-        rows = pl.ds(pl.multiple_of(y * 32, 32), 32)
-        rs[0, rows, :] = got[:, :128]
-        rs[1, rows, :] = got[:, 128:]
-        return carry
-
-    lax.fori_loop(0, GRID, column, 0, unroll=2)
-
-    def last(p, carry):
-        got = [split(rs[c, pl.ds(p, 128, stride=32), :]) for c in range(2)]
-        right = jnp.concatenate(
-            [jnp.concatenate([got[0][i], got[1][i]], axis=1) for i in range(2)], axis=0
-        )
-        res = dot(proj_ref[...], right)
-        res = res[:32] + res[32:]
-        rows = pl.ds(pl.multiple_of(p * 32, 32), 32)
+            fields.append(dot(f3_ref[...], jnp.concatenate([head, tail, head], axis=0)))
+        res = []
+        for i in range(2):
+            xr = slice(i * 128, (i + 1) * 128)
+            er, ei = fields[0][xr, :128], fields[0][xr, 128:]
+            cr, ci = fields[1][xr, :128], fields[1][xr, 128:]
+            total = er * er + ei * ei
+            turn = er * ci - ei * cr
+            turn = turn + turn
+            gr_h, gr_l = split(total * ci + turn * er)
+            gi_h, gi_l = split(turn * ei - total * cr)
+            right = jnp.concatenate(
+                [jnp.concatenate([gr_h, gi_h], axis=1), jnp.concatenate([gr_l, gi_l], axis=1)], axis=0
+            )
+            t_h, t_l = split(tt_ref[...] * k_ref[pl.ds(2 * u + i, 1), :])
+            left = jnp.concatenate(
+                [
+                    jnp.concatenate([t_h, t_h], axis=1),
+                    jnp.concatenate([t_l, jnp.zeros_like(t_l)], axis=1),
+                ],
+                axis=0,
+            )
+            got = dot(left, right)
+            res.append(got[:32] + got[32:])
+        rows = pl.ds(pl.multiple_of(u * 16, 16), 16)
+        for g in range(4):
+            both = jnp.concatenate([res[i][g * 8:(g + 1) * 8] for i in range(2)], axis=0)
+            head, tail = split(both)
+            rs[0, g, rows, :] = head
+            rs[1, g, rows, :] = tail
+
+    def columns(v, carry):
+        column(v, 0)
+        column(v, 1)
+        return carry
+
+    lax.fori_loop(0, GRID // 4, columns, 0)
+
+    def last(g, carry):
+        head, tail = rs[0, g], rs[1, g]
+        res = dot(proj_ref[0], head) + (dot(proj_ref[0], tail) + dot(proj_ref[1], head))
+        rows = pl.ds(pl.multiple_of(g * 256, 256), 256)
         for c in range(2):
             head, tail = split(res[:, c * 128:(c + 1) * 128])
             ks[c, rows, 0:128] = head
             ks[c, rows, 128:256] = tail
         return carry
 
-    lax.fori_loop(0, 32, last, 0, unroll=2)
+    lax.fori_loop(0, 4, last, 0)
 
     def finish(j, carry):
         rows = pl.ds(pl.multiple_of(j * 256, 256), 256)
@@ -144,24 +158,24 @@
     lax.fori_loop(0, 4, finish, 0)
 
 
-def kerr_call(received, place, back, fwd, proj, tt, k):
+def kerr_call(received, *constants):
     vm = pl.BlockSpec(memory_space=pltpu.VMEM)
     return pl.pallas_call(
         kerr_kernel,
         name="kerr",
         out_shape=jax.ShapeDtypeStruct((ZL, 32, 8, 128), F32),
-        in_specs=[vm] * 7,
+        in_specs=[vm] * (1 + len(constants)),
         out_specs=vm,
         scratch_shapes=[
             pltpu.VMEM((4, MODES, 256), BF),
             pltpu.VMEM((4, MODES, 256), BF),
-            pltpu.VMEM((4, ORDER * GRID, 128), F32),
-            pltpu.VMEM((2, ORDER * GRID, 128), F32),
+            pltpu.VMEM((4, 32, 2, 8, 8, 128), F32),
+            pltpu.VMEM((2, 4, MODES, 256), BF),
             pltpu.VMEM((2, MODES, 256), BF),
         ],
         compiler_params=pltpu.CompilerParams(vmem_limit_bytes=48 * 2**20),
         cost_estimate=pl.CostEstimate(flops=2 * 10**10, bytes_accessed=8 * 2**20, transcendentals=0),
-    )(received, place, back, fwd, proj, tt, k)
+    )(received, *constants)
 
 
 def three(a_h, a_l, b_h, b_l):
@@ -260,21 +274,36 @@
     return lax.dynamic_slice_in_dim(jnp.concatenate([have, have], axis=0), size - me, size, 0)
 
 
+def kerr_tables():
+    t = hermite_table()
+    t_h, t_l = [part.astype(np.float64) for part in halves(t)]
+
+    def stacked(build):
+        return np.concatenate([build(t_h), build(t_h), build(t_l)], axis=1).astype(jnp.bfloat16)
+
+    eye = np.eye(2)
+
+    def sum_q(table):
+        return np.einsum("yq,ab->yabq", table, eye).reshape(256, 64)
+
+    def sum_p(table):
+        return np.einsum("xkhp,ab->axkhbp", table.reshape(128, 8, 2, 2), eye).reshape(256, 64)
+
+    def sum_y(table):
+        return np.einsum("yq,ab->aqyb", table, np.eye(8)).reshape(256, 1024)
+
+    proj = np.stack([sum_y(t_h), sum_y(t_l)]).astype(jnp.bfloat16)
+    return stacked(sum_q), stacked(sum_p), proj, np.ascontiguousarray(t.T).astype(np.float32)
+
+
 def kerr_constants(mode_order, region, chi):
-    t = hermite_table()
-    t_h, t_l = halves(t)
-    fwd = np.concatenate([t_h, t_h, t_l], axis=1)
-    proj = np.concatenate(
-        [np.concatenate([t_h.T, t_h.T], axis=1), np.concatenate([t_l.T, np.zeros_like(t_l.T)], axis=1)],
-        axis=0,
-    )
-    tt = np.ascontiguousarray(t.T).astype(np.float32)
+    f2, f3, proj, tt = kerr_tables()
     matches = (region[None, :, :] == jnp.arange(REGIONS, dtype=jnp.int32)[:, None, None]).astype(F32)
     k = 2.0 * jnp.sum(matches * chi[:, None, None], axis=0).T
     index = jnp.arange(MODES, dtype=jnp.int32)
     place = (index[:, None] == mode_order[None, :]).astype(BF)
     back = (mode_order[:, None] == index[None, :]).astype(BF)
-    return place, back, fwd, proj, tt, k
+    return place, back, f2, f3, proj, tt, k
 
 
 def on_device(forward, cotangent, mode_order, region, chi, phase, loss):

time: 187 us -> 166 us (0.89)
  Pallas kernels: 57.3 us -> 37.9 us
    pallas_call x1, Pallas kernels: 52.6 us -> 33.3 us  [kerr_call(): pl.pallas_call(kerr_kernel, name='kerr', out_shape=jax.ShapeDtypeStruct((...]
where the time goes in v1:
time: 166 us; the launch traced here: 165 us
  waiting for transfers between devices  67.2 us (40%)
  Pallas kernels  37.9 us (23%)
  starting transfers between devices  30.8 us (19%)
  blocking collectives  18.4 us (11%)
  other arithmetic  5.77 us (3%)
  local copies, waits for them, and re-layouts  5.09 us (3%)
    all_to_all x1, waiting for transfers between devices, on_device(): lax.all_to_all(send, 'ma', split_axis=0, concat_axis=0, tiled=True)  45.5 us
    pallas_call x1, Pallas kernels, kerr_call(): pl.pallas_call(kerr_kernel, name='kerr', out_shape=jax.ShapeDtypeStruct((...  33.3 us
    all_to_all x1, waiting for transfers between devices, on_device(): lax.all_to_all(source, ('gz', 'ma'), split_axis=0, concat_axis=0, tiled=T...  18.8 us
    all_to_all x1, blocking collectives, on_device(): lax.all_to_all(result, 'gz', split_axis=0, concat_axis=0, tiled=True)  18.4 us
    all_to_all x1, starting transfers between devices, on_device(): lax.all_to_all(send, 'ma', split_axis=0, concat_axis=0, tiled=True)  12.2 us
    all_to_all x1, starting transfers between devices, on_device(): lax.all_to_all(source, ('gz', 'ma'), split_axis=0, concat_axis=0, tiled=T...  11.2 us
    ppermute x3, starting transfers between devices, gathered_loss(): have = jnp.concatenate([have, lax.ppermute(have, 'gz', route)], axis=0)  7.42 us
    pallas_call x1, Pallas kernels, spectral_call(): pl.pallas_call(spectral_kernel, name='spectral', out_shape=jax.ShapeDtype...  4.63 us
  transfers between devices with their start and end apart: 5, of which 4 were waited for; matrix products, arithmetic and copies ran while one was open for 3% of the time, Pallas kernels for 0%

profile of v1, /device:TPU:1, one launch (start us, length us, event | category | flops | bytes accessed | tf_op | source)
XLA Modules:
  0.0 165.4 jit_solution(3902114824541518297)
XLA Ops:
  0.0 1.5 copy.32
  1.5 0.6 copy.26
  2.1 0.2 copy.31
  2.3 0.6 copy.25
  2.9 1.5 maximum_bitcast_fusion
  4.5 12.2 %all-to-all-start = ((f32[32,4,32,128]{3,2,1,0:T(8,128)}), f32[32,4,32,128]{3,2,1,0:T(8,128)S(1)}, u32[]{:S(2)}, u32[]{:S(2)}) async-start(f32[32,4,32,128]{3,2,1,0:T(8,128)} %maximum_bitcast_fusion), calls=%async_computation | async-start | bytes 4194304 | tf_op jit(solution)/shard_map/all_to_all | solution.py:313
  16.6 0.1 select_reduce_fusion
  16.9 2.6 %fusion.1 = (bf16[1024,1024]{1,0:T(8,128)(2,1)}, bf16[1024,1024]{1,0:T(8,128)(2,1)}) fusion(s32[1024]{0:T(1024)S(1)} %copy-done.11), kind=kLoop, calls=%fused_computation.3 | loop fusion | flops 4194304 | bytes 4198400 | tf_op jit(solution)/shard_map/convert_element_type | solution.py:305
  19.6 45.5 %all-to-all-done.x_ref = f32[32,4,32,128]{3,2,1,0:T(8,128)S(1)} async-done(((f32[32,4,32,128]{3,2,1,0:T(8,128)}), f32[32,4,32,128]{3,2,1,0:T(8,128)S(1)}, u32[]{:S(2)}, u32[]{:S(2)}) %all-to-all-start) | async-done | bytes 2097184 | tf_op jit(solution)/shard_map/all_to_all | solution.py:313
  65.1 33.3 %kerr.1 = f32[8,32,8,128]{3,2,1,0:T(8,128)} custom-call(f32[32,4,32,128]{3,2,1,0:T(8,128)S(1)} %all-to-all-done.x_ref, bf16[1024,1024]{1,0:T(8,128)(2,1)} %get-tuple-element.8.place_ref, bf16[1024,1024]{1,0:T(8,128)(2,1)} %get-tuple-element.7.back_ref, bf16[256,192]{1,0:T(8,128)(2,1)S(1)} %copy-done.5, bf16[256,192]{1,0:T(8,128)(2,1)S(1)} %copy-done.6, ...), custom_call_target="tpu_custom_call" | custom-call | flops 20000000000 | bytes 8388608 | tf_op jit(solution)/shard_map/kerr/pallas_call | solution.py:163
  98.4 11.2 %all-to-all-start.1 = ((f32[256,8,128]{2,1,0:T(8,128)}), f32[256,8,128]{2,1,0:T(8,128)S(1)}, u32[]{:S(2)}, u32[]{:S(2)}) async-start(f32[256,8,128]{2,1,0:T(8,128)} %bitcast.2), calls=%async_computation.1 | async-start | bytes 2097152 | tf_op jit(solution)/shard_map/all_to_all | solution.py:317
  109.7 2.2 %collective-permute-start = (f32[1,32]{1,0:T(1,128)S(1)}, f32[1,32]{1,0:T(1,128)S(1)}, u32[]{:S(2)}, u32[]{:S(2)}) collective-permute-start(f32[1,32]{1,0:T(1,128)S(1)} %copy-done.12), channel_id=1, source_target_pairs={{32,0},{64,32},{96,64},{128,96},{160,128},{192,160},{224,192},{0,2... | collective-permute-start | bytes 392 | tf_op jit(solution)/shard_map/ppermute | solution.py:271
  111.9 1.4 dynamic-slice_cosine_fusion
  113.2 0.1 neg.20
  113.4 3.5 %collective-permute-start.1 = (f32[2,32]{1,0:T(2,128)S(1)}, f32[2,32]{1,0:T(2,128)S(1)}, u32[]{:S(2)}, u32[]{:S(2)}) collective-permute-start(f32[2,32]{1,0:T(2,128)S(1)} %pad_maximum_fusion.3), channel_id=1, source_target_pairs={{64,0},{96,32},{128,64},{160,96},{192,128},{224,160},{0,192},{32,2... | collective-permute-start | bytes 776 | tf_op jit(solution)/shard_map/ppermute | solution.py:271
  117.0 0.1 cos.20
  117.2 0.4 collective-permute-done.1
  117.6 1.8 %collective-permute-start.2 = (f32[4,32]{1,0:T(4,128)S(1)}, f32[4,32]{1,0:T(4,128)S(1)}, u32[]{:S(2)}, u32[]{:S(2)}) collective-permute-start(f32[4,32]{1,0:T(4,128)S(1)} %pad_maximum_fusion.2), channel_id=1, source_target_pairs={{128,0},{160,32},{192,64},{224,96},{0,128},{32,160},{64,192},{96,2... | collective-permute-start | bytes 1544 | tf_op jit(solution)/shard_map/ppermute | solution.py:271
  119.4 2.5 %collective-permute-done.2 = f32[4,32]{1,0:T(4,128)S(1)} collective-permute-done((f32[4,32]{1,0:T(4,128)S(1)}, f32[4,32]{1,0:T(4,128)S(1)}, u32[]{:S(2)}, u32[]{:S(2)}) %collective-permute-start.2) | collective-permute-done | bytes 544 | tf_op jit(solution)/shard_map/ppermute | solution.py:271
  122.1 18.8 %all-to-all-done.1 = f32[256,8,128]{2,1,0:T(8,128)S(1)} async-done(((f32[256,8,128]{2,1,0:T(8,128)}), f32[256,8,128]{2,1,0:T(8,128)S(1)}, u32[]{:S(2)}, u32[]{:S(2)}) %all-to-all-start.1) | async-done | bytes 1048608 | tf_op jit(solution)/shard_map/all_to_all | solution.py:317
  141.0 4.6 %spectral.1 = f32[8,256,128]{2,1,0:T(8,128)S(1)} custom-call(f32[8,32,8,128]{3,2,1,0:T(8,128)S(1)} %bitcast.25, f32[8,1,8,128]{3,2,1,0:T(8,128)S(1)} %broadcast_in_dim.2.l_ref, f32[2,128,128]{2,1,0:T(8,128)S(1)} %pad_maximum_fusion.ph_ref, bf16[2,256,256]{2,1,0:T(8,128)(2,1)S(1)} %copy-done.1, bf16[2,256,256]{2,1,0:T(8,128)(2,1)S(1)} %copy-done.2, ...), custom_call_target="tpu_custom_call" | custom-call | flops 3000000000 | bytes 4194304 | tf_op jit(solution)/shard_map/spectral/pallas_call | solution.py:253
  145.7 18.4 %all_to_all.15 = f32[8,256,128]{2,1,0:T(8,128)S(1)} all-to-all(f32[8,256,128]{2,1,0:T(8,128)S(1)} %spectral.1), channel_id=1, replica_groups=mesh['gz'=8,'ma'=32] {'gz'}, dimensions={0} | all-to-all | bytes 2097152 | tf_op jit(solution)/shard_map/all_to_all | solution.py:325
  164.1 0.2 copy.30
  164.3 1.2 reshape.58
  (40 shorter events, 0.7 us)
Async XLA Ops:
  0.0 2.1 %copy-start.9 = (f32[1,2,32,4096]{3,2,1,0:T(8,128)S(1)}, f32[1,2,32,4096]{3,2,1,0:T(8,128)}, u32[]{:S(2)}) copy-start(f32[1,2,32,4096]{3,2,1,0:T(8,128)} %param.16) | copy-start | bytes 3145732
  4.5 12.2 %copy-start.10 = (s32[128,128]{1,0:T(8,128)S(1)}, s32[128,128]{1,0:T(8,128)}, u32[]{:S(2)}) copy-start(s32[128,128]{1,0:T(8,128)} %param.19) | copy-start | bytes 196612
  4.5 12.2 %copy-start.13 = (f32[8]{0:T(128)S(1)}, f32[8]{0:T(128)}, u32[]{:S(2)}) copy-start(f32[8]{0:T(128)} %param.20) | copy-start | bytes 100
  4.5 12.4 %copy-start.11 = (s32[1024]{0:T(1024)S(1)}, s32[1024]{0:T(1024)}, u32[]{:S(2)}) copy-start(s32[1024]{0:T(1024)} %param.18) | copy-start | bytes 12292
  4.5 60.6 %all-to-all-start = ((f32[32,4,32,128]{3,2,1,0:T(8,128)}), f32[32,4,32,128]{3,2,1,0:T(8,128)S(1)}, u32[]{:S(2)}, u32[]{:S(2)}) async-start(f32[32,4,32,128]{3,2,1,0:T(8,128)} %maximum_bitcast_fusion), calls=%async_computation | async-start | bytes 4194304 | tf_op jit(solution)/shard_map/all_to_all | solution.py:313
  16.9 48.2 %copy-start = (bf16[2,256,1024]{2,1,0:T(8,128)(2,1)S(1)}, bf16[2,256,1024]{2,1,0:T(8,128)(2,1)}, u32[]{:S(2)}) copy-start(bf16[2,256,1024]{2,1,0:T(8,128)(2,1)} %constant.53.clone.proj_ref) | copy-start | bytes 3145732
  16.9 48.2 %copy-start.5 = (bf16[256,192]{1,0:T(8,128)(2,1)S(1)}, bf16[256,192]{1,0:T(8,128)(2,1)}, u32[]{:S(2)}) copy-start(bf16[256,192]{1,0:T(8,128)(2,1)} %constant.51.clone.f2_ref) | copy-start | bytes 294916
  16.9 48.2 %copy-start.6 = (bf16[256,192]{1,0:T(8,128)(2,1)S(1)}, bf16[256,192]{1,0:T(8,128)(2,1)}, u32[]{:S(2)}) copy-start(bf16[256,192]{1,0:T(8,128)(2,1)} %constant.52.clone.f3_ref) | copy-start | bytes 294916
  16.9 48.2 %copy-start.8 = (f32[32,128]{1,0:T(8,128)S(1)}, f32[32,128]{1,0:T(8,128)}, u32[]{:S(2)}) copy-start(f32[32,128]{1,0:T(8,128)} %constant.54.clone.tt_ref) | copy-start | bytes 49156
  98.4 11.3 %copy-start.12 = (f32[1,32]{1,0:T(1,128)S(1)}, f32[1,32]{1,0:T(1,128)}, u32[]{:S(2)}) copy-start(f32[1,32]{1,0:T(1,128)} %param.22) | copy-start | bytes 388
  98.4 42.6 %copy-start.1 = (bf16[2,256,256]{2,1,0:T(8,128)(2,1)S(1)}, bf16[2,256,256]{2,1,0:T(8,128)(2,1)}, u32[]{:S(2)}) copy-start(bf16[2,256,256]{2,1,0:T(8,128)(2,1)} %constant.55.clone.w1_ref) | copy-start | bytes 786436
  98.4 42.6 %copy-start.2 = (bf16[2,256,256]{2,1,0:T(8,128)(2,1)S(1)}, bf16[2,256,256]{2,1,0:T(8,128)(2,1)}, u32[]{:S(2)}) copy-start(bf16[2,256,256]{2,1,0:T(8,128)(2,1)} %constant.56.clone.w2_ref) | copy-start | bytes 786436
  98.4 42.6 %copy-start.3 = (bf16[2,256,256]{2,1,0:T(8,128)(2,1)S(1)}, bf16[2,256,256]{2,1,0:T(8,128)(2,1)}, u32[]{:S(2)}) copy-start(bf16[2,256,256]{2,1,0:T(8,128)(2,1)} %constant.57.clone.w3_ref) | copy-start | bytes 786436
  98.4 42.6 %copy-start.4 = (bf16[2,256,256]{2,1,0:T(8,128)(2,1)S(1)}, bf16[2,256,256]{2,1,0:T(8,128)(2,1)}, u32[]{:S(2)}) copy-start(bf16[2,256,256]{2,1,0:T(8,128)(2,1)} %constant.58.clone.w4_ref) | copy-start | bytes 786436
  98.4 42.6 %copy-start.7 = (f32[2,32,128]{2,1,0:T(8,128)S(1)}, f32[2,32,128]{2,1,0:T(8,128)}, u32[]{:S(2)}) copy-start(f32[2,32,128]{2,1,0:T(8,128)} %constant.59.clone.tw_ref) | copy-start | bytes 98308
  98.4 42.5 %all-to-all-start.1 = ((f32[256,8,128]{2,1,0:T(8,128)}), f32[256,8,128]{2,1,0:T(8,128)S(1)}, u32[]{:S(2)}, u32[]{:S(2)}) async-start(f32[256,8,128]{2,1,0:T(8,128)} %bitcast.2), calls=%async_computation.1 | async-start | bytes 2097152 | tf_op jit(solution)/shard_map/all_to_all | solution.py:317
  109.7 3.7 %collective-permute-start = (f32[1,32]{1,0:T(1,128)S(1)}, f32[1,32]{1,0:T(1,128)S(1)}, u32[]{:S(2)}, u32[]{:S(2)}) collective-permute-start(f32[1,32]{1,0:T(1,128)S(1)} %copy-done.12), channel_id=1, source_target_pairs={{32,0},{64,32},{96,64},{128,96},{160,128},{192,160},{224,192},{0,2... | collective-permute-start | bytes 392 | tf_op jit(solution)/shard_map/ppermute | solution.py:271
  113.4 4.2 %collective-permute-start.1 = (f32[2,32]{1,0:T(2,128)S(1)}, f32[2,32]{1,0:T(2,128)S(1)}, u32[]{:S(2)}, u32[]{:S(2)}) collective-permute-start(f32[2,32]{1,0:T(2,128)S(1)} %pad_maximum_fusion.3), channel_id=1, source_target_pairs={{64,0},{96,32},{128,64},{160,96},{192,128},{224,160},{0,192},{32,2... | collective-permute-start | bytes 776 | tf_op jit(solution)/shard_map/ppermute | solution.py:271
  117.6 4.3 %collective-permute-start.2 = (f32[4,32]{1,0:T(4,128)S(1)}, f32[4,32]{1,0:T(4,128)S(1)}, u32[]{:S(2)}, u32[]{:S(2)}) collective-permute-start(f32[4,32]{1,0:T(4,128)S(1)} %pad_maximum_fusion.2), channel_id=1, source_target_pairs={{128,0},{160,32},{192,64},{224,96},{0,128},{32,160},{64,192},{96,2... | collective-permute-start | bytes 1544 | tf_op jit(solution)/shard_map/ppermute | solution.py:271

commit v2 on v1

--- a/solution.py
+++ b/solution.py
@@ -50,7 +50,7 @@
 
 
 def kerr_kernel(x_ref, place_ref, back_ref, f2_ref, f3_ref, proj_ref, tt_ref, k_ref, o_ref,
-                xs, fs, gs, rs, ks):
+                xs, fs, gs, rs, ks, fb):
     def split_in(j, carry):
         rows = pl.ds(pl.multiple_of(j * 32, 32), 32)
         for f in range(4):
@@ -87,19 +87,20 @@
 
     lax.fori_loop(0, 8, first, 0)
 
-    def column(v, parity):
-        u = 2 * v + parity
-        fields = []
+    def grid(v, parity, slot):
         for pair in range(2):
             got = [split(gs[2 * pair + c, v, parity].reshape(64, 128)) for c in range(2)]
             head = jnp.concatenate([got[0][0], got[1][0]], axis=1)
             tail = jnp.concatenate([got[0][1], got[1][1]], axis=1)
-            fields.append(dot(f3_ref[...], jnp.concatenate([head, tail, head], axis=0)))
+            fb[slot, pair] = dot(f3_ref[...], jnp.concatenate([head, tail, head], axis=0))
+
+    def column(v, parity):
+        u = 2 * v + parity
         res = []
         for i in range(2):
             xr = slice(i * 128, (i + 1) * 128)
-            er, ei = fields[0][xr, :128], fields[0][xr, 128:]
-            cr, ci = fields[1][xr, :128], fields[1][xr, 128:]
+            er, ei = fb[parity, 0, xr, :128], fb[parity, 0, xr, 128:]
+            cr, ci = fb[parity, 1, xr, :128], fb[parity, 1, xr, 128:]
             total = er * er + ei * ei
             turn = er * ci - ei * cr
             turn = turn + turn
@@ -126,11 +127,14 @@
             rs[1, g, rows, :] = tail
 
     def columns(v, carry):
+        grid(v, 1, 1)
         column(v, 0)
+        grid(jnp.minimum(v + 1, GRID // 4 - 1), 0, 0)
         column(v, 1)
         return carry
 
-    lax.fori_loop(0, GRID // 4, columns, 0)
+    grid(0, 0, 0)
+    lax.fori_loop(0, GRID // 4, columns, 0, unroll=2)
 
     def last(g, carry):
         head, tail = rs[0, g], rs[1, g]
@@ -172,6 +176,7 @@
             pltpu.VMEM((4, 32, 2, 8, 8, 128), F32),
             pltpu.VMEM((2, 4, MODES, 256), BF),
             pltpu.VMEM((2, MODES, 256), BF),
+            pltpu.VMEM((2, 2, 256, 256), F32),
         ],
         compiler_params=pltpu.CompilerParams(vmem_limit_bytes=48 * 2**20),
         cost_estimate=pl.CostEstimate(flops=2 * 10**10, bytes_accessed=8 * 2**20, transcendentals=0),

time: 166 us -> 156 us (0.940)
  Pallas kernels: 37.9 us -> 28.4 us
    pallas_call x1, Pallas kernels: 33.3 us -> 23.7 us  [kerr_call(): pl.pallas_call(kerr_kernel, name='kerr', out_shape=jax.ShapeDtypeStruct((...]
where the time goes in v2:
time: 156 us
  waiting for transfers between devices  67.2 us (43%)
  starting transfers between devices  30.8 us (20%)
  Pallas kernels  28.4 us (18%)
  blocking collectives  18.4 us (12%)
  other arithmetic  5.77 us (4%)
  local copies, waits for them, and re-layouts  5.09 us (3%)
    all_to_all x1, waiting for transfers between devices, on_device(): lax.all_to_all(send, 'ma', split_axis=0, concat_axis=0, tiled=True)  45.5 us
    pallas_call x1, Pallas kernels, kerr_call(): pl.pallas_call(kerr_kernel, name='kerr', out_shape=jax.ShapeDtypeStruct((...  23.7 us
    all_to_all x1, waiting for transfers between devices, on_device(): lax.all_to_all(source, ('gz', 'ma'), split_axis=0, concat_axis=0, tiled=T...  18.8 us
    all_to_all x1, blocking collectives, on_device(): lax.all_to_all(result, 'gz', split_axis=0, concat_axis=0, tiled=True)  18.4 us
    all_to_all x1, starting transfers between devices, on_device(): lax.all_to_all(send, 'ma', split_axis=0, concat_axis=0, tiled=True)  12.2 us
    all_to_all x1, starting transfers between devices, on_device(): lax.all_to_all(source, ('gz', 'ma'), split_axis=0, concat_axis=0, tiled=T...  11.2 us
    ppermute x3, starting transfers between devices, gathered_loss(): have = jnp.concatenate([have, lax.ppermute(have, 'gz', route)], axis=0)  7.42 us
    pallas_call x1, Pallas kernels, spectral_call(): pl.pallas_call(spectral_kernel, name='spectral', out_shape=jax.ShapeDtype...  4.63 us
  transfers between devices with their start and end apart: 5, of which 4 were waited for; matrix products, arithmetic and copies ran while one was open for 3% of the time, Pallas kernels for 0%

profile of v2, /device:TPU:1, one launch (start us, length us, event | category | flops | bytes accessed | tf_op | source)
XLA Modules:
  0.0 155.9 jit_solution(1063509561943446986)
XLA Ops:
  0.0 1.5 copy.32
  1.5 0.6 copy.26
  2.1 0.2 copy.31
  2.3 0.6 copy.25
  2.9 1.5 maximum_bitcast_fusion
  4.5 12.2 %all-to-all-start = ((f32[32,4,32,128]{3,2,1,0:T(8,128)}), f32[32,4,32,128]{3,2,1,0:T(8,128)S(1)}, u32[]{:S(2)}, u32[]{:S(2)}) async-start(f32[32,4,32,128]{3,2,1,0:T(8,128)} %maximum_bitcast_fusion), calls=%async_computation | async-start | bytes 4194304 | tf_op jit(solution)/shard_map/all_to_all | solution.py:318
  16.6 0.1 select_reduce_fusion
  16.9 2.6 %fusion.1 = (bf16[1024,1024]{1,0:T(8,128)(2,1)}, bf16[1024,1024]{1,0:T(8,128)(2,1)}) fusion(s32[1024]{0:T(1024)S(1)} %copy-done.11), kind=kLoop, calls=%fused_computation.3 | loop fusion | flops 4194304 | bytes 4198400 | tf_op jit(solution)/shard_map/convert_element_type | solution.py:310
  19.6 45.5 %all-to-all-done.x_ref = f32[32,4,32,128]{3,2,1,0:T(8,128)S(1)} async-done(((f32[32,4,32,128]{3,2,1,0:T(8,128)}), f32[32,4,32,128]{3,2,1,0:T(8,128)S(1)}, u32[]{:S(2)}, u32[]{:S(2)}) %all-to-all-start) | async-done | bytes 2097184 | tf_op jit(solution)/shard_map/all_to_all | solution.py:318
  65.1 23.7 %kerr.1 = f32[8,32,8,128]{3,2,1,0:T(8,128)} custom-call(f32[32,4,32,128]{3,2,1,0:T(8,128)S(1)} %all-to-all-done.x_ref, bf16[1024,1024]{1,0:T(8,128)(2,1)} %get-tuple-element.8.place_ref, bf16[1024,1024]{1,0:T(8,128)(2,1)} %get-tuple-element.7.back_ref, bf16[256,192]{1,0:T(8,128)(2,1)S(1)} %copy-done.5, bf16[256,192]{1,0:T(8,128)(2,1)S(1)} %copy-done.6, ...), custom_call_target="tpu_custom_call" | custom-call | flops 20000000000 | bytes 8388608 | tf_op jit(solution)/shard_map/kerr/pallas_call | solution.py:167
  88.9 11.2 %all-to-all-start.1 = ((f32[256,8,128]{2,1,0:T(8,128)}), f32[256,8,128]{2,1,0:T(8,128)S(1)}, u32[]{:S(2)}, u32[]{:S(2)}) async-start(f32[256,8,128]{2,1,0:T(8,128)} %bitcast.2), calls=%async_computation.1 | async-start | bytes 2097152 | tf_op jit(solution)/shard_map/all_to_all | solution.py:322
  100.2 2.2 %collective-permute-start = (f32[1,32]{1,0:T(1,128)S(1)}, f32[1,32]{1,0:T(1,128)S(1)}, u32[]{:S(2)}, u32[]{:S(2)}) collective-permute-start(f32[1,32]{1,0:T(1,128)S(1)} %copy-done.12), channel_id=1, source_target_pairs={{32,0},{64,32},{96,64},{128,96},{160,128},{192,160},{224,192},{0,2... | collective-permute-start | bytes 392 | tf_op jit(solution)/shard_map/ppermute | solution.py:276
  102.3 1.4 dynamic-slice_cosine_fusion
  103.7 0.1 neg.20
  103.9 3.5 %collective-permute-start.1 = (f32[2,32]{1,0:T(2,128)S(1)}, f32[2,32]{1,0:T(2,128)S(1)}, u32[]{:S(2)}, u32[]{:S(2)}) collective-permute-start(f32[2,32]{1,0:T(2,128)S(1)} %pad_maximum_fusion.3), channel_id=1, source_target_pairs={{64,0},{96,32},{128,64},{160,96},{192,128},{224,160},{0,192},{32,2... | collective-permute-start | bytes 776 | tf_op jit(solution)/shard_map/ppermute | solution.py:276
  107.4 0.1 cos.20
  107.7 0.4 collective-permute-done.1
  108.1 1.8 %collective-permute-start.2 = (f32[4,32]{1,0:T(4,128)S(1)}, f32[4,32]{1,0:T(4,128)S(1)}, u32[]{:S(2)}, u32[]{:S(2)}) collective-permute-start(f32[4,32]{1,0:T(4,128)S(1)} %pad_maximum_fusion.2), channel_id=1, source_target_pairs={{128,0},{160,32},{192,64},{224,96},{0,128},{32,160},{64,192},{96,2... | collective-permute-start | bytes 1544 | tf_op jit(solution)/shard_map/ppermute | solution.py:276
  109.9 2.5 %collective-permute-done.2 = f32[4,32]{1,0:T(4,128)S(1)} collective-permute-done((f32[4,32]{1,0:T(4,128)S(1)}, f32[4,32]{1,0:T(4,128)S(1)}, u32[]{:S(2)}, u32[]{:S(2)}) %collective-permute-start.2) | collective-permute-done | bytes 544 | tf_op jit(solution)/shard_map/ppermute | solution.py:276
  112.6 18.8 %all-to-all-done.1 = f32[256,8,128]{2,1,0:T(8,128)S(1)} async-done(((f32[256,8,128]{2,1,0:T(8,128)}), f32[256,8,128]{2,1,0:T(8,128)S(1)}, u32[]{:S(2)}, u32[]{:S(2)}) %all-to-all-start.1) | async-done | bytes 1048608 | tf_op jit(solution)/shard_map/all_to_all | solution.py:322
  131.5 4.6 %spectral.1 = f32[8,256,128]{2,1,0:T(8,128)S(1)} custom-call(f32[8,32,8,128]{3,2,1,0:T(8,128)S(1)} %bitcast.25, f32[8,1,8,128]{3,2,1,0:T(8,128)S(1)} %broadcast_in_dim.2.l_ref, f32[2,128,128]{2,1,0:T(8,128)S(1)} %pad_maximum_fusion.ph_ref, bf16[2,256,256]{2,1,0:T(8,128)(2,1)S(1)} %copy-done.1, bf16[2,256,256]{2,1,0:T(8,128)(2,1)S(1)} %copy-done.2, ...), custom_call_target="tpu_custom_call" | custom-call | flops 3000000000 | bytes 4194304 | tf_op jit(solution)/shard_map/spectral/pallas_call | solution.py:258
  136.1 18.4 %all_to_all.15 = f32[8,256,128]{2,1,0:T(8,128)S(1)} all-to-all(f32[8,256,128]{2,1,0:T(8,128)S(1)} %spectral.1), channel_id=1, replica_groups=mesh['gz'=8,'ma'=32] {'gz'}, dimensions={0} | all-to-all | bytes 2097152 | tf_op jit(solution)/shard_map/all_to_all | solution.py:330
  154.5 0.2 copy.30
  154.7 1.2 reshape.58
  (40 shorter events, 0.7 us)
Async XLA Ops:
  0.0 2.1 %copy-start.9 = (f32[1,2,32,4096]{3,2,1,0:T(8,128)S(1)}, f32[1,2,32,4096]{3,2,1,0:T(8,128)}, u32[]{:S(2)}) copy-start(f32[1,2,32,4096]{3,2,1,0:T(8,128)} %param.16) | copy-start | bytes 3145732
  4.5 12.2 %copy-start.10 = (s32[128,128]{1,0:T(8,128)S(1)}, s32[128,128]{1,0:T(8,128)}, u32[]{:S(2)}) copy-start(s32[128,128]{1,0:T(8,128)} %param.19) | copy-start | bytes 196612
  4.5 12.2 %copy-start.13 = (f32[8]{0:T(128)S(1)}, f32[8]{0:T(128)}, u32[]{:S(2)}) copy-start(f32[8]{0:T(128)} %param.20) | copy-start | bytes 100
  4.5 12.4 %copy-start.11 = (s32[1024]{0:T(1024)S(1)}, s32[1024]{0:T(1024)}, u32[]{:S(2)}) copy-start(s32[1024]{0:T(1024)} %param.18) | copy-start | bytes 12292
  4.5 60.6 %all-to-all-start = ((f32[32,4,32,128]{3,2,1,0:T(8,128)}), f32[32,4,32,128]{3,2,1,0:T(8,128)S(1)}, u32[]{:S(2)}, u32[]{:S(2)}) async-start(f32[32,4,32,128]{3,2,1,0:T(8,128)} %maximum_bitcast_fusion), calls=%async_computation | async-start | bytes 4194304 | tf_op jit(solution)/shard_map/all_to_all | solution.py:318
  16.9 48.2 %copy-start = (bf16[2,256,1024]{2,1,0:T(8,128)(2,1)S(1)}, bf16[2,256,1024]{2,1,0:T(8,128)(2,1)}, u32[]{:S(2)}) copy-start(bf16[2,256,1024]{2,1,0:T(8,128)(2,1)} %constant.53.clone.proj_ref) | copy-start | bytes 3145732
  16.9 48.2 %copy-start.5 = (bf16[256,192]{1,0:T(8,128)(2,1)S(1)}, bf16[256,192]{1,0:T(8,128)(2,1)}, u32[]{:S(2)}) copy-start(bf16[256,192]{1,0:T(8,128)(2,1)} %constant.51.clone.f2_ref) | copy-start | bytes 294916
  16.9 48.2 %copy-start.6 = (bf16[256,192]{1,0:T(8,128)(2,1)S(1)}, bf16[256,192]{1,0:T(8,128)(2,1)}, u32[]{:S(2)}) copy-start(bf16[256,192]{1,0:T(8,128)(2,1)} %constant.52.clone.f3_ref) | copy-start | bytes 294916
  16.9 48.2 %copy-start.8 = (f32[32,128]{1,0:T(8,128)S(1)}, f32[32,128]{1,0:T(8,128)}, u32[]{:S(2)}) copy-start(f32[32,128]{1,0:T(8,128)} %constant.54.clone.tt_ref) | copy-start | bytes 49156
  88.9 11.3 %copy-start.12 = (f32[1,32]{1,0:T(1,128)S(1)}, f32[1,32]{1,0:T(1,128)}, u32[]{:S(2)}) copy-start(f32[1,32]{1,0:T(1,128)} %param.22) | copy-start | bytes 388
  88.9 42.6 %copy-start.1 = (bf16[2,256,256]{2,1,0:T(8,128)(2,1)S(1)}, bf16[2,256,256]{2,1,0:T(8,128)(2,1)}, u32[]{:S(2)}) copy-start(bf16[2,256,256]{2,1,0:T(8,128)(2,1)} %constant.55.clone.w1_ref) | copy-start | bytes 786436
  88.9 42.6 %copy-start.2 = (bf16[2,256,256]{2,1,0:T(8,128)(2,1)S(1)}, bf16[2,256,256]{2,1,0:T(8,128)(2,1)}, u32[]{:S(2)}) copy-start(bf16[2,256,256]{2,1,0:T(8,128)(2,1)} %constant.56.clone.w2_ref) | copy-start | bytes 786436
  88.9 42.6 %copy-start.3 = (bf16[2,256,256]{2,1,0:T(8,128)(2,1)S(1)}, bf16[2,256,256]{2,1,0:T(8,128)(2,1)}, u32[]{:S(2)}) copy-start(bf16[2,256,256]{2,1,0:T(8,128)(2,1)} %constant.57.clone.w3_ref) | copy-start | bytes 786436
  88.9 42.6 %copy-start.4 = (bf16[2,256,256]{2,1,0:T(8,128)(2,1)S(1)}, bf16[2,256,256]{2,1,0:T(8,128)(2,1)}, u32[]{:S(2)}) copy-start(bf16[2,256,256]{2,1,0:T(8,128)(2,1)} %constant.58.clone.w4_ref) | copy-start | bytes 786436
  88.9 42.6 %copy-start.7 = (f32[2,32,128]{2,1,0:T(8,128)S(1)}, f32[2,32,128]{2,1,0:T(8,128)}, u32[]{:S(2)}) copy-start(f32[2,32,128]{2,1,0:T(8,128)} %constant.59.clone.tw_ref) | copy-start | bytes 98308
  88.9 42.5 %all-to-all-start.1 = ((f32[256,8,128]{2,1,0:T(8,128)}), f32[256,8,128]{2,1,0:T(8,128)S(1)}, u32[]{:S(2)}, u32[]{:S(2)}) async-start(f32[256,8,128]{2,1,0:T(8,128)} %bitcast.2), calls=%async_computation.1 | async-start | bytes 2097152 | tf_op jit(solution)/shard_map/all_to_all | solution.py:322
  100.2 3.7 %collective-permute-start = (f32[1,32]{1,0:T(1,128)S(1)}, f32[1,32]{1,0:T(1,128)S(1)}, u32[]{:S(2)}, u32[]{:S(2)}) collective-permute-start(f32[1,32]{1,0:T(1,128)S(1)} %copy-done.12), channel_id=1, source_target_pairs={{32,0},{64,32},{96,64},{128,96},{160,128},{192,160},{224,192},{0,2... | collective-permute-start | bytes 392 | tf_op jit(solution)/shard_map/ppermute | solution.py:276
  103.9 4.2 %collective-permute-start.1 = (f32[2,32]{1,0:T(2,128)S(1)}, f32[2,32]{1,0:T(2,128)S(1)}, u32[]{:S(2)}, u32[]{:S(2)}) collective-permute-start(f32[2,32]{1,0:T(2,128)S(1)} %pad_maximum_fusion.3), channel_id=1, source_target_pairs={{64,0},{96,32},{128,64},{160,96},{192,128},{224,160},{0,192},{32,2... | collective-permute-start | bytes 776 | tf_op jit(solution)/shard_map/ppermute | solution.py:276
  108.1 4.3 %collective-permute-start.2 = (f32[4,32]{1,0:T(4,128)S(1)}, f32[4,32]{1,0:T(4,128)S(1)}, u32[]{:S(2)}, u32[]{:S(2)}) collective-permute-start(f32[4,32]{1,0:T(4,128)S(1)} %pad_maximum_fusion.2), channel_id=1, source_target_pairs={{128,0},{160,32},{192,64},{224,96},{0,128},{32,160},{64,192},{96,2... | collective-permute-start | bytes 1544 | tf_op jit(solution)/shard_map/ppermute | solution.py:276

commit v3 on v2

--- a/solution.py
+++ b/solution.py
@@ -49,8 +49,38 @@
     return jnp.dot(a, b, preferred_element_type=F32)
 
 
-def kerr_kernel(x_ref, place_ref, back_ref, f2_ref, f3_ref, proj_ref, tt_ref, k_ref, o_ref,
-                xs, fs, gs, rs, ks, fb):
+def pack_kernel(f_ref, c_ref, o_ref):
+    for j in range(f_ref.shape[3] // 128):
+        o_ref[j, 0:2] = f_ref[0, :, :, j * 128:(j + 1) * 128]
+        o_ref[j, 2:4] = c_ref[0, :, :, j * 128:(j + 1) * 128]
+
+
+def pack_call(forward, cotangent):
+    steps = 4
+    spec = pl.BlockSpec((1, 2, 32, TIME // steps), lambda i: (0, 0, 0, i))
+    return pl.pallas_call(
+        pack_kernel,
+        name="pack",
+        grid=(steps,),
+        out_shape=jax.ShapeDtypeStruct((32, 4, 32, 128), F32),
+        in_specs=[spec, spec],
+        out_specs=pl.BlockSpec((32 // steps, 4, 32, 128), lambda i: (i, 0, 0, 0)),
+        compiler_params=pltpu.CompilerParams(vmem_limit_bytes=60 * 2**20),
+        cost_estimate=pl.CostEstimate(flops=2**20, bytes_accessed=4 * 2**20, transcendentals=0),
+    )(forward, cotangent)
+
+
+def kerr_kernel(x_ref, place_hbm, back_hbm, f2_ref, f3_ref, proj_hbm, tt_ref, k_ref, o_hbm,
+                xs, fs, gs, rs, ks, fb, place_ref, back_ref, proj_ref, o_ref, sems, out_sems):
+    loads = [
+        pltpu.make_async_copy(source, target, sems.at[i])
+        for i, (source, target) in enumerate(
+            ((place_hbm, place_ref), (proj_hbm, proj_ref), (back_hbm, back_ref))
+        )
+    ]
+    for load in loads:
+        load.start()
+
     def split_in(j, carry):
         rows = pl.ds(pl.multiple_of(j * 32, 32), 32)
         for f in range(4):
@@ -65,6 +95,7 @@
         fs[f] = dot(place_ref[...], xs[f]).astype(BF)
         return carry
 
+    loads[0].wait()
     lax.fori_loop(0, 4, place, 0)
 
     def first(k, carry):
@@ -85,7 +116,7 @@
                 gs[2 * pair + c, :, 1, k] = high[:, :, lanes]
         return carry
 
-    lax.fori_loop(0, 8, first, 0)
+    lax.fori_loop(0, 8, first, 0, unroll=2)
 
     def grid(v, parity, slot):
         for pair in range(2):
@@ -146,7 +177,12 @@
             ks[c, rows, 128:256] = tail
         return carry
 
-    lax.fori_loop(0, 4, last, 0)
+    loads[1].wait()
+    lax.fori_loop(0, 4, last, 0, unroll=2)
+
+    def store(j):
+        part = pl.ds(j * 8, 8)
+        return pltpu.make_async_copy(o_ref.at[:, part], o_hbm.at[:, part], out_sems.at[j])
 
     def finish(j, carry):
         rows = pl.ds(pl.multiple_of(j * 256, 256), 256)
@@ -157,19 +193,24 @@
                 value = res[i * 32:(i + 1) * 32] + x_ref[j * 8 + i, 2 + c]
                 for g in range(8):
                     o_ref[g, j * 8 + i, c * 4:(c + 1) * 4, :] = value[g * 4:(g + 1) * 4]
-        return carry
-
+        store(j).start()
+        return carry
+
+    loads[2].wait()
     lax.fori_loop(0, 4, finish, 0)
+    for j in range(4):
+        store(j).wait()
 
 
 def kerr_call(received, *constants):
     vm = pl.BlockSpec(memory_space=pltpu.VMEM)
+    hbm = pl.BlockSpec(memory_space=pl.ANY)
     return pl.pallas_call(
         kerr_kernel,
         name="kerr",
         out_shape=jax.ShapeDtypeStruct((ZL, 32, 8, 128), F32),
-        in_specs=[vm] * (1 + len(constants)),
-        out_specs=vm,
+        in_specs=[vm, hbm, hbm, vm, vm, hbm, vm, vm],
+        out_specs=hbm,
         scratch_shapes=[
             pltpu.VMEM((4, MODES, 256), BF),
             pltpu.VMEM((4, MODES, 256), BF),
@@ -177,8 +218,14 @@
             pltpu.VMEM((2, 4, MODES, 256), BF),
             pltpu.VMEM((2, MODES, 256), BF),
             pltpu.VMEM((2, 2, 256, 256), F32),
+            pltpu.VMEM((MODES, MODES), BF),
+            pltpu.VMEM((MODES, MODES), BF),
+            pltpu.VMEM((2, 256, MODES), BF),
+            pltpu.VMEM((ZL, 32, 8, 128), F32),
+            pltpu.SemaphoreType.DMA((3,)),
+            pltpu.SemaphoreType.DMA((4,)),
         ],
-        compiler_params=pltpu.CompilerParams(vmem_limit_bytes=48 * 2**20),
+        compiler_params=pltpu.CompilerParams(vmem_limit_bytes=54 * 2**20),
         cost_estimate=pl.CostEstimate(flops=2 * 10**10, bytes_accessed=8 * 2**20, transcendentals=0),
     )(received, *constants)
 
@@ -313,8 +360,7 @@
 
 def on_device(forward, cotangent, mode_order, region, chi, phase, loss):
     me = lax.axis_index("gz")
-    both = jnp.concatenate([forward[0], cotangent[0]], axis=0)
-    send = both.reshape(4, 32, 32, BLOCK).transpose(2, 0, 1, 3)
+    send = pack_call(forward, cotangent)
     received = lax.all_to_all(send, "ma", split_axis=0, concat_axis=0, tiled=True)
     constants = kerr_constants(mode_order, region, chi)
     source = kerr_call(received, *constants)

time: 156 us -> 157 us (level)
  Pallas kernels: 28.4 us -> 31.8 us
  local copies, waits for them, and re-layouts: 5.09 us -> 3.51 us
    pallas_call x0 -> x1, Pallas kernels: none -> 3.79 us  [pack_call(): pl.pallas_call(pack_kernel, name='pack', grid=(steps,), out_shape=jax.Sha...]
  transfers between devices with their start and end apart: 5 -> 5, of which waited for: 4 -> 4; matrix products, arithmetic and copies ran while one was open for 3% -> 4% of each run, Pallas kernels for 0% -> 0%
where the time goes in v3:
time: 157 us; the launch traced here: 156 us
  waiting for transfers between devices  66.7 us (42%)
  Pallas kernels  31.8 us (20%)
  starting transfers between devices  30.8 us (20%)
  blocking collectives  18.4 us (12%)
  other arithmetic  4.85 us (3%)
  local copies, waits for them, and re-layouts  3.51 us (2%)
    all_to_all x1, waiting for transfers between devices, on_device(): lax.all_to_all(send, 'ma', split_axis=0, concat_axis=0, tiled=True)  45 us
    pallas_call x1, Pallas kernels, kerr_call(): pl.pallas_call(kerr_kernel, name='kerr', out_shape=jax.ShapeDtypeStruct((...  23.4 us
    all_to_all x1, waiting for transfers between devices, on_device(): lax.all_to_all(source, ('gz', 'ma'), split_axis=0, concat_axis=0, tiled=T...  18.8 us
    all_to_all x1, blocking collectives, on_device(): lax.all_to_all(result, 'gz', split_axis=0, concat_axis=0, tiled=True)  18.4 us
    all_to_all x1, starting transfers between devices, on_device(): lax.all_to_all(send, 'ma', split_axis=0, concat_axis=0, tiled=True)  12.2 us
    all_to_all x1, starting transfers between devices, on_device(): lax.all_to_all(source, ('gz', 'ma'), split_axis=0, concat_axis=0, tiled=T...  11.3 us
    ppermute x3, starting transfers between devices, gathered_loss(): have = jnp.concatenate([have, lax.ppermute(have, 'gz', route)], axis=0)  7.42 us
    pallas_call x1, Pallas kernels, spectral_call(): pl.pallas_call(spectral_kernel, name='spectral', out_shape=jax.ShapeDtype...  4.63 us
  transfers between devices with their start and end apart: 5, of which 4 were waited for; matrix products, arithmetic and copies ran while one was open for 4% of the time, Pallas kernels for 0%

profile of v3, /device:TPU:1, one launch (start us, length us, event | category | flops | bytes accessed | tf_op | source)
XLA Modules:
  0.0 156.2 jit_solution(4528568392838356851)
XLA Ops:
  0.0 3.8 %pack.1 = f32[32,4,32,128]{3,2,1,0:T(8,128)} custom-call(f32[1,2,32,4096]{3,2,1,0:T(8,128)} %f_ref.1, f32[1,2,32,4096]{3,2,1,0:T(8,128)} %c_ref.1), custom_call_target="tpu_custom_call" | custom-call | flops 1048576 | bytes 4194304 | tf_op jit(solution)/shard_map/pack/pallas_call | solution.py:61
  3.8 12.2 %all-to-all-start = ((f32[32,4,32,128]{3,2,1,0:T(8,128)}), f32[32,4,32,128]{3,2,1,0:T(8,128)S(1)}, u32[]{:S(2)}, u32[]{:S(2)}) async-start(f32[32,4,32,128]{3,2,1,0:T(8,128)} %pack.1), calls=%async_computation | async-start | bytes 4194304 | tf_op jit(solution)/shard_map/all_to_all | solution.py:364
  16.0 0.1 select_reduce_fusion
  16.2 0.6 multiply_bitcast_fusion.k_ref
  16.8 2.6 %fusion.1 = (bf16[1024,1024]{1,0:T(8,128)(2,1)}, bf16[1024,1024]{1,0:T(8,128)(2,1)}) fusion(s32[1024]{0:T(1024)S(1)} %copy-done.7), kind=kLoop, calls=%fused_computation.3 | loop fusion | flops 4194304 | bytes 4198400 | tf_op jit(solution)/shard_map/convert_element_type | solution.py:357
  19.5 45.0 %all-to-all-done.x_ref = f32[32,4,32,128]{3,2,1,0:T(8,128)S(1)} async-done(((f32[32,4,32,128]{3,2,1,0:T(8,128)}), f32[32,4,32,128]{3,2,1,0:T(8,128)S(1)}, u32[]{:S(2)}, u32[]{:S(2)}) %all-to-all-start) | async-done | bytes 2097184 | tf_op jit(solution)/shard_map/all_to_all | solution.py:364
  64.5 1.4 copy-done.5
  65.8 23.4 %kerr.1 = f32[8,32,8,128]{3,2,1,0:T(8,128)} custom-call(f32[32,4,32,128]{3,2,1,0:T(8,128)} %copy-done.5, bf16[1024,1024]{1,0:T(8,128)(2,1)} %get-tuple-element.8.place_hbm, bf16[1024,1024]{1,0:T(8,128)(2,1)} %get-tuple-element.7.back_hbm, bf16[256,192]{1,0:T(8,128)(2,1)} %constant.51.clone.f2_ref, bf16[256,192]{1,0:T(8,128)(2,1)} %constant.52.clone.f3_ref, ...), custom_call_target="tpu_custom_call" | custom-call | flops 20000000000 | bytes 8388608 | tf_op jit(solution)/shard_map/kerr/pallas_call | solution.py:208
  89.2 11.3 %all-to-all-start.1 = ((f32[256,8,128]{2,1,0:T(8,128)}), f32[256,8,128]{2,1,0:T(8,128)S(1)}, u32[]{:S(2)}, u32[]{:S(2)}) async-start(f32[256,8,128]{2,1,0:T(8,128)} %bitcast.17), calls=%async_computation.1 | async-start | bytes 2097152 | tf_op jit(solution)/shard_map/all_to_all | solution.py:368
  100.5 2.2 %collective-permute-start = (f32[1,32]{1,0:T(1,128)S(1)}, f32[1,32]{1,0:T(1,128)S(1)}, u32[]{:S(2)}, u32[]{:S(2)}) collective-permute-start(f32[1,32]{1,0:T(1,128)S(1)} %copy-done.8), channel_id=1, source_target_pairs={{32,0},{64,32},{96,64},{128,96},{160,128},{192,160},{224,192},{0,2... | collective-permute-start | bytes 392 | tf_op jit(solution)/shard_map/ppermute | solution.py:323
  102.7 1.4 dynamic-slice_cosine_fusion
  104.1 0.1 neg.20
  104.2 3.5 %collective-permute-start.1 = (f32[2,32]{1,0:T(2,128)S(1)}, f32[2,32]{1,0:T(2,128)S(1)}, u32[]{:S(2)}, u32[]{:S(2)}) collective-permute-start(f32[2,32]{1,0:T(2,128)S(1)} %pad_maximum_fusion.3), channel_id=1, source_target_pairs={{64,0},{96,32},{128,64},{160,96},{192,128},{224,160},{0,192},{32,2... | collective-permute-start | bytes 776 | tf_op jit(solution)/shard_map/ppermute | solution.py:323
  107.7 0.1 copy.25
  107.8 0.1 cos.20
  107.9 0.1 copy.24
  108.0 0.4 collective-permute-done.1
  108.4 1.8 %collective-permute-start.2 = (f32[4,32]{1,0:T(4,128)S(1)}, f32[4,32]{1,0:T(4,128)S(1)}, u32[]{:S(2)}, u32[]{:S(2)}) collective-permute-start(f32[4,32]{1,0:T(4,128)S(1)} %pad_maximum_fusion.2), channel_id=1, source_target_pairs={{128,0},{160,32},{192,64},{224,96},{0,128},{32,160},{64,192},{96,2... | collective-permute-start | bytes 1544 | tf_op jit(solution)/shard_map/ppermute | solution.py:323
  110.2 2.5 %collective-permute-done.2 = f32[4,32]{1,0:T(4,128)S(1)} collective-permute-done((f32[4,32]{1,0:T(4,128)S(1)}, f32[4,32]{1,0:T(4,128)S(1)}, u32[]{:S(2)}, u32[]{:S(2)}) %collective-permute-start.2) | collective-permute-done | bytes 544 | tf_op jit(solution)/shard_map/ppermute | solution.py:323
  112.9 18.8 %all-to-all-done.1 = f32[256,8,128]{2,1,0:T(8,128)S(1)} async-done(((f32[256,8,128]{2,1,0:T(8,128)}), f32[256,8,128]{2,1,0:T(8,128)S(1)}, u32[]{:S(2)}, u32[]{:S(2)}) %all-to-all-start.1) | async-done | bytes 1048608 | tf_op jit(solution)/shard_map/all_to_all | solution.py:368
  131.8 4.6 %spectral.1 = f32[8,256,128]{2,1,0:T(8,128)S(1)} custom-call(f32[8,32,8,128]{3,2,1,0:T(8,128)S(1)} %bitcast.13, f32[8,1,8,128]{3,2,1,0:T(8,128)S(1)} %broadcast_in_dim.2.l_ref, f32[2,128,128]{2,1,0:T(8,128)S(1)} %pad_maximum_fusion.ph_ref, bf16[2,256,256]{2,1,0:T(8,128)(2,1)S(1)} %copy-done, bf16[2,256,256]{2,1,0:T(8,128)(2,1)S(1)} %copy-done.1, ...), custom_call_target="tpu_custom_call" | custom-call | flops 3000000000 | bytes 4194304 | tf_op jit(solution)/shard_map/spectral/pallas_call | solution.py:305
  136.5 18.4 %all_to_all.15 = f32[8,256,128]{2,1,0:T(8,128)S(1)} all-to-all(f32[8,256,128]{2,1,0:T(8,128)S(1)} %spectral.1), channel_id=1, replica_groups=mesh['gz'=8,'ma'=32] {'gz'}, dimensions={0} | all-to-all | bytes 2097152 | tf_op jit(solution)/shard_map/all_to_all | solution.py:376
  154.9 0.2 copy.26
  155.1 1.2 reshape.53
  (28 shorter events, 0.4 us)
Async XLA Ops:
  3.8 12.2 %copy-start.6 = (s32[128,128]{1,0:T(8,128)S(1)}, s32[128,128]{1,0:T(8,128)}, u32[]{:S(2)}) copy-start(s32[128,128]{1,0:T(8,128)} %param.19) | copy-start | bytes 196612
  3.8 12.2 %copy-start.9 = (f32[8]{0:T(128)S(1)}, f32[8]{0:T(128)}, u32[]{:S(2)}) copy-start(f32[8]{0:T(128)} %param.20) | copy-start | bytes 100
  3.8 13.0 %copy-start.7 = (s32[1024]{0:T(1024)S(1)}, s32[1024]{0:T(1024)}, u32[]{:S(2)}) copy-start(s32[1024]{0:T(1024)} %param.18) | copy-start | bytes 12292
  3.8 60.6 %all-to-all-start = ((f32[32,4,32,128]{3,2,1,0:T(8,128)}), f32[32,4,32,128]{3,2,1,0:T(8,128)S(1)}, u32[]{:S(2)}, u32[]{:S(2)}) async-start(f32[32,4,32,128]{3,2,1,0:T(8,128)} %pack.1), calls=%async_computation | async-start | bytes 4194304 | tf_op jit(solution)/shard_map/all_to_all | solution.py:364
  64.5 1.4 copy-start.5
  89.2 11.3 %copy-start.8 = (f32[1,32]{1,0:T(1,128)S(1)}, f32[1,32]{1,0:T(1,128)}, u32[]{:S(2)}) copy-start(f32[1,32]{1,0:T(1,128)} %param.22) | copy-start | bytes 388
  89.2 42.6 %copy-start = (bf16[2,256,256]{2,1,0:T(8,128)(2,1)S(1)}, bf16[2,256,256]{2,1,0:T(8,128)(2,1)}, u32[]{:S(2)}) copy-start(bf16[2,256,256]{2,1,0:T(8,128)(2,1)} %constant.55.clone.w1_ref) | copy-start | bytes 786436
  89.2 42.6 %copy-start.1 = (bf16[2,256,256]{2,1,0:T(8,128)(2,1)S(1)}, bf16[2,256,256]{2,1,0:T(8,128)(2,1)}, u32[]{:S(2)}) copy-start(bf16[2,256,256]{2,1,0:T(8,128)(2,1)} %constant.56.clone.w2_ref) | copy-start | bytes 786436
  89.2 42.6 %copy-start.2 = (bf16[2,256,256]{2,1,0:T(8,128)(2,1)S(1)}, bf16[2,256,256]{2,1,0:T(8,128)(2,1)}, u32[]{:S(2)}) copy-start(bf16[2,256,256]{2,1,0:T(8,128)(2,1)} %constant.57.clone.w3_ref) | copy-start | bytes 786436
  89.2 42.6 %copy-start.3 = (bf16[2,256,256]{2,1,0:T(8,128)(2,1)S(1)}, bf16[2,256,256]{2,1,0:T(8,128)(2,1)}, u32[]{:S(2)}) copy-start(bf16[2,256,256]{2,1,0:T(8,128)(2,1)} %constant.58.clone.w4_ref) | copy-start | bytes 786436
  89.2 42.6 %copy-start.4 = (f32[2,32,128]{2,1,0:T(8,128)S(1)}, f32[2,32,128]{2,1,0:T(8,128)}, u32[]{:S(2)}) copy-start(f32[2,32,128]{2,1,0:T(8,128)} %constant.59.clone.tw_ref) | copy-start | bytes 98308
  89.2 42.5 %all-to-all-start.1 = ((f32[256,8,128]{2,1,0:T(8,128)}), f32[256,8,128]{2,1,0:T(8,128)S(1)}, u32[]{:S(2)}, u32[]{:S(2)}) async-start(f32[256,8,128]{2,1,0:T(8,128)} %bitcast.17), calls=%async_computation.1 | async-start | bytes 2097152 | tf_op jit(solution)/shard_map/all_to_all | solution.py:368
  100.5 3.7 %collective-permute-start = (f32[1,32]{1,0:T(1,128)S(1)}, f32[1,32]{1,0:T(1,128)S(1)}, u32[]{:S(2)}, u32[]{:S(2)}) collective-permute-start(f32[1,32]{1,0:T(1,128)S(1)} %copy-done.8), channel_id=1, source_target_pairs={{32,0},{64,32},{96,64},{128,96},{160,128},{192,160},{224,192},{0,2... | collective-permute-start | bytes 392 | tf_op jit(solution)/shard_map/ppermute | solution.py:323
  104.2 4.2 %collective-permute-start.1 = (f32[2,32]{1,0:T(2,128)S(1)}, f32[2,32]{1,0:T(2,128)S(1)}, u32[]{:S(2)}, u32[]{:S(2)}) collective-permute-start(f32[2,32]{1,0:T(2,128)S(1)} %pad_maximum_fusion.3), channel_id=1, source_target_pairs={{64,0},{96,32},{128,64},{160,96},{192,128},{224,160},{0,192},{32,2... | collective-permute-start | bytes 776 | tf_op jit(solution)/shard_map/ppermute | solution.py:323
  108.4 4.3 %collective-permute-start.2 = (f32[4,32]{1,0:T(4,128)S(1)}, f32[4,32]{1,0:T(4,128)S(1)}, u32[]{:S(2)}, u32[]{:S(2)}) collective-permute-start(f32[4,32]{1,0:T(4,128)S(1)} %pad_maximum_fusion.2), channel_id=1, source_target_pairs={{128,0},{160,32},{192,64},{224,96},{0,128},{32,160},{64,192},{96,2... | collective-permute-start | bytes 1544 | tf_op jit(solution)/shard_map/ppermute | solution.py:323

commit v4 on v2

--- a/solution.py
+++ b/solution.py
@@ -1,3 +1,4 @@
+import functools
 import math
 
 import jax
@@ -16,6 +17,7 @@
 BLOCK = 128
 OUTER = 32
 ZL = 8
+LIMIT = 24 * 2**20
 PER = 4
 BF = jnp.bfloat16
 F32 = jnp.float32
@@ -49,11 +51,66 @@
     return jnp.dot(a, b, preferred_element_type=F32)
 
 
-def kerr_kernel(x_ref, place_ref, back_ref, f2_ref, f3_ref, proj_ref, tt_ref, k_ref, o_ref,
-                xs, fs, gs, rs, ks, fb):
+def swapped(value):
+    return pltpu.roll(value, 64, 1)
+
+
+def pack_kernel(f_ref, c_ref, o_ref, *, half):
+    low = lax.broadcasted_iota(jnp.int32, (32, 128), 1) < 64
+    for j in range(f_ref.shape[3] // 128):
+        lanes = slice(j * 128, (j + 1) * 128)
+        for i, ref in enumerate((f_ref, c_ref)):
+            re, im = ref[0, 0, :, lanes], ref[0, 1, :, lanes]
+            if half:
+                o_ref[j, i] = jnp.where(low, swapped(re), im)
+            else:
+                o_ref[j, i] = jnp.where(low, re, swapped(im))
+
+
+def pack_call(forward, cotangent, half):
+    steps = 4
+    spec = pl.BlockSpec((1, 2, 32, TIME // steps), lambda i: (0, 0, 0, i))
+    return pl.pallas_call(
+        functools.partial(pack_kernel, half=half),
+        name="pack",
+        grid=(steps,),
+        out_shape=jax.ShapeDtypeStruct((32, 2, 32, 128), F32),
+        in_specs=[spec, spec],
+        out_specs=pl.BlockSpec((32 // steps, 2, 32, 128), lambda i: (i, 0, 0, 0)),
+        compiler_params=pltpu.CompilerParams(vmem_limit_bytes=60 * 2**20),
+        cost_estimate=pl.CostEstimate(flops=2**20, bytes_accessed=3 * 2**20, transcendentals=0),
+    )(forward, cotangent)
+
+
+def kerr_kernel(x_ref, order_ref, back_hbm, f2_ref, f3_ref, proj_hbm, tt_ref, k_ref, *refs, final):
+    if final:
+        other_hbm, o_hbm = refs[0], refs[1]
+        refs = refs[2:]
+    else:
+        o_ref = refs[0]
+        refs = refs[1:]
+    xs, fs, gs, rs, ks, fb, place_ref, back_ref, proj_ref, sems = refs[:10]
+    moves = [(proj_hbm, proj_ref), (back_hbm, back_ref)]
+    if final:
+        other_ref = refs[10]
+        moves.append((other_hbm, other_ref))
+    loads = [
+        pltpu.make_async_copy(source, target, sems.at[i])
+        for i, (source, target) in enumerate(moves)
+    ]
+    for load in loads:
+        load.start()
+
+    def one_hot(j, carry):
+        rows = pl.ds(pl.multiple_of(j * 32, 32), 32)
+        index = lax.broadcasted_iota(jnp.int32, (32, MODES), 0) + j * 32
+        place_ref[rows, :] = jnp.where(index == order_ref[...], 1.0, 0.0).astype(BF)
+        return carry
+
+    lax.fori_loop(0, 32, one_hot, 0, unroll=2)
     def split_in(j, carry):
         rows = pl.ds(pl.multiple_of(j * 32, 32), 32)
-        for f in range(4):
+        for f in range(2):
             head, tail = split(x_ref[j, f])
             xs[f, rows, 0:128] = head
             xs[f, rows, 128:256] = tail
@@ -65,38 +122,42 @@
         fs[f] = dot(place_ref[...], xs[f]).astype(BF)
         return carry
 
-    lax.fori_loop(0, 4, place, 0)
+    lax.fori_loop(0, 2, place, 0)
 
     def first(k, carry):
-        for pair in range(2):
-            got = []
-            for h in range(2):
-                rows = pl.ds(pl.multiple_of(k * 128 + h * 64, 64), 64)
-                a, b = fs[2 * pair, rows, :], fs[2 * pair + 1, rows, :]
-                head = jnp.concatenate([a[:, :128], b[:, :128]], axis=1)
-                tail = jnp.concatenate([a[:, 128:], b[:, 128:]], axis=1)
-                res = dot(f2_ref[...], jnp.concatenate([head, tail, head], axis=0))
-                got.append(res.reshape(32, 8, 256))
-            low = jnp.concatenate([got[0][:, :4], got[1][:, :4]], axis=1)
-            high = jnp.concatenate([got[0][:, 4:], got[1][:, 4:]], axis=1)
-            for c in range(2):
-                lanes = slice(c * 128, (c + 1) * 128)
-                gs[2 * pair + c, :, 0, k] = low[:, :, lanes]
-                gs[2 * pair + c, :, 1, k] = high[:, :, lanes]
-        return carry
-
-    lax.fori_loop(0, 8, first, 0)
+        got = []
+        for h in range(2):
+            rows = pl.ds(pl.multiple_of(k * 128 + h * 64, 64), 64)
+            a, b = fs[0, rows, :], fs[1, rows, :]
+            head = jnp.concatenate([a[:, :128], b[:, :128]], axis=1)
+            tail = jnp.concatenate([a[:, 128:], b[:, 128:]], axis=1)
+            res = dot(f2_ref[...], jnp.concatenate([head, tail, head], axis=0))
+            lanes = []
+            for f in range(2):
+                v0, v1 = res[:128, f * 128:(f + 1) * 128], res[128:, f * 128:(f + 1) * 128]
+                lanes += [jnp.where(low, v0, swapped(v1)), jnp.where(low, swapped(v0), v1)]
+            got.append([lane.reshape(16, 8, 128) for lane in lanes])
+        for f in range(4):
+            a, b = got[0][f], got[1][f]
+            lanes = slice(f * 128, (f + 1) * 128)
+            gs[:, 0, k, :, lanes] = jnp.concatenate([a[:, :4], b[:, :4]], axis=1)
+            gs[:, 1, k, :, lanes] = jnp.concatenate([a[:, 4:], b[:, 4:]], axis=1)
+        return carry
+
+    low = lax.broadcasted_iota(jnp.int32, (128, 128), 1) < 64
+    lax.fori_loop(0, 8, first, 0, unroll=2)
 
     def grid(v, parity, slot):
         for pair in range(2):
-            got = [split(gs[2 * pair + c, v, parity].reshape(64, 128)) for c in range(2)]
-            head = jnp.concatenate([got[0][0], got[1][0]], axis=1)
-            tail = jnp.concatenate([got[0][1], got[1][1]], axis=1)
+            head, tail = split(
+                gs[v, parity, :, :, pair * 256:(pair + 1) * 256].reshape(64, 256)
+            )
             fb[slot, pair] = dot(f3_ref[...], jnp.concatenate([head, tail, head], axis=0))
 
     def column(v, parity):
         u = 2 * v + parity
-        res = []
+        few = low[:32]
+        res = ([], [])
         for i in range(2):
             xr = slice(i * 128, (i + 1) * 128)
             er, ei = fb[parity, 0, xr, :128], fb[parity, 0, xr, 128:]
@@ -109,78 +170,113 @@
             right = jnp.concatenate(
                 [jnp.concatenate([gr_h, gi_h], axis=1), jnp.concatenate([gr_l, gi_l], axis=1)], axis=0
             )
-            t_h, t_l = split(tt_ref[...] * k_ref[pl.ds(2 * u + i, 1), :])
-            left = jnp.concatenate(
-                [
-                    jnp.concatenate([t_h, t_h], axis=1),
-                    jnp.concatenate([t_l, jnp.zeros_like(t_l)], axis=1),
-                ],
-                axis=0,
-            )
-            got = dot(left, right)
-            res.append(got[:32] + got[32:])
-        rows = pl.ds(pl.multiple_of(u * 16, 16), 16)
-        for g in range(4):
-            both = jnp.concatenate([res[i][g * 8:(g + 1) * 8] for i in range(2)], axis=0)
-            head, tail = split(both)
-            rs[0, g, rows, :] = head
-            rs[1, g, rows, :] = tail
+            left = []
+            for far in range(2):
+                t_h, t_l = split(tt_ref[...] * k_ref[pl.ds(2 * u + i + 64 * far, 1), :])
+                left.append(jnp.concatenate([t_h, t_h], axis=1))
+                left.append(jnp.concatenate([t_l, jnp.zeros_like(t_l)], axis=1))
+            got = dot(jnp.concatenate(left, axis=0), right)
+            near, far = got[:32] + got[32:64], got[64:96] + got[96:]
+            res[0].append(jnp.where(few, near[:, :128], swapped(near[:, 128:])))
+            res[1].append(jnp.where(few, swapped(far[:, :128]), far[:, 128:]))
+        for far in range(2):
+            rows = pl.ds(pl.multiple_of(u * 16 + 512 * far, 16), 16)
+            for g in range(4):
+                both = jnp.concatenate([res[far][i][g * 8:(g + 1) * 8] for i in range(2)], axis=0)
+                head, tail = split(both)
+                lanes = slice(g % 2 * 128, (g % 2 + 1) * 128)
+                rs[0, g // 2, rows, lanes] = head
+                rs[1, g // 2, rows, lanes] = tail
 
     def columns(v, carry):
         grid(v, 1, 1)
         column(v, 0)
-        grid(jnp.minimum(v + 1, GRID // 4 - 1), 0, 0)
+        grid(jnp.minimum(v + 1, GRID // 8 - 1), 0, 0)
         column(v, 1)
         return carry
 
     grid(0, 0, 0)
-    lax.fori_loop(0, GRID // 4, columns, 0, unroll=2)
+    lax.fori_loop(0, GRID // 8, columns, 0, unroll=2)
 
     def last(g, carry):
         head, tail = rs[0, g], rs[1, g]
         res = dot(proj_ref[0], head) + (dot(proj_ref[0], tail) + dot(proj_ref[1], head))
-        rows = pl.ds(pl.multiple_of(g * 256, 256), 256)
-        for c in range(2):
-            head, tail = split(res[:, c * 128:(c + 1) * 128])
-            ks[c, rows, 0:128] = head
-            ks[c, rows, 128:256] = tail
-        return carry
-
-    lax.fori_loop(0, 4, last, 0)
+        for i in range(2):
+            rows = pl.ds(pl.multiple_of(g * 512 + i * 256, 256), 256)
+            head, tail = split(res[:, i * 128:(i + 1) * 128])
+            ks[rows, 0:128] = head
+            ks[rows, 128:256] = tail
+        return carry
+
+    loads[0].wait()
+    lax.fori_loop(0, 2, last, 0)
+
+    half = lax.broadcasted_iota(jnp.int32, (256, 128), 1) < 64
+
+    def store(j):
+        part = pl.ds(j * 8, 8)
+        return pltpu.make_async_copy(refs[11].at[:, part], o_hbm.at[:, part], refs[12].at[j])
 
     def finish(j, carry):
         rows = pl.ds(pl.multiple_of(j * 256, 256), 256)
+        res = dot(back_ref[rows, :], ks[...])
+        res = res[:, :128] + res[:, 128:]
+        cot = jnp.concatenate([x_ref[j * 8 + i, 1] for i in range(8)], axis=0)
+        value = cot + res
+        if not final:
+            o_ref[rows, :] = value
+            return carry
+        other = other_ref[rows, :]
+        parts = (jnp.where(half, other, swapped(value)), jnp.where(half, swapped(other), value))
         for c in range(2):
-            res = dot(back_ref[rows, :], ks[c])
-            res = res[:, :128] + res[:, 128:]
             for i in range(8):
-                value = res[i * 32:(i + 1) * 32] + x_ref[j * 8 + i, 2 + c]
                 for g in range(8):
-                    o_ref[g, j * 8 + i, c * 4:(c + 1) * 4, :] = value[g * 4:(g + 1) * 4]
-        return carry
-
+                    row = i * 32 + g * 4
+                    refs[11][g, j * 8 + i, c * 4:(c + 1) * 4, :] = parts[c][row:row + 4]
+        store(j).start()
+        return carry
+
+    for load in loads[1:]:
+        load.wait()
     lax.fori_loop(0, 4, finish, 0)
-
-
-def kerr_call(received, *constants):
+    if final:
+        for j in range(4):
+            store(j).wait()
+
+
+def kerr_call(received, other, *constants):
     vm = pl.BlockSpec(memory_space=pltpu.VMEM)
+    hbm = pl.BlockSpec(memory_space=pl.ANY)
+    final = other is not None
+    shape = (ZL, 32, 8, 128) if final else (MODES, 128)
+    scratch = [
+        pltpu.VMEM((2, MODES, 256), BF),
+        pltpu.VMEM((2, MODES, 256), BF),
+        pltpu.VMEM((16, 2, 8, 8, 512), F32),
+        pltpu.VMEM((2, 2, MODES, 256), BF),
+        pltpu.VMEM((MODES, 256), BF),
+        pltpu.VMEM((2, 2, 256, 256), F32),
+        pltpu.VMEM((MODES, MODES), BF),
+        pltpu.VMEM((MODES, MODES), BF),
+        pltpu.VMEM((2, 256, MODES), BF),
+        pltpu.SemaphoreType.DMA((3 if final else 2,)),
+    ]
+    if final:
+        scratch += [
+            pltpu.VMEM((MODES, 128), F32),
+            pltpu.VMEM((ZL, 32, 8, 128), F32),
+            pltpu.SemaphoreType.DMA((4,)),
+        ]
     return pl.pallas_call(
-        kerr_kernel,
+        functools.partial(kerr_kernel, final=final),
         name="kerr",
-        out_shape=jax.ShapeDtypeStruct((ZL, 32, 8, 128), F32),
-        in_specs=[vm] * (1 + len(constants)),
-        out_specs=vm,
-        scratch_shapes=[
-            pltpu.VMEM((4, MODES, 256), BF),
-            pltpu.VMEM((4, MODES, 256), BF),
-            pltpu.VMEM((4, 32, 2, 8, 8, 128), F32),
-            pltpu.VMEM((2, 4, MODES, 256), BF),
-            pltpu.VMEM((2, MODES, 256), BF),
-            pltpu.VMEM((2, 2, 256, 256), F32),
-        ],
-        compiler_params=pltpu.CompilerParams(vmem_limit_bytes=48 * 2**20),
-        cost_estimate=pl.CostEstimate(flops=2 * 10**10, bytes_accessed=8 * 2**20, transcendentals=0),
-    )(received, *constants)
+        out_shape=jax.ShapeDtypeStruct(shape, F32),
+        in_specs=[vm, vm, hbm, vm, vm, hbm, vm, vm] + ([hbm] if final else []),
+        out_specs=hbm if final else vm,
+        scratch_shapes=scratch,
+        compiler_params=pltpu.CompilerParams(vmem_limit_bytes=LIMIT),
+        cost_estimate=pl.CostEstimate(flops=10**10, bytes_accessed=8 * 2**20, transcendentals=0),
+    )(received, *constants, *([other] if final else []))
 
 
 def three(a_h, a_l, b_h, b_l):
@@ -306,18 +402,18 @@
     matches = (region[None, :, :] == jnp.arange(REGIONS, dtype=jnp.int32)[:, None, None]).astype(F32)
     k = 2.0 * jnp.sum(matches * chi[:, None, None], axis=0).T
     index = jnp.arange(MODES, dtype=jnp.int32)
-    place = (index[:, None] == mode_order[None, :]).astype(BF)
     back = (mode_order[:, None] == index[None, :]).astype(BF)
-    return place, back, f2, f3, proj, tt, k
+    return mode_order[None, :], back, f2, f3, proj, tt, k
 
 
 def on_device(forward, cotangent, mode_order, region, chi, phase, loss):
     me = lax.axis_index("gz")
-    both = jnp.concatenate([forward[0], cotangent[0]], axis=0)
-    send = both.reshape(4, 32, 32, BLOCK).transpose(2, 0, 1, 3)
-    received = lax.all_to_all(send, "ma", split_axis=0, concat_axis=0, tiled=True)
     constants = kerr_constants(mode_order, region, chi)
-    source = kerr_call(received, *constants)
+    source = None
+    for half in range(2):
+        send = pack_call(forward, cotangent, half)
+        received = lax.all_to_all(send, "ma", split_axis=0, concat_axis=0, tiled=True)
+        source = kerr_call(received, source, *constants)
     source = source.reshape(256, 8, 128)
     gathered = lax.all_to_all(source, ("gz", "ma"), split_axis=0, concat_axis=0, tiled=True)
     factors = lax.dynamic_slice_in_dim(gathered_loss(loss), me * PER, PER, 1)

time: 156 us -> 160 us (1.026)
  waiting for transfers between devices: 67.2 us -> 53.4 us
  Pallas kernels: 28.4 us -> 41 us
  starting transfers between devices: 30.8 us -> 37.8 us
  other arithmetic: 5.77 us -> 2.01 us
    all_to_all x1 -> x2, waiting for transfers between devices: 45.5 us -> 31.7 us  [on_device(): lax.all_to_all(send, 'ma', split_axis=0, concat_axis=0, tiled=True)]
    pallas_call x1 -> x4, Pallas kernels: 23.7 us -> 36.4 us  [the longest x2 28.8 us: kerr_call(): pl.pallas_call(functools.partial(kerr_kernel, final=final), name='kerr',...]
    all_to_all x1 -> x2, starting transfers between devices: 12.2 us -> 18.5 us  [on_device(): lax.all_to_all(send, 'ma', split_axis=0, concat_axis=0, tiled=True)]
    unnamed x30 -> x32, local copies, waits for them, and re-layouts: 1.76 us -> 4.35 us
    convert_element_type x1, other arithmetic: 2.65 us -> 0.4 us  [kerr_constants(): back = (mode_order[:, None] == index[None, :]).astype(BF)]
  transfers between devices with their start and end apart: 5 -> 6, of which waited for: 4 -> 5; matrix products, arithmetic and copies ran while one was open for 3% -> 2% of each run, Pallas kernels for 0% -> 11%
where the time goes in v4:
time: 160 us; the launch traced here: 159 us
  waiting for transfers between devices  53.4 us (33%)
  Pallas kernels  41 us (26%)
  starting transfers between devices  37.8 us (24%)
  blocking collectives  18.4 us (11%)
  local copies, waits for them, and re-layouts  6.45 us (4%)
  other arithmetic  2.01 us (1%)
    all_to_all x2, waiting for transfers between devices, on_device(): lax.all_to_all(send, 'ma', split_axis=0, concat_axis=0, tiled=True)  31.7 us
    pallas_call x2, Pallas kernels, kerr_call(): pl.pallas_call(functools.partial(kerr_kernel, final=final), name='kerr',...  28.8 us
    all_to_all x1, waiting for transfers between devices, on_device(): lax.all_to_all(source, ('gz', 'ma'), split_axis=0, concat_axis=0, tiled=T...  18.8 us
    all_to_all x2, starting transfers between devices, on_device(): lax.all_to_all(send, 'ma', split_axis=0, concat_axis=0, tiled=True)  18.5 us
    all_to_all x1, blocking collectives, on_device(): lax.all_to_all(result, 'gz', split_axis=0, concat_axis=0, tiled=True)  18.4 us
    all_to_all x1, starting transfers between devices, on_device(): lax.all_to_all(source, ('gz', 'ma'), split_axis=0, concat_axis=0, tiled=T...  11.9 us
    pallas_call x2, Pallas kernels, pack_call(): pl.pallas_call(functools.partial(pack_kernel, half=half), name='pack', gr...  7.56 us
    ppermute x3, starting transfers between devices, gathered_loss(): have = jnp.concatenate([have, lax.ppermute(have, 'gz', route)], axis=0)  7.42 us
  transfers between devices with their start and end apart: 6, of which 5 were waited for; matrix products, arithmetic and copies ran while one was open for 2% of the time, Pallas kernels for 11%

profile of v4, /device:TPU:1, one launch (start us, length us, event | category | flops | bytes accessed | tf_op | source)
XLA Modules:
  0.0 159.4 jit_solution(12109137964271343382)
XLA Ops:
  0.0 3.8 %pack.3 = f32[32,2,32,128]{3,2,1,0:T(8,128)} custom-call(f32[1,2,32,4096]{3,2,1,0:T(8,128)} %f_ref.3, f32[1,2,32,4096]{3,2,1,0:T(8,128)} %c_ref.3), custom_call_target="tpu_custom_call" | custom-call | flops 1048576 | bytes 3145728 | tf_op jit(solution)/shard_map/pack/pallas_call | solution.py:73
  3.8 12.0 %all-to-all-start.1 = ((f32[32,2,32,128]{3,2,1,0:T(8,128)}), f32[32,2,32,128]{3,2,1,0:T(8,128)S(1)}, u32[]{:S(2)}, u32[]{:S(2)}) async-start(f32[32,2,32,128]{3,2,1,0:T(8,128)} %pack.3), calls=%async_computation.1 | async-start | bytes 2097152 | tf_op jit(solution)/shard_map/all_to_all | solution.py:415
  15.8 3.8 %pack.2 = f32[32,2,32,128]{3,2,1,0:T(8,128)} custom-call(f32[1,2,32,4096]{3,2,1,0:T(8,128)} %f_ref.3, f32[1,2,32,4096]{3,2,1,0:T(8,128)} %c_ref.3), custom_call_target="tpu_custom_call" | custom-call | flops 1048576 | bytes 3145728 | tf_op jit(solution)/shard_map/pack/pallas_call | solution.py:73
  19.6 22.4 %all-to-all-done.1.x_ref = f32[32,2,32,128]{3,2,1,0:T(8,128)S(1)} async-done(((f32[32,2,32,128]{3,2,1,0:T(8,128)}), f32[32,2,32,128]{3,2,1,0:T(8,128)S(1)}, u32[]{:S(2)}, u32[]{:S(2)}) %all-to-all-start.1) | async-done | bytes 1048608 | tf_op jit(solution)/shard_map/all_to_all | solution.py:415
  42.0 6.5 %all-to-all-start = ((f32[32,2,32,128]{3,2,1,0:T(8,128)}), f32[32,2,32,128]{3,2,1,0:T(8,128)}, u32[]{:S(2)}, u32[]{:S(2)}) async-start(f32[32,2,32,128]{3,2,1,0:T(8,128)} %pack.2), calls=%async_computation | async-start | bytes 2097152 | tf_op jit(solution)/shard_map/all_to_all | solution.py:415
  48.8 0.4 fusion.back_hbm
  49.2 1.2 copy-done.1
  50.4 13.2 %kerr.2.refs_0_ = f32[1024,128]{1,0:T(8,128)S(1)} custom-call(f32[32,2,32,128]{3,2,1,0:T(8,128)S(1)} %all-to-all-done.1.x_ref, s32[1,1024]{1,0:T(1,128)S(1)} %bitcast.15, bf16[1024,1024]{1,0:T(8,128)(2,1)S(1)} %fusion.back_hbm, bf16[256,192]{1,0:T(8,128)(2,1)S(1)} %copy-done.8, bf16[256,192]{1,0:T(8,128)(2,1)S(1)} %copy-done.7, ...), custom_call_target="tpu_custom_call" | custom-call | flops 10000000000 | bytes 8388608 | tf_op jit(solution)/shard_map/kerr/pallas_call | solution.py:270
  63.7 0.8 copy-done.11
  64.5 9.4 %all-to-all-done.x_ref = f32[32,2,32,128]{3,2,1,0:T(8,128)} async-done(((f32[32,2,32,128]{3,2,1,0:T(8,128)}), f32[32,2,32,128]{3,2,1,0:T(8,128)}, u32[]{:S(2)}, u32[]{:S(2)}) %all-to-all-start) | async-done | bytes 1048608 | tf_op jit(solution)/shard_map/all_to_all | solution.py:415
  73.9 1.2 copy-done.2
  75.1 1.0 copy-done.12
  76.2 15.6 %kerr.3 = f32[8,32,8,128]{3,2,1,0:T(8,128)} custom-call(f32[32,2,32,128]{3,2,1,0:T(8,128)} %all-to-all-done.x_ref, s32[1,1024]{1,0:T(1,128)S(1)} %bitcast.16, bf16[1024,1024]{1,0:T(8,128)(2,1)S(1)} %fusion.back_hbm, bf16[256,192]{1,0:T(8,128)(2,1)S(1)} %copy-done.8, bf16[256,192]{1,0:T(8,128)(2,1)S(1)} %copy-done.7, bf16[2,256,1024]{2,1,0:T(8,128)(2,1)S(1)} %copy-done.2, ...), custom_call_target="tpu_custom_call" | custom-call | flops 10000000000 | bytes 8388608 | tf_op jit(solution)/shard_map/kerr/pallas_call | solution.py:270
  91.8 11.9 %all-to-all-start.2 = ((f32[256,8,128]{2,1,0:T(8,128)}), f32[256,8,128]{2,1,0:T(8,128)S(1)}, u32[]{:S(2)}, u32[]{:S(2)}) async-start(f32[256,8,128]{2,1,0:T(8,128)} %bitcast.2), calls=%async_computation.2 | async-start | bytes 2097152 | tf_op jit(solution)/shard_map/all_to_all | solution.py:418
  103.7 2.2 %collective-permute-start = (f32[1,32]{1,0:T(1,128)S(1)}, f32[1,32]{1,0:T(1,128)S(1)}, u32[]{:S(2)}, u32[]{:S(2)}) collective-permute-start(f32[1,32]{1,0:T(1,128)S(1)} %copy-done.14), channel_id=1, source_target_pairs={{32,0},{64,32},{96,64},{128,96},{160,128},{192,160},{224,192},{0,2... | collective-permute-start | bytes 392 | tf_op jit(solution)/shard_map/ppermute | solution.py:372
  105.8 1.4 dynamic-slice_cosine_fusion
  107.4 3.5 %collective-permute-start.1 = (f32[2,32]{1,0:T(2,128)S(1)}, f32[2,32]{1,0:T(2,128)S(1)}, u32[]{:S(2)}, u32[]{:S(2)}) collective-permute-start(f32[2,32]{1,0:T(2,128)S(1)} %pad_maximum_fusion.3), channel_id=1, source_target_pairs={{64,0},{96,32},{128,64},{160,96},{192,128},{224,160},{0,192},{32,2... | collective-permute-start | bytes 776 | tf_op jit(solution)/shard_map/ppermute | solution.py:372
  111.2 0.4 collective-permute-done.1
  111.6 1.8 %collective-permute-start.2 = (f32[4,32]{1,0:T(4,128)S(1)}, f32[4,32]{1,0:T(4,128)S(1)}, u32[]{:S(2)}, u32[]{:S(2)}) collective-permute-start(f32[4,32]{1,0:T(4,128)S(1)} %pad_maximum_fusion.2), channel_id=1, source_target_pairs={{128,0},{160,32},{192,64},{224,96},{0,128},{32,160},{64,192},{96,2... | collective-permute-start | bytes 1544 | tf_op jit(solution)/shard_map/ppermute | solution.py:372
  113.4 2.5 %collective-permute-done.2 = f32[4,32]{1,0:T(4,128)S(1)} collective-permute-done((f32[4,32]{1,0:T(4,128)S(1)}, f32[4,32]{1,0:T(4,128)S(1)}, u32[]{:S(2)}, u32[]{:S(2)}) %collective-permute-start.2) | collective-permute-done | bytes 544 | tf_op jit(solution)/shard_map/ppermute | solution.py:372
  116.1 18.8 %all-to-all-done.2 = f32[256,8,128]{2,1,0:T(8,128)S(1)} async-done(((f32[256,8,128]{2,1,0:T(8,128)}), f32[256,8,128]{2,1,0:T(8,128)S(1)}, u32[]{:S(2)}, u32[]{:S(2)}) %all-to-all-start.2) | async-done | bytes 1048608 | tf_op jit(solution)/shard_map/all_to_all | solution.py:418
  135.0 4.6 %spectral.1 = f32[8,256,128]{2,1,0:T(8,128)S(1)} custom-call(f32[8,32,8,128]{3,2,1,0:T(8,128)S(1)} %bitcast.14, f32[8,1,8,128]{3,2,1,0:T(8,128)S(1)} %broadcast_in_dim.5.l_ref, f32[2,128,128]{2,1,0:T(8,128)S(1)} %pad_maximum_fusion.ph_ref, bf16[2,256,256]{2,1,0:T(8,128)(2,1)S(1)} %copy-done.6, bf16[2,256,256]{2,1,0:T(8,128)(2,1)S(1)} %copy-done.5, ...), custom_call_target="tpu_custom_call" | custom-call | flops 3000000000 | bytes 4194304 | tf_op jit(solution)/shard_map/spectral/pallas_call | solution.py:354
  139.6 18.4 %all_to_all.20 = f32[8,256,128]{2,1,0:T(8,128)S(1)} all-to-all(f32[8,256,128]{2,1,0:T(8,128)S(1)} %spectral.1), channel_id=1, replica_groups=mesh['gz'=8,'ma'=32] {'gz'}, dimensions={0} | all-to-all | bytes 2097152 | tf_op jit(solution)/shard_map/all_to_all | solution.py:426
  158.2 1.2 reshape.52
  (44 shorter events, 1.3 us)
Async XLA Ops:
  3.8 38.2 %all-to-all-start.1 = ((f32[32,2,32,128]{3,2,1,0:T(8,128)}), f32[32,2,32,128]{3,2,1,0:T(8,128)S(1)}, u32[]{:S(2)}, u32[]{:S(2)}) async-start(f32[32,2,32,128]{3,2,1,0:T(8,128)} %pack.3), calls=%async_computation.1 | async-start | bytes 2097152 | tf_op jit(solution)/shard_map/all_to_all | solution.py:415
  15.8 32.7 %copy-start.13 = (s32[128,128]{1,0:T(8,128)S(1)}, s32[128,128]{1,0:T(8,128)}, u32[]{:S(2)}) copy-start(s32[128,128]{1,0:T(8,128)} %param.19) | copy-start | bytes 196612
  15.8 32.7 %copy-start.15 = (f32[8]{0:T(128)S(1)}, f32[8]{0:T(128)}, u32[]{:S(2)}) copy-start(f32[8]{0:T(128)} %param.20) | copy-start | bytes 100
  15.8 32.9 %copy-start = (s32[1024]{0:T(1024)S(1)}, s32[1024]{0:T(1024)}, u32[]{:S(2)}) copy-start(s32[1024]{0:T(1024)} %param.18) | copy-start | bytes 12292
  19.6 29.6 %copy-start.7 = (bf16[256,192]{1,0:T(8,128)(2,1)S(1)}, bf16[256,192]{1,0:T(8,128)(2,1)}, u32[]{:S(2)}) copy-start(bf16[256,192]{1,0:T(8,128)(2,1)} %constant.52.clone.f3_ref) | copy-start | bytes 294916
  19.6 29.6 %copy-start.8 = (bf16[256,192]{1,0:T(8,128)(2,1)S(1)}, bf16[256,192]{1,0:T(8,128)(2,1)}, u32[]{:S(2)}) copy-start(bf16[256,192]{1,0:T(8,128)(2,1)} %constant.51.clone.f2_ref) | copy-start | bytes 294916
  19.6 29.6 %copy-start.10 = (f32[32,128]{1,0:T(8,128)S(1)}, f32[32,128]{1,0:T(8,128)}, u32[]{:S(2)}) copy-start(f32[32,128]{1,0:T(8,128)} %constant.54.clone.tt_ref) | copy-start | bytes 49156
  42.0 31.9 %all-to-all-start = ((f32[32,2,32,128]{3,2,1,0:T(8,128)}), f32[32,2,32,128]{3,2,1,0:T(8,128)}, u32[]{:S(2)}, u32[]{:S(2)}) async-start(f32[32,2,32,128]{3,2,1,0:T(8,128)} %pack.2), calls=%async_computation | async-start | bytes 2097152 | tf_op jit(solution)/shard_map/all_to_all | solution.py:415
  49.2 1.2 copy-start.1
  63.7 0.8 copy-start.11
  73.9 1.2 copy-start.2
  75.1 1.0 copy-start.12
  91.7 11.9 %copy-start.14 = (f32[1,32]{1,0:T(1,128)S(1)}, f32[1,32]{1,0:T(1,128)}, u32[]{:S(2)}) copy-start(f32[1,32]{1,0:T(1,128)} %param.22) | copy-start | bytes 388
  91.7 43.2 %copy-start.3 = (bf16[2,256,256]{2,1,0:T(8,128)(2,1)S(1)}, bf16[2,256,256]{2,1,0:T(8,128)(2,1)}, u32[]{:S(2)}) copy-start(bf16[2,256,256]{2,1,0:T(8,128)(2,1)} %constant.58.clone.w4_ref) | copy-start | bytes 786436
  91.7 43.2 %copy-start.4 = (bf16[2,256,256]{2,1,0:T(8,128)(2,1)S(1)}, bf16[2,256,256]{2,1,0:T(8,128)(2,1)}, u32[]{:S(2)}) copy-start(bf16[2,256,256]{2,1,0:T(8,128)(2,1)} %constant.57.clone.w3_ref) | copy-start | bytes 786436
  91.8 43.2 %copy-start.5 = (bf16[2,256,256]{2,1,0:T(8,128)(2,1)S(1)}, bf16[2,256,256]{2,1,0:T(8,128)(2,1)}, u32[]{:S(2)}) copy-start(bf16[2,256,256]{2,1,0:T(8,128)(2,1)} %constant.56.clone.w2_ref) | copy-start | bytes 786436
  91.8 43.2 %copy-start.6 = (bf16[2,256,256]{2,1,0:T(8,128)(2,1)S(1)}, bf16[2,256,256]{2,1,0:T(8,128)(2,1)}, u32[]{:S(2)}) copy-start(bf16[2,256,256]{2,1,0:T(8,128)(2,1)} %constant.55.clone.w1_ref) | copy-start | bytes 786436
  91.8 43.2 %copy-start.9 = (f32[2,32,128]{2,1,0:T(8,128)S(1)}, f32[2,32,128]{2,1,0:T(8,128)}, u32[]{:S(2)}) copy-start(f32[2,32,128]{2,1,0:T(8,128)} %constant.59.clone.tw_ref) | copy-start | bytes 98308
  91.8 43.1 %all-to-all-start.2 = ((f32[256,8,128]{2,1,0:T(8,128)}), f32[256,8,128]{2,1,0:T(8,128)S(1)}, u32[]{:S(2)}, u32[]{:S(2)}) async-start(f32[256,8,128]{2,1,0:T(8,128)} %bitcast.2), calls=%async_computation.2 | async-start | bytes 2097152 | tf_op jit(solution)/shard_map/all_to_all | solution.py:418
  103.7 3.7 %collective-permute-start = (f32[1,32]{1,0:T(1,128)S(1)}, f32[1,32]{1,0:T(1,128)S(1)}, u32[]{:S(2)}, u32[]{:S(2)}) collective-permute-start(f32[1,32]{1,0:T(1,128)S(1)} %copy-done.14), channel_id=1, source_target_pairs={{32,0},{64,32},{96,64},{128,96},{160,128},{192,160},{224,192},{0,2... | collective-permute-start | bytes 392 | tf_op jit(solution)/shard_map/ppermute | solution.py:372
  107.4 4.2 %collective-permute-start.1 = (f32[2,32]{1,0:T(2,128)S(1)}, f32[2,32]{1,0:T(2,128)S(1)}, u32[]{:S(2)}, u32[]{:S(2)}) collective-permute-start(f32[2,32]{1,0:T(2,128)S(1)} %pad_maximum_fusion.3), channel_id=1, source_target_pairs={{64,0},{96,32},{128,64},{160,96},{192,128},{224,160},{0,192},{32,2... | collective-permute-start | bytes 776 | tf_op jit(solution)/shard_map/ppermute | solution.py:372
  111.6 4.3 %collective-permute-start.2 = (f32[4,32]{1,0:T(4,128)S(1)}, f32[4,32]{1,0:T(4,128)S(1)}, u32[]{:S(2)}, u32[]{:S(2)}) collective-permute-start(f32[4,32]{1,0:T(4,128)S(1)} %pad_maximum_fusion.2), channel_id=1, source_target_pairs={{128,0},{160,32},{192,64},{224,96},{0,128},{32,160},{64,192},{96,2... | collective-permute-start | bytes 1544 | tf_op jit(solution)/shard_map/ppermute | solution.py:372

commit v5 on v3

--- a/solution.py
+++ b/solution.py
@@ -16,6 +16,7 @@
 BLOCK = 128
 OUTER = 32
 ZL = 8
+LIMIT = 48 * 2**20
 PER = 4
 BF = jnp.bfloat16
 F32 = jnp.float32
@@ -70,16 +71,24 @@
     )(forward, cotangent)
 
 
-def kerr_kernel(x_ref, place_hbm, back_hbm, f2_ref, f3_ref, proj_hbm, tt_ref, k_ref, o_hbm,
+def kerr_kernel(x_ref, order_ref, back_hbm, f2_ref, f3_ref, proj_hbm, tt_ref, k_ref, o_hbm,
                 xs, fs, gs, rs, ks, fb, place_ref, back_ref, proj_ref, o_ref, sems, out_sems):
     loads = [
         pltpu.make_async_copy(source, target, sems.at[i])
         for i, (source, target) in enumerate(
-            ((place_hbm, place_ref), (proj_hbm, proj_ref), (back_hbm, back_ref))
+            ((proj_hbm, proj_ref), (back_hbm, back_ref))
         )
     ]
     for load in loads:
         load.start()
+
+    def one_hot(j, carry):
+        rows = pl.ds(pl.multiple_of(j * 32, 32), 32)
+        index = lax.broadcasted_iota(jnp.int32, (32, MODES), 0) + j * 32
+        place_ref[rows, :] = jnp.where(index == order_ref[...], 1.0, 0.0).astype(BF)
+        return carry
+
+    lax.fori_loop(0, 32, one_hot, 0, unroll=2)
 
     def split_in(j, carry):
         rows = pl.ds(pl.multiple_of(j * 32, 32), 32)
@@ -95,7 +104,6 @@
         fs[f] = dot(place_ref[...], xs[f]).astype(BF)
         return carry
 
-    loads[0].wait()
     lax.fori_loop(0, 4, place, 0)
 
     def first(k, carry):
@@ -177,7 +185,7 @@
             ks[c, rows, 128:256] = tail
         return carry
 
-    loads[1].wait()
+    loads[0].wait()
     lax.fori_loop(0, 4, last, 0, unroll=2)
 
     def store(j):
@@ -196,7 +204,7 @@
         store(j).start()
         return carry
 
-    loads[2].wait()
+    loads[1].wait()
     lax.fori_loop(0, 4, finish, 0)
     for j in range(4):
         store(j).wait()
@@ -209,7 +217,7 @@
         kerr_kernel,
         name="kerr",
         out_shape=jax.ShapeDtypeStruct((ZL, 32, 8, 128), F32),
-        in_specs=[vm, hbm, hbm, vm, vm, hbm, vm, vm],
+        in_specs=[vm, vm, hbm, vm, vm, hbm, vm, vm],
         out_specs=hbm,
         scratch_shapes=[
             pltpu.VMEM((4, MODES, 256), BF),
@@ -222,10 +230,10 @@
             pltpu.VMEM((MODES, MODES), BF),
             pltpu.VMEM((2, 256, MODES), BF),
             pltpu.VMEM((ZL, 32, 8, 128), F32),
-            pltpu.SemaphoreType.DMA((3,)),
+            pltpu.SemaphoreType.DMA((2,)),
             pltpu.SemaphoreType.DMA((4,)),
         ],
-        compiler_params=pltpu.CompilerParams(vmem_limit_bytes=54 * 2**20),
+        compiler_params=pltpu.CompilerParams(vmem_limit_bytes=LIMIT),
         cost_estimate=pl.CostEstimate(flops=2 * 10**10, bytes_accessed=8 * 2**20, transcendentals=0),
     )(received, *constants)
 
@@ -271,7 +279,7 @@
         o_ref[z0 + 1] = final[:, 128:]
         return carry
 
-    lax.fori_loop(0, ZL // 2, pair, 0)
+    lax.fori_loop(0, ZL // 2, pair, 0, unroll=4)
 
 
 def spectral_constants():
@@ -353,9 +361,8 @@
     matches = (region[None, :, :] == jnp.arange(REGIONS, dtype=jnp.int32)[:, None, None]).astype(F32)
     k = 2.0 * jnp.sum(matches * chi[:, None, None], axis=0).T
     index = jnp.arange(MODES, dtype=jnp.int32)
-    place = (index[:, None] == mode_order[None, :]).astype(BF)
     back = (mode_order[:, None] == index[None, :]).astype(BF)
-    return place, back, f2, f3, proj, tt, k
+    return mode_order[None, :], back, f2, f3, proj, tt, k
 
 
 def on_device(forward, cotangent, mode_order, region, chi, phase, loss):

time: 157 us -> 152 us (0.968)
  Pallas kernels: 31.8 us -> 28.3 us
    pallas_call x1, Pallas kernels: 23.4 us -> 21.1 us  [kerr_call(): pl.pallas_call(kerr_kernel, name='kerr', out_shape=jax.ShapeDtypeStruct((...]
where the time goes in v5:
time: 152 us; the launch traced here: 151 us
  waiting for transfers between devices  65.7 us (43%)
  starting transfers between devices  30.8 us (20%)
  Pallas kernels  28.3 us (19%)
  blocking collectives  18.4 us (12%)
  other arithmetic  5.12 us (3%)
  local copies, waits for them, and re-layouts  2.82 us (2%)
    all_to_all x1, waiting for transfers between devices, on_device(): lax.all_to_all(send, 'ma', split_axis=0, concat_axis=0, tiled=True)  44 us
    pallas_call x1, Pallas kernels, kerr_call(): pl.pallas_call(kerr_kernel, name='kerr', out_shape=jax.ShapeDtypeStruct((...  21.1 us
    all_to_all x1, waiting for transfers between devices, on_device(): lax.all_to_all(source, ('gz', 'ma'), split_axis=0, concat_axis=0, tiled=T...  18.8 us
    all_to_all x1, blocking collectives, on_device(): lax.all_to_all(result, 'gz', split_axis=0, concat_axis=0, tiled=True)  18.4 us
    all_to_all x1, starting transfers between devices, on_device(): lax.all_to_all(send, 'ma', split_axis=0, concat_axis=0, tiled=True)  12.2 us
    all_to_all x1, starting transfers between devices, on_device(): lax.all_to_all(source, ('gz', 'ma'), split_axis=0, concat_axis=0, tiled=T...  11.3 us
    ppermute x3, starting transfers between devices, gathered_loss(): have = jnp.concatenate([have, lax.ppermute(have, 'gz', route)], axis=0)  7.42 us
    pallas_call x1, Pallas kernels, pack_call(): pl.pallas_call(pack_kernel, name='pack', grid=(steps,), out_shape=jax.Sha...  3.78 us
  transfers between devices with their start and end apart: 5, of which 4 were waited for; matrix products, arithmetic and copies ran while one was open for 4% of the time, Pallas kernels for 0%

profile of v5, /device:TPU:1, one launch (start us, length us, event | category | flops | bytes accessed | tf_op | source)
XLA Modules:
  0.0 151.4 jit_solution(13366378643153986242)
XLA Ops:
  0.0 3.8 %pack.1 = f32[32,4,32,128]{3,2,1,0:T(8,128)} custom-call(f32[1,2,32,4096]{3,2,1,0:T(8,128)} %f_ref.1, f32[1,2,32,4096]{3,2,1,0:T(8,128)} %c_ref.1), custom_call_target="tpu_custom_call" | custom-call | flops 1048576 | bytes 4194304 | tf_op jit(solution)/shard_map/pack/pallas_call | solution.py:62
  3.8 12.2 %all-to-all-start = ((f32[32,4,32,128]{3,2,1,0:T(8,128)}), f32[32,4,32,128]{3,2,1,0:T(8,128)S(1)}, u32[]{:S(2)}, u32[]{:S(2)}) async-start(f32[32,4,32,128]{3,2,1,0:T(8,128)} %pack.1), calls=%async_computation | async-start | bytes 4194304 | tf_op jit(solution)/shard_map/all_to_all | solution.py:371
  16.0 1.1 select_reduce_fusion
  17.1 0.7 copy.23
  17.8 0.8 multiply_bitcast_fusion.k_ref
  18.6 1.7 %fusion.back_hbm = bf16[1024,1024]{1,0:T(8,128)(2,1)} fusion(s32[1024]{0:T(1024)S(1)} %copy-done), kind=kLoop, calls=%fused_computation.1 | loop fusion | flops 2097152 | bytes 2101248 | tf_op jit(solution)/shard_map/convert_element_type | solution.py:364
  20.4 44.0 %all-to-all-done.x_ref = f32[32,4,32,128]{3,2,1,0:T(8,128)S(1)} async-done(((f32[32,4,32,128]{3,2,1,0:T(8,128)}), f32[32,4,32,128]{3,2,1,0:T(8,128)S(1)}, u32[]{:S(2)}, u32[]{:S(2)}) %all-to-all-start) | async-done | bytes 2097184 | tf_op jit(solution)/shard_map/all_to_all | solution.py:371
  64.4 21.1 %kerr.1 = f32[8,32,8,128]{3,2,1,0:T(8,128)} custom-call(f32[32,4,32,128]{3,2,1,0:T(8,128)S(1)} %all-to-all-done.x_ref, s32[1,1024]{1,0:T(1,128)S(1)} %bitcast.15, bf16[1024,1024]{1,0:T(8,128)(2,1)} %fusion.back_hbm, bf16[256,192]{1,0:T(8,128)(2,1)S(1)} %copy-done.6, bf16[256,192]{1,0:T(8,128)(2,1)S(1)} %copy-done.7, bf16[2,256,1024]{2,1,0:T(8,128)(2,1)S(1)} %copy-done.1, ...), custom_call_target="tpu_custom_call" | custom-call | flops 20000000000 | bytes 8388608 | tf_op jit(solution)/shard_map/kerr/pallas_call | solution.py:216
  85.6 11.3 %all-to-all-start.1 = ((f32[256,8,128]{2,1,0:T(8,128)}), f32[256,8,128]{2,1,0:T(8,128)S(1)}, u32[]{:S(2)}, u32[]{:S(2)}) async-start(f32[256,8,128]{2,1,0:T(8,128)} %bitcast.2), calls=%async_computation.1 | async-start | bytes 2097152 | tf_op jit(solution)/shard_map/all_to_all | solution.py:375
  96.9 2.2 %collective-permute-start = (f32[1,32]{1,0:T(1,128)S(1)}, f32[1,32]{1,0:T(1,128)S(1)}, u32[]{:S(2)}, u32[]{:S(2)}) collective-permute-start(f32[1,32]{1,0:T(1,128)S(1)} %copy-done.10), channel_id=1, source_target_pairs={{32,0},{64,32},{96,64},{128,96},{160,128},{192,160},{224,192},{0,2... | collective-permute-start | bytes 392 | tf_op jit(solution)/shard_map/ppermute | solution.py:331
  99.1 1.4 dynamic-slice_cosine_fusion
  100.4 0.1 neg.20
  100.6 3.5 %collective-permute-start.1 = (f32[2,32]{1,0:T(2,128)S(1)}, f32[2,32]{1,0:T(2,128)S(1)}, u32[]{:S(2)}, u32[]{:S(2)}) collective-permute-start(f32[2,32]{1,0:T(2,128)S(1)} %pad_maximum_fusion.3), channel_id=1, source_target_pairs={{64,0},{96,32},{128,64},{160,96},{192,128},{224,160},{0,192},{32,2... | collective-permute-start | bytes 776 | tf_op jit(solution)/shard_map/ppermute | solution.py:331
  104.1 0.1 copy.25
  104.2 0.1 cos.20
  104.3 0.1 copy.24
  104.4 0.4 collective-permute-done.1
  104.8 1.8 %collective-permute-start.2 = (f32[4,32]{1,0:T(4,128)S(1)}, f32[4,32]{1,0:T(4,128)S(1)}, u32[]{:S(2)}, u32[]{:S(2)}) collective-permute-start(f32[4,32]{1,0:T(4,128)S(1)} %pad_maximum_fusion.2), channel_id=1, source_target_pairs={{128,0},{160,32},{192,64},{224,96},{0,128},{32,160},{64,192},{96,2... | collective-permute-start | bytes 1544 | tf_op jit(solution)/shard_map/ppermute | solution.py:331
  106.6 2.5 %collective-permute-done.2 = f32[4,32]{1,0:T(4,128)S(1)} collective-permute-done((f32[4,32]{1,0:T(4,128)S(1)}, f32[4,32]{1,0:T(4,128)S(1)}, u32[]{:S(2)}, u32[]{:S(2)}) %collective-permute-start.2) | collective-permute-done | bytes 544 | tf_op jit(solution)/shard_map/ppermute | solution.py:331
  109.3 18.8 %all-to-all-done.1 = f32[256,8,128]{2,1,0:T(8,128)S(1)} async-done(((f32[256,8,128]{2,1,0:T(8,128)}), f32[256,8,128]{2,1,0:T(8,128)S(1)}, u32[]{:S(2)}, u32[]{:S(2)}) %all-to-all-start.1) | async-done | bytes 1048608 | tf_op jit(solution)/shard_map/all_to_all | solution.py:375
  128.2 3.4 %spectral.1 = f32[8,256,128]{2,1,0:T(8,128)S(1)} custom-call(f32[8,32,8,128]{3,2,1,0:T(8,128)S(1)} %bitcast.14, f32[8,1,8,128]{3,2,1,0:T(8,128)S(1)} %broadcast_in_dim.5.l_ref, f32[2,128,128]{2,1,0:T(8,128)S(1)} %pad_maximum_fusion.ph_ref, bf16[2,256,256]{2,1,0:T(8,128)(2,1)S(1)} %copy-done.2, bf16[2,256,256]{2,1,0:T(8,128)(2,1)S(1)} %copy-done.3, ...), custom_call_target="tpu_custom_call" | custom-call | flops 3000000000 | bytes 4194304 | tf_op jit(solution)/shard_map/spectral/pallas_call | solution.py:313
  131.6 18.4 %all_to_all.15 = f32[8,256,128]{2,1,0:T(8,128)S(1)} all-to-all(f32[8,256,128]{2,1,0:T(8,128)S(1)} %spectral.1), channel_id=1, replica_groups=mesh['gz'=8,'ma'=32] {'gz'}, dimensions={0} | all-to-all | bytes 2097152 | tf_op jit(solution)/shard_map/all_to_all | solution.py:383
  150.0 0.2 copy.26
  150.2 1.2 reshape.52
  (32 shorter events, 0.4 us)
Async XLA Ops:
  3.8 12.2 %copy-start.11 = (f32[8]{0:T(128)S(1)}, f32[8]{0:T(128)}, u32[]{:S(2)}) copy-start(f32[8]{0:T(128)} %param.20) | copy-start | bytes 100
  3.8 14.9 %copy-start = (s32[1024]{0:T(1024)S(1)}, s32[1024]{0:T(1024)}, u32[]{:S(2)}) copy-start(s32[1024]{0:T(1024)} %param.18) | copy-start | bytes 12292
  3.8 60.6 %all-to-all-start = ((f32[32,4,32,128]{3,2,1,0:T(8,128)}), f32[32,4,32,128]{3,2,1,0:T(8,128)S(1)}, u32[]{:S(2)}, u32[]{:S(2)}) async-start(f32[32,4,32,128]{3,2,1,0:T(8,128)} %pack.1), calls=%async_computation | async-start | bytes 4194304 | tf_op jit(solution)/shard_map/all_to_all | solution.py:371
  16.0 48.5 %copy-start.1 = (bf16[2,256,1024]{2,1,0:T(8,128)(2,1)S(1)}, bf16[2,256,1024]{2,1,0:T(8,128)(2,1)}, u32[]{:S(2)}) copy-start(bf16[2,256,1024]{2,1,0:T(8,128)(2,1)} %constant.53.clone.proj_hbm) | copy-start | bytes 3145732
  16.0 48.5 %copy-start.6 = (bf16[256,192]{1,0:T(8,128)(2,1)S(1)}, bf16[256,192]{1,0:T(8,128)(2,1)}, u32[]{:S(2)}) copy-start(bf16[256,192]{1,0:T(8,128)(2,1)} %constant.51.clone.f2_ref) | copy-start | bytes 294916
  16.0 48.4 %copy-start.7 = (bf16[256,192]{1,0:T(8,128)(2,1)S(1)}, bf16[256,192]{1,0:T(8,128)(2,1)}, u32[]{:S(2)}) copy-start(bf16[256,192]{1,0:T(8,128)(2,1)} %constant.52.clone.f3_ref) | copy-start | bytes 294916
  16.0 48.4 %copy-start.9 = (f32[32,128]{1,0:T(8,128)S(1)}, f32[32,128]{1,0:T(8,128)}, u32[]{:S(2)}) copy-start(f32[32,128]{1,0:T(8,128)} %constant.54.clone.tt_ref) | copy-start | bytes 49156
  85.6 11.3 %copy-start.10 = (f32[1,32]{1,0:T(1,128)S(1)}, f32[1,32]{1,0:T(1,128)}, u32[]{:S(2)}) copy-start(f32[1,32]{1,0:T(1,128)} %param.22) | copy-start | bytes 388
  85.6 42.6 %copy-start.2 = (bf16[2,256,256]{2,1,0:T(8,128)(2,1)S(1)}, bf16[2,256,256]{2,1,0:T(8,128)(2,1)}, u32[]{:S(2)}) copy-start(bf16[2,256,256]{2,1,0:T(8,128)(2,1)} %constant.55.clone.w1_ref) | copy-start | bytes 786436
  85.6 42.6 %copy-start.3 = (bf16[2,256,256]{2,1,0:T(8,128)(2,1)S(1)}, bf16[2,256,256]{2,1,0:T(8,128)(2,1)}, u32[]{:S(2)}) copy-start(bf16[2,256,256]{2,1,0:T(8,128)(2,1)} %constant.56.clone.w2_ref) | copy-start | bytes 786436
  85.6 42.6 %copy-start.4 = (bf16[2,256,256]{2,1,0:T(8,128)(2,1)S(1)}, bf16[2,256,256]{2,1,0:T(8,128)(2,1)}, u32[]{:S(2)}) copy-start(bf16[2,256,256]{2,1,0:T(8,128)(2,1)} %constant.57.clone.w3_ref) | copy-start | bytes 786436
  85.6 42.6 %copy-start.5 = (bf16[2,256,256]{2,1,0:T(8,128)(2,1)S(1)}, bf16[2,256,256]{2,1,0:T(8,128)(2,1)}, u32[]{:S(2)}) copy-start(bf16[2,256,256]{2,1,0:T(8,128)(2,1)} %constant.58.clone.w4_ref) | copy-start | bytes 786436
  85.6 42.6 %copy-start.8 = (f32[2,32,128]{2,1,0:T(8,128)S(1)}, f32[2,32,128]{2,1,0:T(8,128)}, u32[]{:S(2)}) copy-start(f32[2,32,128]{2,1,0:T(8,128)} %constant.59.clone.tw_ref) | copy-start | bytes 98308
  85.6 42.5 %all-to-all-start.1 = ((f32[256,8,128]{2,1,0:T(8,128)}), f32[256,8,128]{2,1,0:T(8,128)S(1)}, u32[]{:S(2)}, u32[]{:S(2)}) async-start(f32[256,8,128]{2,1,0:T(8,128)} %bitcast.2), calls=%async_computation.1 | async-start | bytes 2097152 | tf_op jit(solution)/shard_map/all_to_all | solution.py:375
  96.9 3.7 %collective-permute-start = (f32[1,32]{1,0:T(1,128)S(1)}, f32[1,32]{1,0:T(1,128)S(1)}, u32[]{:S(2)}, u32[]{:S(2)}) collective-permute-start(f32[1,32]{1,0:T(1,128)S(1)} %copy-done.10), channel_id=1, source_target_pairs={{32,0},{64,32},{96,64},{128,96},{160,128},{192,160},{224,192},{0,2... | collective-permute-start | bytes 392 | tf_op jit(solution)/shard_map/ppermute | solution.py:331
  100.6 4.2 %collective-permute-start.1 = (f32[2,32]{1,0:T(2,128)S(1)}, f32[2,32]{1,0:T(2,128)S(1)}, u32[]{:S(2)}, u32[]{:S(2)}) collective-permute-start(f32[2,32]{1,0:T(2,128)S(1)} %pad_maximum_fusion.3), channel_id=1, source_target_pairs={{64,0},{96,32},{128,64},{160,96},{192,128},{224,160},{0,192},{32,2... | collective-permute-start | bytes 776 | tf_op jit(solution)/shard_map/ppermute | solution.py:331
  104.8 4.3 %collective-permute-start.2 = (f32[4,32]{1,0:T(4,128)S(1)}, f32[4,32]{1,0:T(4,128)S(1)}, u32[]{:S(2)}, u32[]{:S(2)}) collective-permute-start(f32[4,32]{1,0:T(4,128)S(1)} %pad_maximum_fusion.2), channel_id=1, source_target_pairs={{128,0},{160,32},{192,64},{224,96},{0,128},{32,160},{64,192},{96,2... | collective-permute-start | bytes 1544 | tf_op jit(solution)/shard_map/ppermute | solution.py:331

commit v6 on v5

--- a/solution.py
+++ b/solution.py
@@ -57,7 +57,7 @@
 
 
 def pack_call(forward, cotangent):
-    steps = 4
+    steps = 2
     spec = pl.BlockSpec((1, 2, 32, TIME // steps), lambda i: (0, 0, 0, i))
     return pl.pallas_call(
         pack_kernel,
@@ -104,7 +104,7 @@
         fs[f] = dot(place_ref[...], xs[f]).astype(BF)
         return carry
 
-    lax.fori_loop(0, 4, place, 0)
+    lax.fori_loop(0, 4, place, 0, unroll=2)
 
     def first(k, carry):
         for pair in range(2):
@@ -173,7 +173,7 @@
         return carry
 
     grid(0, 0, 0)
-    lax.fori_loop(0, GRID // 4, columns, 0, unroll=2)
+    lax.fori_loop(0, GRID // 4, columns, 0, unroll=4)
 
     def last(g, carry):
         head, tail = rs[0, g], rs[1, g]
@@ -205,7 +205,7 @@
         return carry
 
     loads[1].wait()
-    lax.fori_loop(0, 4, finish, 0)
+    lax.fori_loop(0, 4, finish, 0, unroll=2)
     for j in range(4):
         store(j).wait()
 

time: 152 us -> 149 us (0.980)
  Pallas kernels: 28.3 us -> 25.3 us
    pallas_call x1, Pallas kernels: 21.1 us -> 19.3 us  [kerr_call(): pl.pallas_call(kerr_kernel, name='kerr', out_shape=jax.ShapeDtypeStruct((...]
where the time goes in v6:
time: 149 us; the launch traced here: 148 us
  waiting for transfers between devices  65.7 us (44%)
  starting transfers between devices  30.8 us (21%)
  Pallas kernels  25.3 us (17%)
  blocking collectives  18.4 us (12%)
  other arithmetic  5.12 us (3%)
  local copies, waits for them, and re-layouts  2.82 us (2%)
    all_to_all x1, waiting for transfers between devices, on_device(): lax.all_to_all(send, 'ma', split_axis=0, concat_axis=0, tiled=True)  44 us
    pallas_call x1, Pallas kernels, kerr_call(): pl.pallas_call(kerr_kernel, name='kerr', out_shape=jax.ShapeDtypeStruct((...  19.3 us
    all_to_all x1, waiting for transfers between devices, on_device(): lax.all_to_all(source, ('gz', 'ma'), split_axis=0, concat_axis=0, tiled=T...  18.8 us
    all_to_all x1, blocking collectives, on_device(): lax.all_to_all(result, 'gz', split_axis=0, concat_axis=0, tiled=True)  18.4 us
    all_to_all x1, starting transfers between devices, on_device(): lax.all_to_all(send, 'ma', split_axis=0, concat_axis=0, tiled=True)  12.2 us
    all_to_all x1, starting transfers between devices, on_device(): lax.all_to_all(source, ('gz', 'ma'), split_axis=0, concat_axis=0, tiled=T...  11.3 us
    ppermute x3, starting transfers between devices, gathered_loss(): have = jnp.concatenate([have, lax.ppermute(have, 'gz', route)], axis=0)  7.42 us
    pallas_call x1, Pallas kernels, spectral_call(): pl.pallas_call(spectral_kernel, name='spectral', out_shape=jax.ShapeDtype...  3.39 us
  transfers between devices with their start and end apart: 5, of which 4 were waited for; matrix products, arithmetic and copies ran while one was open for 4% of the time, Pallas kernels for 0%

profile of v6, /device:TPU:1, one launch (start us, length us, event | category | flops | bytes accessed | tf_op | source)
XLA Modules:
  0.0 148.4 jit_solution(8483782966153762725)
XLA Ops:
  0.0 2.6 %pack.1 = f32[32,4,32,128]{3,2,1,0:T(8,128)} custom-call(f32[1,2,32,4096]{3,2,1,0:T(8,128)} %f_ref.1, f32[1,2,32,4096]{3,2,1,0:T(8,128)} %c_ref.1), custom_call_target="tpu_custom_call" | custom-call | flops 1048576 | bytes 4194304 | tf_op jit(solution)/shard_map/pack/pallas_call | solution.py:62
  2.6 12.2 %all-to-all-start = ((f32[32,4,32,128]{3,2,1,0:T(8,128)}), f32[32,4,32,128]{3,2,1,0:T(8,128)S(1)}, u32[]{:S(2)}, u32[]{:S(2)}) async-start(f32[32,4,32,128]{3,2,1,0:T(8,128)} %pack.1), calls=%async_computation | async-start | bytes 4194304 | tf_op jit(solution)/shard_map/all_to_all | solution.py:371
  14.8 1.1 select_reduce_fusion
  15.9 0.7 copy.23
  16.6 0.8 multiply_bitcast_fusion.k_ref
  17.5 1.7 %fusion.back_hbm = bf16[1024,1024]{1,0:T(8,128)(2,1)} fusion(s32[1024]{0:T(1024)S(1)} %copy-done), kind=kLoop, calls=%fused_computation.1 | loop fusion | flops 2097152 | bytes 2101248 | tf_op jit(solution)/shard_map/convert_element_type | solution.py:364
  19.2 44.0 %all-to-all-done.x_ref = f32[32,4,32,128]{3,2,1,0:T(8,128)S(1)} async-done(((f32[32,4,32,128]{3,2,1,0:T(8,128)}), f32[32,4,32,128]{3,2,1,0:T(8,128)S(1)}, u32[]{:S(2)}, u32[]{:S(2)}) %all-to-all-start) | async-done | bytes 2097184 | tf_op jit(solution)/shard_map/all_to_all | solution.py:371
  63.3 19.3 %kerr.1 = f32[8,32,8,128]{3,2,1,0:T(8,128)} custom-call(f32[32,4,32,128]{3,2,1,0:T(8,128)S(1)} %all-to-all-done.x_ref, s32[1,1024]{1,0:T(1,128)S(1)} %bitcast.15, bf16[1024,1024]{1,0:T(8,128)(2,1)} %fusion.back_hbm, bf16[256,192]{1,0:T(8,128)(2,1)S(1)} %copy-done.6, bf16[256,192]{1,0:T(8,128)(2,1)S(1)} %copy-done.7, bf16[2,256,1024]{2,1,0:T(8,128)(2,1)S(1)} %copy-done.1, ...), custom_call_target="tpu_custom_call" | custom-call | flops 20000000000 | bytes 8388608 | tf_op jit(solution)/shard_map/kerr/pallas_call | solution.py:216
  82.6 11.3 %all-to-all-start.1 = ((f32[256,8,128]{2,1,0:T(8,128)}), f32[256,8,128]{2,1,0:T(8,128)S(1)}, u32[]{:S(2)}, u32[]{:S(2)}) async-start(f32[256,8,128]{2,1,0:T(8,128)} %bitcast.2), calls=%async_computation.1 | async-start | bytes 2097152 | tf_op jit(solution)/shard_map/all_to_all | solution.py:375
  93.9 2.2 %collective-permute-start = (f32[1,32]{1,0:T(1,128)S(1)}, f32[1,32]{1,0:T(1,128)S(1)}, u32[]{:S(2)}, u32[]{:S(2)}) collective-permute-start(f32[1,32]{1,0:T(1,128)S(1)} %copy-done.10), channel_id=1, source_target_pairs={{32,0},{64,32},{96,64},{128,96},{160,128},{192,160},{224,192},{0,2... | collective-permute-start | bytes 392 | tf_op jit(solution)/shard_map/ppermute | solution.py:331
  96.1 1.4 dynamic-slice_cosine_fusion
  97.4 0.1 neg.20
  97.6 3.5 %collective-permute-start.1 = (f32[2,32]{1,0:T(2,128)S(1)}, f32[2,32]{1,0:T(2,128)S(1)}, u32[]{:S(2)}, u32[]{:S(2)}) collective-permute-start(f32[2,32]{1,0:T(2,128)S(1)} %pad_maximum_fusion.3), channel_id=1, source_target_pairs={{64,0},{96,32},{128,64},{160,96},{192,128},{224,160},{0,192},{32,2... | collective-permute-start | bytes 776 | tf_op jit(solution)/shard_map/ppermute | solution.py:331
  101.1 0.1 copy.25
  101.2 0.1 cos.20
  101.3 0.1 copy.24
  101.4 0.4 collective-permute-done.1
  101.8 1.8 %collective-permute-start.2 = (f32[4,32]{1,0:T(4,128)S(1)}, f32[4,32]{1,0:T(4,128)S(1)}, u32[]{:S(2)}, u32[]{:S(2)}) collective-permute-start(f32[4,32]{1,0:T(4,128)S(1)} %pad_maximum_fusion.2), channel_id=1, source_target_pairs={{128,0},{160,32},{192,64},{224,96},{0,128},{32,160},{64,192},{96,2... | collective-permute-start | bytes 1544 | tf_op jit(solution)/shard_map/ppermute | solution.py:331
  103.6 2.5 %collective-permute-done.2 = f32[4,32]{1,0:T(4,128)S(1)} collective-permute-done((f32[4,32]{1,0:T(4,128)S(1)}, f32[4,32]{1,0:T(4,128)S(1)}, u32[]{:S(2)}, u32[]{:S(2)}) %collective-permute-start.2) | collective-permute-done | bytes 544 | tf_op jit(solution)/shard_map/ppermute | solution.py:331
  106.3 18.8 %all-to-all-done.1 = f32[256,8,128]{2,1,0:T(8,128)S(1)} async-done(((f32[256,8,128]{2,1,0:T(8,128)}), f32[256,8,128]{2,1,0:T(8,128)S(1)}, u32[]{:S(2)}, u32[]{:S(2)}) %all-to-all-start.1) | async-done | bytes 1048608 | tf_op jit(solution)/shard_map/all_to_all | solution.py:375
  125.2 3.4 %spectral.1 = f32[8,256,128]{2,1,0:T(8,128)S(1)} custom-call(f32[8,32,8,128]{3,2,1,0:T(8,128)S(1)} %bitcast.14, f32[8,1,8,128]{3,2,1,0:T(8,128)S(1)} %broadcast_in_dim.5.l_ref, f32[2,128,128]{2,1,0:T(8,128)S(1)} %pad_maximum_fusion.ph_ref, bf16[2,256,256]{2,1,0:T(8,128)(2,1)S(1)} %copy-done.2, bf16[2,256,256]{2,1,0:T(8,128)(2,1)S(1)} %copy-done.3, ...), custom_call_target="tpu_custom_call" | custom-call | flops 3000000000 | bytes 4194304 | tf_op jit(solution)/shard_map/spectral/pallas_call | solution.py:313
  128.6 18.4 %all_to_all.15 = f32[8,256,128]{2,1,0:T(8,128)S(1)} all-to-all(f32[8,256,128]{2,1,0:T(8,128)S(1)} %spectral.1), channel_id=1, replica_groups=mesh['gz'=8,'ma'=32] {'gz'}, dimensions={0} | all-to-all | bytes 2097152 | tf_op jit(solution)/shard_map/all_to_all | solution.py:383
  147.0 0.2 copy.26
  147.2 1.2 reshape.52
  (32 shorter events, 0.4 us)
Async XLA Ops:
  2.6 12.2 %copy-start.11 = (f32[8]{0:T(128)S(1)}, f32[8]{0:T(128)}, u32[]{:S(2)}) copy-start(f32[8]{0:T(128)} %param.20) | copy-start | bytes 100
  2.6 14.9 %copy-start = (s32[1024]{0:T(1024)S(1)}, s32[1024]{0:T(1024)}, u32[]{:S(2)}) copy-start(s32[1024]{0:T(1024)} %param.18) | copy-start | bytes 12292
  2.6 60.6 %all-to-all-start = ((f32[32,4,32,128]{3,2,1,0:T(8,128)}), f32[32,4,32,128]{3,2,1,0:T(8,128)S(1)}, u32[]{:S(2)}, u32[]{:S(2)}) async-start(f32[32,4,32,128]{3,2,1,0:T(8,128)} %pack.1), calls=%async_computation | async-start | bytes 4194304 | tf_op jit(solution)/shard_map/all_to_all | solution.py:371
  14.8 48.5 %copy-start.1 = (bf16[2,256,1024]{2,1,0:T(8,128)(2,1)S(1)}, bf16[2,256,1024]{2,1,0:T(8,128)(2,1)}, u32[]{:S(2)}) copy-start(bf16[2,256,1024]{2,1,0:T(8,128)(2,1)} %constant.53.clone.proj_hbm) | copy-start | bytes 3145732
  14.8 48.5 %copy-start.6 = (bf16[256,192]{1,0:T(8,128)(2,1)S(1)}, bf16[256,192]{1,0:T(8,128)(2,1)}, u32[]{:S(2)}) copy-start(bf16[256,192]{1,0:T(8,128)(2,1)} %constant.51.clone.f2_ref) | copy-start | bytes 294916
  14.8 48.4 %copy-start.7 = (bf16[256,192]{1,0:T(8,128)(2,1)S(1)}, bf16[256,192]{1,0:T(8,128)(2,1)}, u32[]{:S(2)}) copy-start(bf16[256,192]{1,0:T(8,128)(2,1)} %constant.52.clone.f3_ref) | copy-start | bytes 294916
  14.8 48.4 %copy-start.9 = (f32[32,128]{1,0:T(8,128)S(1)}, f32[32,128]{1,0:T(8,128)}, u32[]{:S(2)}) copy-start(f32[32,128]{1,0:T(8,128)} %constant.54.clone.tt_ref) | copy-start | bytes 49156
  82.5 11.3 %copy-start.10 = (f32[1,32]{1,0:T(1,128)S(1)}, f32[1,32]{1,0:T(1,128)}, u32[]{:S(2)}) copy-start(f32[1,32]{1,0:T(1,128)} %param.22) | copy-start | bytes 388
  82.6 42.6 %copy-start.2 = (bf16[2,256,256]{2,1,0:T(8,128)(2,1)S(1)}, bf16[2,256,256]{2,1,0:T(8,128)(2,1)}, u32[]{:S(2)}) copy-start(bf16[2,256,256]{2,1,0:T(8,128)(2,1)} %constant.55.clone.w1_ref) | copy-start | bytes 786436
  82.6 42.6 %copy-start.3 = (bf16[2,256,256]{2,1,0:T(8,128)(2,1)S(1)}, bf16[2,256,256]{2,1,0:T(8,128)(2,1)}, u32[]{:S(2)}) copy-start(bf16[2,256,256]{2,1,0:T(8,128)(2,1)} %constant.56.clone.w2_ref) | copy-start | bytes 786436
  82.6 42.6 %copy-start.4 = (bf16[2,256,256]{2,1,0:T(8,128)(2,1)S(1)}, bf16[2,256,256]{2,1,0:T(8,128)(2,1)}, u32[]{:S(2)}) copy-start(bf16[2,256,256]{2,1,0:T(8,128)(2,1)} %constant.57.clone.w3_ref) | copy-start | bytes 786436
  82.6 42.6 %copy-start.5 = (bf16[2,256,256]{2,1,0:T(8,128)(2,1)S(1)}, bf16[2,256,256]{2,1,0:T(8,128)(2,1)}, u32[]{:S(2)}) copy-start(bf16[2,256,256]{2,1,0:T(8,128)(2,1)} %constant.58.clone.w4_ref) | copy-start | bytes 786436
  82.6 42.6 %copy-start.8 = (f32[2,32,128]{2,1,0:T(8,128)S(1)}, f32[2,32,128]{2,1,0:T(8,128)}, u32[]{:S(2)}) copy-start(f32[2,32,128]{2,1,0:T(8,128)} %constant.59.clone.tw_ref) | copy-start | bytes 98308
  82.6 42.5 %all-to-all-start.1 = ((f32[256,8,128]{2,1,0:T(8,128)}), f32[256,8,128]{2,1,0:T(8,128)S(1)}, u32[]{:S(2)}, u32[]{:S(2)}) async-start(f32[256,8,128]{2,1,0:T(8,128)} %bitcast.2), calls=%async_computation.1 | async-start | bytes 2097152 | tf_op jit(solution)/shard_map/all_to_all | solution.py:375
  93.9 3.7 %collective-permute-start = (f32[1,32]{1,0:T(1,128)S(1)}, f32[1,32]{1,0:T(1,128)S(1)}, u32[]{:S(2)}, u32[]{:S(2)}) collective-permute-start(f32[1,32]{1,0:T(1,128)S(1)} %copy-done.10), channel_id=1, source_target_pairs={{32,0},{64,32},{96,64},{128,96},{160,128},{192,160},{224,192},{0,2... | collective-permute-start | bytes 392 | tf_op jit(solution)/shard_map/ppermute | solution.py:331
  97.6 4.2 %collective-permute-start.1 = (f32[2,32]{1,0:T(2,128)S(1)}, f32[2,32]{1,0:T(2,128)S(1)}, u32[]{:S(2)}, u32[]{:S(2)}) collective-permute-start(f32[2,32]{1,0:T(2,128)S(1)} %pad_maximum_fusion.3), channel_id=1, source_target_pairs={{64,0},{96,32},{128,64},{160,96},{192,128},{224,160},{0,192},{32,2... | collective-permute-start | bytes 776 | tf_op jit(solution)/shard_map/ppermute | solution.py:331
  101.8 4.3 %collective-permute-start.2 = (f32[4,32]{1,0:T(4,128)S(1)}, f32[4,32]{1,0:T(4,128)S(1)}, u32[]{:S(2)}, u32[]{:S(2)}) collective-permute-start(f32[4,32]{1,0:T(4,128)S(1)} %pad_maximum_fusion.2), channel_id=1, source_target_pairs={{128,0},{160,32},{192,64},{224,96},{0,128},{32,160},{64,192},{96,2... | collective-permute-start | bytes 1544 | tf_op jit(solution)/shard_map/ppermute | solution.py:331

commit v7 on v6

--- a/solution.py
+++ b/solution.py
@@ -16,7 +16,7 @@
 BLOCK = 128
 OUTER = 32
 ZL = 8
-LIMIT = 48 * 2**20
+LIMIT = 50 * 2**20
 PER = 4
 BF = jnp.bfloat16
 F32 = jnp.float32
@@ -158,12 +158,11 @@
             )
             got = dot(left, right)
             res.append(got[:32] + got[32:])
-        rows = pl.ds(pl.multiple_of(u * 16, 16), 16)
-        for g in range(4):
-            both = jnp.concatenate([res[i][g * 8:(g + 1) * 8] for i in range(2)], axis=0)
-            head, tail = split(both)
-            rs[0, g, rows, :] = head
-            rs[1, g, rows, :] = tail
+        rows = pl.ds(pl.multiple_of(u * 8, 8), 8)
+        for g in range(8):
+            rs[g, rows, :] = jnp.concatenate(
+                [res[i][g * 4:(g + 1) * 4] for i in range(2)], axis=0
+            )
 
     def columns(v, carry):
         grid(v, 1, 1)
@@ -173,12 +172,12 @@
         return carry
 
     grid(0, 0, 0)
-    lax.fori_loop(0, GRID // 4, columns, 0, unroll=4)
+    lax.fori_loop(0, GRID // 4, columns, 0, unroll=8)
 
     def last(g, carry):
-        head, tail = rs[0, g], rs[1, g]
+        head, tail = split(rs[g])
         res = dot(proj_ref[0], head) + (dot(proj_ref[0], tail) + dot(proj_ref[1], head))
-        rows = pl.ds(pl.multiple_of(g * 256, 256), 256)
+        rows = pl.ds(pl.multiple_of(g * 128, 128), 128)
         for c in range(2):
             head, tail = split(res[:, c * 128:(c + 1) * 128])
             ks[c, rows, 0:128] = head
@@ -186,7 +185,7 @@
         return carry
 
     loads[0].wait()
-    lax.fori_loop(0, 4, last, 0, unroll=2)
+    lax.fori_loop(0, 8, last, 0, unroll=4)
 
     def store(j):
         part = pl.ds(j * 8, 8)
@@ -223,12 +222,12 @@
             pltpu.VMEM((4, MODES, 256), BF),
             pltpu.VMEM((4, MODES, 256), BF),
             pltpu.VMEM((4, 32, 2, 8, 8, 128), F32),
-            pltpu.VMEM((2, 4, MODES, 256), BF),
+            pltpu.VMEM((8, MODES // 2, 256), F32),
             pltpu.VMEM((2, MODES, 256), BF),
             pltpu.VMEM((2, 2, 256, 256), F32),
             pltpu.VMEM((MODES, MODES), BF),
             pltpu.VMEM((MODES, MODES), BF),
-            pltpu.VMEM((2, 256, MODES), BF),
+            pltpu.VMEM((2, 128, MODES // 2), BF),
             pltpu.VMEM((ZL, 32, 8, 128), F32),
             pltpu.SemaphoreType.DMA((2,)),
             pltpu.SemaphoreType.DMA((4,)),
@@ -350,7 +349,7 @@
         return np.einsum("xkhp,ab->axkhbp", table.reshape(128, 8, 2, 2), eye).reshape(256, 64)
 
     def sum_y(table):
-        return np.einsum("yq,ab->aqyb", table, np.eye(8)).reshape(256, 1024)
+        return np.einsum("yq,ab->aqyb", table, np.eye(4)).reshape(128, 512)
 
     proj = np.stack([sum_y(t_h), sum_y(t_l)]).astype(jnp.bfloat16)
     return stacked(sum_q), stacked(sum_p), proj, np.ascontiguousarray(t.T).astype(np.float32)

time: 149 us -> 147 us (0.987)
  waiting for transfers between devices: 65.7 us -> 68.1 us
  other arithmetic: 5.12 us -> 3.34 us
    all_to_all x1, waiting for transfers between devices: 44 us -> 46.4 us  [on_device(): lax.all_to_all(send, 'ma', split_axis=0, concat_axis=0, tiled=True)]
  transfers between devices with their start and end apart: 5 -> 5, of which waited for: 4 -> 4; matrix products, arithmetic and copies ran while one was open for 4% -> 3% of each run, Pallas kernels for 0% -> 0%
where the time goes in v7:
time: 147 us
  waiting for transfers between devices  68.1 us (46%)
  starting transfers between devices  30.8 us (21%)
  Pallas kernels  23.9 us (16%)
  blocking collectives  18.4 us (13%)
  other arithmetic  3.34 us (2%)
  local copies, waits for them, and re-layouts  2.18 us (1%)
    all_to_all x1, waiting for transfers between devices, on_device(): lax.all_to_all(send, 'ma', split_axis=0, concat_axis=0, tiled=True)  46.4 us
    all_to_all x1, waiting for transfers between devices, on_device(): lax.all_to_all(source, ('gz', 'ma'), split_axis=0, concat_axis=0, tiled=T...  18.8 us
    all_to_all x1, blocking collectives, on_device(): lax.all_to_all(result, 'gz', split_axis=0, concat_axis=0, tiled=True)  18.4 us
    pallas_call x1, Pallas kernels, kerr_call(): pl.pallas_call(kerr_kernel, name='kerr', out_shape=jax.ShapeDtypeStruct((...  17.9 us
    all_to_all x1, starting transfers between devices, on_device(): lax.all_to_all(send, 'ma', split_axis=0, concat_axis=0, tiled=True)  12.2 us
    all_to_all x1, starting transfers between devices, on_device(): lax.all_to_all(source, ('gz', 'ma'), split_axis=0, concat_axis=0, tiled=T...  11.3 us
    ppermute x3, starting transfers between devices, gathered_loss(): have = jnp.concatenate([have, lax.ppermute(have, 'gz', route)], axis=0)  7.42 us
    pallas_call x1, Pallas kernels, spectral_call(): pl.pallas_call(spectral_kernel, name='spectral', out_shape=jax.ShapeDtype...  3.4 us
  transfers between devices with their start and end apart: 5, of which 4 were waited for; matrix products, arithmetic and copies ran while one was open for 3% of the time, Pallas kernels for 0%

profile of v7, /device:TPU:1, one launch (start us, length us, event | category | flops | bytes accessed | tf_op | source)
XLA Modules:
  0.0 147.1 jit_solution(3543130664090100680)
XLA Ops:
  0.0 2.6 %pack.1 = f32[32,4,32,128]{3,2,1,0:T(8,128)} custom-call(f32[1,2,32,4096]{3,2,1,0:T(8,128)} %f_ref.1, f32[1,2,32,4096]{3,2,1,0:T(8,128)} %c_ref.1), custom_call_target="tpu_custom_call" | custom-call | flops 1048576 | bytes 4194304 | tf_op jit(solution)/shard_map/pack/pallas_call | solution.py:62
  2.6 12.2 %all-to-all-start = ((f32[32,4,32,128]{3,2,1,0:T(8,128)}), f32[32,4,32,128]{3,2,1,0:T(8,128)S(1)}, u32[]{:S(2)}, u32[]{:S(2)}) async-start(f32[32,4,32,128]{3,2,1,0:T(8,128)} %pack.1), calls=%async_computation | async-start | bytes 4194304 | tf_op jit(solution)/shard_map/all_to_all | solution.py:370
  14.9 0.1 select_reduce_fusion
  15.0 0.1 copy.23
  15.1 1.7 %fusion.back_hbm = bf16[1024,1024]{1,0:T(8,128)(2,1)} fusion(s32[1024]{0:T(1024)S(1)} %copy-done), kind=kLoop, calls=%fused_computation.1 | loop fusion | flops 2097152 | bytes 2101248 | tf_op jit(solution)/shard_map/convert_element_type | solution.py:363
  16.8 46.4 %all-to-all-done.x_ref = f32[32,4,32,128]{3,2,1,0:T(8,128)S(1)} async-done(((f32[32,4,32,128]{3,2,1,0:T(8,128)}), f32[32,4,32,128]{3,2,1,0:T(8,128)S(1)}, u32[]{:S(2)}, u32[]{:S(2)}) %all-to-all-start) | async-done | bytes 2097184 | tf_op jit(solution)/shard_map/all_to_all | solution.py:370
  63.3 17.9 %kerr.1 = f32[8,32,8,128]{3,2,1,0:T(8,128)} custom-call(f32[32,4,32,128]{3,2,1,0:T(8,128)S(1)} %all-to-all-done.x_ref, s32[1,1024]{1,0:T(1,128)S(1)} %bitcast.15, bf16[1024,1024]{1,0:T(8,128)(2,1)} %fusion.back_hbm, bf16[256,192]{1,0:T(8,128)(2,1)S(1)} %copy-done.6, bf16[256,192]{1,0:T(8,128)(2,1)S(1)} %copy-done.7, bf16[2,128,512]{2,1,0:T(8,128)(2,1)S(1)} %copy-done.5, ...), custom_call_target="tpu_custom_call" | custom-call | flops 20000000000 | bytes 8388608 | tf_op jit(solution)/shard_map/kerr/pallas_call | solution.py:215
  81.3 11.3 %all-to-all-start.1 = ((f32[256,8,128]{2,1,0:T(8,128)}), f32[256,8,128]{2,1,0:T(8,128)S(1)}, u32[]{:S(2)}, u32[]{:S(2)}) async-start(f32[256,8,128]{2,1,0:T(8,128)} %bitcast.2), calls=%async_computation.1 | async-start | bytes 2097152 | tf_op jit(solution)/shard_map/all_to_all | solution.py:374
  92.6 2.2 %collective-permute-start = (f32[1,32]{1,0:T(1,128)S(1)}, f32[1,32]{1,0:T(1,128)S(1)}, u32[]{:S(2)}, u32[]{:S(2)}) collective-permute-start(f32[1,32]{1,0:T(1,128)S(1)} %copy-done.11), channel_id=1, source_target_pairs={{32,0},{64,32},{96,64},{128,96},{160,128},{192,160},{224,192},{0,2... | collective-permute-start | bytes 392 | tf_op jit(solution)/shard_map/ppermute | solution.py:330
  94.7 1.4 dynamic-slice_cosine_fusion
  96.1 0.1 neg.20
  96.3 3.5 %collective-permute-start.1 = (f32[2,32]{1,0:T(2,128)S(1)}, f32[2,32]{1,0:T(2,128)S(1)}, u32[]{:S(2)}, u32[]{:S(2)}) collective-permute-start(f32[2,32]{1,0:T(2,128)S(1)} %pad_maximum_fusion.3), channel_id=1, source_target_pairs={{64,0},{96,32},{128,64},{160,96},{192,128},{224,160},{0,192},{32,2... | collective-permute-start | bytes 776 | tf_op jit(solution)/shard_map/ppermute | solution.py:330
  99.7 0.1 copy.25
  99.8 0.1 cos.20
  100.0 0.1 copy.24
  100.1 0.4 collective-permute-done.1
  100.5 1.8 %collective-permute-start.2 = (f32[4,32]{1,0:T(4,128)S(1)}, f32[4,32]{1,0:T(4,128)S(1)}, u32[]{:S(2)}, u32[]{:S(2)}) collective-permute-start(f32[4,32]{1,0:T(4,128)S(1)} %pad_maximum_fusion.2), channel_id=1, source_target_pairs={{128,0},{160,32},{192,64},{224,96},{0,128},{32,160},{64,192},{96,2... | collective-permute-start | bytes 1544 | tf_op jit(solution)/shard_map/ppermute | solution.py:330
  102.3 2.5 %collective-permute-done.2 = f32[4,32]{1,0:T(4,128)S(1)} collective-permute-done((f32[4,32]{1,0:T(4,128)S(1)}, f32[4,32]{1,0:T(4,128)S(1)}, u32[]{:S(2)}, u32[]{:S(2)}) %collective-permute-start.2) | collective-permute-done | bytes 544 | tf_op jit(solution)/shard_map/ppermute | solution.py:330
  104.9 0.1 pad_maximum_fusion.1
  105.0 18.8 %all-to-all-done.1 = f32[256,8,128]{2,1,0:T(8,128)S(1)} async-done(((f32[256,8,128]{2,1,0:T(8,128)}), f32[256,8,128]{2,1,0:T(8,128)S(1)}, u32[]{:S(2)}, u32[]{:S(2)}) %all-to-all-start.1) | async-done | bytes 1048608 | tf_op jit(solution)/shard_map/all_to_all | solution.py:374
  123.9 3.4 %spectral.1 = f32[8,256,128]{2,1,0:T(8,128)S(1)} custom-call(f32[8,32,8,128]{3,2,1,0:T(8,128)S(1)} %bitcast.14, f32[8,1,8,128]{3,2,1,0:T(8,128)S(1)} %broadcast_in_dim.5.l_ref, f32[2,128,128]{2,1,0:T(8,128)S(1)} %pad_maximum_fusion.ph_ref, bf16[2,256,256]{2,1,0:T(8,128)(2,1)S(1)} %copy-done.1, bf16[2,256,256]{2,1,0:T(8,128)(2,1)S(1)} %copy-done.2, ...), custom_call_target="tpu_custom_call" | custom-call | flops 3000000000 | bytes 4194304 | tf_op jit(solution)/shard_map/spectral/pallas_call | solution.py:312
  127.3 18.4 %all_to_all.15 = f32[8,256,128]{2,1,0:T(8,128)S(1)} all-to-all(f32[8,256,128]{2,1,0:T(8,128)S(1)} %spectral.1), channel_id=1, replica_groups=mesh['gz'=8,'ma'=32] {'gz'}, dimensions={0} | all-to-all | bytes 2097152 | tf_op jit(solution)/shard_map/all_to_all | solution.py:382
  145.7 0.2 copy.26
  145.9 1.2 reshape.52
  (34 shorter events, 0.3 us)
Async XLA Ops:
  2.6 12.2 %copy-start.10 = (s32[128,128]{1,0:T(8,128)S(1)}, s32[128,128]{1,0:T(8,128)}, u32[]{:S(2)}) copy-start(s32[128,128]{1,0:T(8,128)} %param.19) | copy-start | bytes 196612
  2.6 12.2 %copy-start.12 = (f32[8]{0:T(128)S(1)}, f32[8]{0:T(128)}, u32[]{:S(2)}) copy-start(f32[8]{0:T(128)} %param.20) | copy-start | bytes 100
  2.6 12.5 %copy-start = (s32[1024]{0:T(1024)S(1)}, s32[1024]{0:T(1024)}, u32[]{:S(2)}) copy-start(s32[1024]{0:T(1024)} %param.18) | copy-start | bytes 12292
  2.6 60.6 %all-to-all-start = ((f32[32,4,32,128]{3,2,1,0:T(8,128)}), f32[32,4,32,128]{3,2,1,0:T(8,128)S(1)}, u32[]{:S(2)}, u32[]{:S(2)}) async-start(f32[32,4,32,128]{3,2,1,0:T(8,128)} %pack.1), calls=%async_computation | async-start | bytes 4194304 | tf_op jit(solution)/shard_map/all_to_all | solution.py:370
  14.8 48.5 %copy-start.5 = (bf16[2,128,512]{2,1,0:T(8,128)(2,1)S(1)}, bf16[2,128,512]{2,1,0:T(8,128)(2,1)}, u32[]{:S(2)}) copy-start(bf16[2,128,512]{2,1,0:T(8,128)(2,1)} %constant.53.clone.proj_hbm) | copy-start | bytes 786436
  14.8 48.4 %copy-start.6 = (bf16[256,192]{1,0:T(8,128)(2,1)S(1)}, bf16[256,192]{1,0:T(8,128)(2,1)}, u32[]{:S(2)}) copy-start(bf16[256,192]{1,0:T(8,128)(2,1)} %constant.51.clone.f2_ref) | copy-start | bytes 294916
  14.8 48.4 %copy-start.7 = (bf16[256,192]{1,0:T(8,128)(2,1)S(1)}, bf16[256,192]{1,0:T(8,128)(2,1)}, u32[]{:S(2)}) copy-start(bf16[256,192]{1,0:T(8,128)(2,1)} %constant.52.clone.f3_ref) | copy-start | bytes 294916
  14.9 48.4 %copy-start.9 = (f32[32,128]{1,0:T(8,128)S(1)}, f32[32,128]{1,0:T(8,128)}, u32[]{:S(2)}) copy-start(f32[32,128]{1,0:T(8,128)} %constant.54.clone.tt_ref) | copy-start | bytes 49156
  81.2 11.3 %copy-start.11 = (f32[1,32]{1,0:T(1,128)S(1)}, f32[1,32]{1,0:T(1,128)}, u32[]{:S(2)}) copy-start(f32[1,32]{1,0:T(1,128)} %param.22) | copy-start | bytes 388
  81.2 42.6 %copy-start.1 = (bf16[2,256,256]{2,1,0:T(8,128)(2,1)S(1)}, bf16[2,256,256]{2,1,0:T(8,128)(2,1)}, u32[]{:S(2)}) copy-start(bf16[2,256,256]{2,1,0:T(8,128)(2,1)} %constant.55.clone.w1_ref) | copy-start | bytes 786436
  81.2 42.6 %copy-start.2 = (bf16[2,256,256]{2,1,0:T(8,128)(2,1)S(1)}, bf16[2,256,256]{2,1,0:T(8,128)(2,1)}, u32[]{:S(2)}) copy-start(bf16[2,256,256]{2,1,0:T(8,128)(2,1)} %constant.56.clone.w2_ref) | copy-start | bytes 786436
  81.3 42.6 %copy-start.3 = (bf16[2,256,256]{2,1,0:T(8,128)(2,1)S(1)}, bf16[2,256,256]{2,1,0:T(8,128)(2,1)}, u32[]{:S(2)}) copy-start(bf16[2,256,256]{2,1,0:T(8,128)(2,1)} %constant.57.clone.w3_ref) | copy-start | bytes 786436
  81.3 42.6 %copy-start.4 = (bf16[2,256,256]{2,1,0:T(8,128)(2,1)S(1)}, bf16[2,256,256]{2,1,0:T(8,128)(2,1)}, u32[]{:S(2)}) copy-start(bf16[2,256,256]{2,1,0:T(8,128)(2,1)} %constant.58.clone.w4_ref) | copy-start | bytes 786436
  81.3 42.6 %copy-start.8 = (f32[2,32,128]{2,1,0:T(8,128)S(1)}, f32[2,32,128]{2,1,0:T(8,128)}, u32[]{:S(2)}) copy-start(f32[2,32,128]{2,1,0:T(8,128)} %constant.59.clone.tw_ref) | copy-start | bytes 98308
  81.3 42.5 %all-to-all-start.1 = ((f32[256,8,128]{2,1,0:T(8,128)}), f32[256,8,128]{2,1,0:T(8,128)S(1)}, u32[]{:S(2)}, u32[]{:S(2)}) async-start(f32[256,8,128]{2,1,0:T(8,128)} %bitcast.2), calls=%async_computation.1 | async-start | bytes 2097152 | tf_op jit(solution)/shard_map/all_to_all | solution.py:374
  92.6 3.7 %collective-permute-start = (f32[1,32]{1,0:T(1,128)S(1)}, f32[1,32]{1,0:T(1,128)S(1)}, u32[]{:S(2)}, u32[]{:S(2)}) collective-permute-start(f32[1,32]{1,0:T(1,128)S(1)} %copy-done.11), channel_id=1, source_target_pairs={{32,0},{64,32},{96,64},{128,96},{160,128},{192,160},{224,192},{0,2... | collective-permute-start | bytes 392 | tf_op jit(solution)/shard_map/ppermute | solution.py:330
  96.3 4.2 %collective-permute-start.1 = (f32[2,32]{1,0:T(2,128)S(1)}, f32[2,32]{1,0:T(2,128)S(1)}, u32[]{:S(2)}, u32[]{:S(2)}) collective-permute-start(f32[2,32]{1,0:T(2,128)S(1)} %pad_maximum_fusion.3), channel_id=1, source_target_pairs={{64,0},{96,32},{128,64},{160,96},{192,128},{224,160},{0,192},{32,2... | collective-permute-start | bytes 776 | tf_op jit(solution)/shard_map/ppermute | solution.py:330
  100.5 4.3 %collective-permute-start.2 = (f32[4,32]{1,0:T(4,128)S(1)}, f32[4,32]{1,0:T(4,128)S(1)}, u32[]{:S(2)}, u32[]{:S(2)}) collective-permute-start(f32[4,32]{1,0:T(4,128)S(1)} %pad_maximum_fusion.2), channel_id=1, source_target_pairs={{128,0},{160,32},{192,64},{224,96},{0,128},{32,160},{64,192},{96,2... | collective-permute-start | bytes 1544 | tf_op jit(solution)/shard_map/ppermute | solution.py:330

commit v8 on v7

--- a/solution.py
+++ b/solution.py
@@ -82,14 +82,6 @@
     for load in loads:
         load.start()
 
-    def one_hot(j, carry):
-        rows = pl.ds(pl.multiple_of(j * 32, 32), 32)
-        index = lax.broadcasted_iota(jnp.int32, (32, MODES), 0) + j * 32
-        place_ref[rows, :] = jnp.where(index == order_ref[...], 1.0, 0.0).astype(BF)
-        return carry
-
-    lax.fori_loop(0, 32, one_hot, 0, unroll=2)
-
     def split_in(j, carry):
         rows = pl.ds(pl.multiple_of(j * 32, 32), 32)
         for f in range(4):
@@ -100,11 +92,15 @@
 
     lax.fori_loop(0, 32, split_in, 0, unroll=4)
 
-    def place(f, carry):
-        fs[f] = dot(place_ref[...], xs[f]).astype(BF)
-        return carry
-
-    lax.fori_loop(0, 4, place, 0, unroll=2)
+    def place(j, carry):
+        rows = pl.ds(pl.multiple_of(j * 256, 256), 256)
+        index = lax.broadcasted_iota(jnp.int32, (256, MODES), 0) + j * 256
+        place_ref[rows, :] = jnp.where(index == order_ref[...], 1.0, 0.0).astype(BF)
+        for f in range(4):
+            fs[f, rows, :] = dot(place_ref[rows, :], xs[f]).astype(BF)
+        return carry
+
+    lax.fori_loop(0, 4, place, 0, unroll=4)
 
     def first(k, carry):
         for pair in range(2):
@@ -124,7 +120,7 @@
                 gs[2 * pair + c, :, 1, k] = high[:, :, lanes]
         return carry
 
-    lax.fori_loop(0, 8, first, 0, unroll=2)
+    lax.fori_loop(0, 8, first, 0, unroll=4)
 
     def grid(v, parity, slot):
         for pair in range(2):

time: 147 us -> 146 us (level)
  no operation moved by 1% of the time
where the time goes in v8:
time: 146 us
  waiting for transfers between devices  67.9 us (47%)
  starting transfers between devices  31 us (21%)
  Pallas kernels  23 us (16%)
  blocking collectives  18.4 us (13%)
  other arithmetic  3.34 us (2%)
  local copies, waits for them, and re-layouts  2.18 us (1%)
    all_to_all x1, waiting for transfers between devices, on_device(): lax.all_to_all(send, 'ma', split_axis=0, concat_axis=0, tiled=True)  46.4 us
    all_to_all x1, waiting for transfers between devices, on_device(): lax.all_to_all(source, ('gz', 'ma'), split_axis=0, concat_axis=0, tiled=T...  18.6 us
    all_to_all x1, blocking collectives, on_device(): lax.all_to_all(result, 'gz', split_axis=0, concat_axis=0, tiled=True)  18.4 us
    pallas_call x1, Pallas kernels, kerr_call(): pl.pallas_call(kerr_kernel, name='kerr', out_shape=jax.ShapeDtypeStruct((...  17 us
    all_to_all x1, starting transfers between devices, on_device(): lax.all_to_all(send, 'ma', split_axis=0, concat_axis=0, tiled=True)  12.2 us
    all_to_all x1, starting transfers between devices, on_device(): lax.all_to_all(source, ('gz', 'ma'), split_axis=0, concat_axis=0, tiled=T...  11.3 us
    ppermute x3, starting transfers between devices, gathered_loss(): have = jnp.concatenate([have, lax.ppermute(have, 'gz', route)], axis=0)  7.6 us
    pallas_call x1, Pallas kernels, spectral_call(): pl.pallas_call(spectral_kernel, name='spectral', out_shape=jax.ShapeDtype...  3.4 us
  transfers between devices with their start and end apart: 5, of which 4 were waited for; matrix products, arithmetic and copies ran while one was open for 3% of the time, Pallas kernels for 0%

profile of v8, /device:TPU:1, one launch (start us, length us, event | category | flops | bytes accessed | tf_op | source)
XLA Modules:
  0.0 146.1 jit_solution(3179865196059767379)
XLA Ops:
  0.0 2.6 %pack.1 = f32[32,4,32,128]{3,2,1,0:T(8,128)} custom-call(f32[1,2,32,4096]{3,2,1,0:T(8,128)} %f_ref.1, f32[1,2,32,4096]{3,2,1,0:T(8,128)} %c_ref.1), custom_call_target="tpu_custom_call" | custom-call | flops 1048576 | bytes 4194304 | tf_op jit(solution)/shard_map/pack/pallas_call | solution.py:62
  2.6 12.2 %all-to-all-start = ((f32[32,4,32,128]{3,2,1,0:T(8,128)}), f32[32,4,32,128]{3,2,1,0:T(8,128)S(1)}, u32[]{:S(2)}, u32[]{:S(2)}) async-start(f32[32,4,32,128]{3,2,1,0:T(8,128)} %pack.1), calls=%async_computation | async-start | bytes 4194304 | tf_op jit(solution)/shard_map/all_to_all | solution.py:366
  14.9 0.1 select_reduce_fusion
  15.0 0.1 copy.23
  15.1 1.7 %fusion.back_hbm = bf16[1024,1024]{1,0:T(8,128)(2,1)} fusion(s32[1024]{0:T(1024)S(1)} %copy-done), kind=kLoop, calls=%fused_computation.1 | loop fusion | flops 2097152 | bytes 2101248 | tf_op jit(solution)/shard_map/convert_element_type | solution.py:359
  16.8 46.4 %all-to-all-done.x_ref = f32[32,4,32,128]{3,2,1,0:T(8,128)S(1)} async-done(((f32[32,4,32,128]{3,2,1,0:T(8,128)}), f32[32,4,32,128]{3,2,1,0:T(8,128)S(1)}, u32[]{:S(2)}, u32[]{:S(2)}) %all-to-all-start) | async-done | bytes 2097184 | tf_op jit(solution)/shard_map/all_to_all | solution.py:366
  63.3 17.0 %kerr.1 = f32[8,32,8,128]{3,2,1,0:T(8,128)} custom-call(f32[32,4,32,128]{3,2,1,0:T(8,128)S(1)} %all-to-all-done.x_ref, s32[1,1024]{1,0:T(1,128)S(1)} %bitcast.15, bf16[1024,1024]{1,0:T(8,128)(2,1)} %fusion.back_hbm, bf16[256,192]{1,0:T(8,128)(2,1)S(1)} %copy-done.6, bf16[256,192]{1,0:T(8,128)(2,1)S(1)} %copy-done.7, bf16[2,128,512]{2,1,0:T(8,128)(2,1)S(1)} %copy-done.5, ...), custom_call_target="tpu_custom_call" | custom-call | flops 20000000000 | bytes 8388608 | tf_op jit(solution)/shard_map/kerr/pallas_call | solution.py:211
  80.3 11.3 %all-to-all-start.1 = ((f32[256,8,128]{2,1,0:T(8,128)}), f32[256,8,128]{2,1,0:T(8,128)S(1)}, u32[]{:S(2)}, u32[]{:S(2)}) async-start(f32[256,8,128]{2,1,0:T(8,128)} %bitcast.2), calls=%async_computation.1 | async-start | bytes 2097152 | tf_op jit(solution)/shard_map/all_to_all | solution.py:370
  91.6 2.2 %collective-permute-start = (f32[1,32]{1,0:T(1,128)S(1)}, f32[1,32]{1,0:T(1,128)S(1)}, u32[]{:S(2)}, u32[]{:S(2)}) collective-permute-start(f32[1,32]{1,0:T(1,128)S(1)} %copy-done.11), channel_id=1, source_target_pairs={{32,0},{64,32},{96,64},{128,96},{160,128},{192,160},{224,192},{0,2... | collective-permute-start | bytes 392 | tf_op jit(solution)/shard_map/ppermute | solution.py:326
  93.8 1.4 dynamic-slice_cosine_fusion
  95.2 0.1 neg.20
  95.3 3.5 %collective-permute-start.1 = (f32[2,32]{1,0:T(2,128)S(1)}, f32[2,32]{1,0:T(2,128)S(1)}, u32[]{:S(2)}, u32[]{:S(2)}) collective-permute-start(f32[2,32]{1,0:T(2,128)S(1)} %pad_maximum_fusion.3), channel_id=1, source_target_pairs={{64,0},{96,32},{128,64},{160,96},{192,128},{224,160},{0,192},{32,2... | collective-permute-start | bytes 776 | tf_op jit(solution)/shard_map/ppermute | solution.py:326
  98.8 0.1 copy.25
  98.9 0.1 cos.20
  99.0 0.1 copy.24
  99.1 0.4 collective-permute-done.1
  99.5 2.0 %collective-permute-start.2 = (f32[4,32]{1,0:T(4,128)S(1)}, f32[4,32]{1,0:T(4,128)S(1)}, u32[]{:S(2)}, u32[]{:S(2)}) collective-permute-start(f32[4,32]{1,0:T(4,128)S(1)} %pad_maximum_fusion.2), channel_id=1, source_target_pairs={{128,0},{160,32},{192,64},{224,96},{0,128},{32,160},{64,192},{96,2... | collective-permute-start | bytes 1544 | tf_op jit(solution)/shard_map/ppermute | solution.py:326
  101.5 2.5 %collective-permute-done.2 = f32[4,32]{1,0:T(4,128)S(1)} collective-permute-done((f32[4,32]{1,0:T(4,128)S(1)}, f32[4,32]{1,0:T(4,128)S(1)}, u32[]{:S(2)}, u32[]{:S(2)}) %collective-permute-start.2) | collective-permute-done | bytes 544 | tf_op jit(solution)/shard_map/ppermute | solution.py:326
  104.2 0.1 pad_maximum_fusion.1
  104.2 18.6 %all-to-all-done.1 = f32[256,8,128]{2,1,0:T(8,128)S(1)} async-done(((f32[256,8,128]{2,1,0:T(8,128)}), f32[256,8,128]{2,1,0:T(8,128)S(1)}, u32[]{:S(2)}, u32[]{:S(2)}) %all-to-all-start.1) | async-done | bytes 1048608 | tf_op jit(solution)/shard_map/all_to_all | solution.py:370
  122.9 3.4 %spectral.1 = f32[8,256,128]{2,1,0:T(8,128)S(1)} custom-call(f32[8,32,8,128]{3,2,1,0:T(8,128)S(1)} %bitcast.14, f32[8,1,8,128]{3,2,1,0:T(8,128)S(1)} %broadcast_in_dim.5.l_ref, f32[2,128,128]{2,1,0:T(8,128)S(1)} %pad_maximum_fusion.ph_ref, bf16[2,256,256]{2,1,0:T(8,128)(2,1)S(1)} %copy-done.1, bf16[2,256,256]{2,1,0:T(8,128)(2,1)S(1)} %copy-done.2, ...), custom_call_target="tpu_custom_call" | custom-call | flops 3000000000 | bytes 4194304 | tf_op jit(solution)/shard_map/spectral/pallas_call | solution.py:308
  126.3 18.4 %all_to_all.15 = f32[8,256,128]{2,1,0:T(8,128)S(1)} all-to-all(f32[8,256,128]{2,1,0:T(8,128)S(1)} %spectral.1), channel_id=1, replica_groups=mesh['gz'=8,'ma'=32] {'gz'}, dimensions={0} | all-to-all | bytes 2097152 | tf_op jit(solution)/shard_map/all_to_all | solution.py:378
  144.7 0.2 copy.26
  145.0 1.2 reshape.52
  (34 shorter events, 0.3 us)
Async XLA Ops:
  2.6 12.2 %copy-start.10 = (s32[128,128]{1,0:T(8,128)S(1)}, s32[128,128]{1,0:T(8,128)}, u32[]{:S(2)}) copy-start(s32[128,128]{1,0:T(8,128)} %param.19) | copy-start | bytes 196612
  2.6 12.2 %copy-start.12 = (f32[8]{0:T(128)S(1)}, f32[8]{0:T(128)}, u32[]{:S(2)}) copy-start(f32[8]{0:T(128)} %param.20) | copy-start | bytes 100
  2.6 12.5 %copy-start = (s32[1024]{0:T(1024)S(1)}, s32[1024]{0:T(1024)}, u32[]{:S(2)}) copy-start(s32[1024]{0:T(1024)} %param.18) | copy-start | bytes 12292
  2.6 60.6 %all-to-all-start = ((f32[32,4,32,128]{3,2,1,0:T(8,128)}), f32[32,4,32,128]{3,2,1,0:T(8,128)S(1)}, u32[]{:S(2)}, u32[]{:S(2)}) async-start(f32[32,4,32,128]{3,2,1,0:T(8,128)} %pack.1), calls=%async_computation | async-start | bytes 4194304 | tf_op jit(solution)/shard_map/all_to_all | solution.py:366
  14.8 48.5 %copy-start.5 = (bf16[2,128,512]{2,1,0:T(8,128)(2,1)S(1)}, bf16[2,128,512]{2,1,0:T(8,128)(2,1)}, u32[]{:S(2)}) copy-start(bf16[2,128,512]{2,1,0:T(8,128)(2,1)} %constant.53.clone.proj_hbm) | copy-start | bytes 786436
  14.8 48.4 %copy-start.6 = (bf16[256,192]{1,0:T(8,128)(2,1)S(1)}, bf16[256,192]{1,0:T(8,128)(2,1)}, u32[]{:S(2)}) copy-start(bf16[256,192]{1,0:T(8,128)(2,1)} %constant.51.clone.f2_ref) | copy-start | bytes 294916
  14.8 48.4 %copy-start.7 = (bf16[256,192]{1,0:T(8,128)(2,1)S(1)}, bf16[256,192]{1,0:T(8,128)(2,1)}, u32[]{:S(2)}) copy-start(bf16[256,192]{1,0:T(8,128)(2,1)} %constant.52.clone.f3_ref) | copy-start | bytes 294916
  14.9 48.4 %copy-start.9 = (f32[32,128]{1,0:T(8,128)S(1)}, f32[32,128]{1,0:T(8,128)}, u32[]{:S(2)}) copy-start(f32[32,128]{1,0:T(8,128)} %constant.54.clone.tt_ref) | copy-start | bytes 49156
  80.3 11.3 %copy-start.11 = (f32[1,32]{1,0:T(1,128)S(1)}, f32[1,32]{1,0:T(1,128)}, u32[]{:S(2)}) copy-start(f32[1,32]{1,0:T(1,128)} %param.22) | copy-start | bytes 388
  80.3 42.6 %copy-start.1 = (bf16[2,256,256]{2,1,0:T(8,128)(2,1)S(1)}, bf16[2,256,256]{2,1,0:T(8,128)(2,1)}, u32[]{:S(2)}) copy-start(bf16[2,256,256]{2,1,0:T(8,128)(2,1)} %constant.55.clone.w1_ref) | copy-start | bytes 786436
  80.3 42.6 %copy-start.2 = (bf16[2,256,256]{2,1,0:T(8,128)(2,1)S(1)}, bf16[2,256,256]{2,1,0:T(8,128)(2,1)}, u32[]{:S(2)}) copy-start(bf16[2,256,256]{2,1,0:T(8,128)(2,1)} %constant.56.clone.w2_ref) | copy-start | bytes 786436
  80.3 42.6 %copy-start.3 = (bf16[2,256,256]{2,1,0:T(8,128)(2,1)S(1)}, bf16[2,256,256]{2,1,0:T(8,128)(2,1)}, u32[]{:S(2)}) copy-start(bf16[2,256,256]{2,1,0:T(8,128)(2,1)} %constant.57.clone.w3_ref) | copy-start | bytes 786436
  80.3 42.6 %copy-start.4 = (bf16[2,256,256]{2,1,0:T(8,128)(2,1)S(1)}, bf16[2,256,256]{2,1,0:T(8,128)(2,1)}, u32[]{:S(2)}) copy-start(bf16[2,256,256]{2,1,0:T(8,128)(2,1)} %constant.58.clone.w4_ref) | copy-start | bytes 786436
  80.3 42.6 %copy-start.8 = (f32[2,32,128]{2,1,0:T(8,128)S(1)}, f32[2,32,128]{2,1,0:T(8,128)}, u32[]{:S(2)}) copy-start(f32[2,32,128]{2,1,0:T(8,128)} %constant.59.clone.tw_ref) | copy-start | bytes 98308
  80.3 42.5 %all-to-all-start.1 = ((f32[256,8,128]{2,1,0:T(8,128)}), f32[256,8,128]{2,1,0:T(8,128)S(1)}, u32[]{:S(2)}, u32[]{:S(2)}) async-start(f32[256,8,128]{2,1,0:T(8,128)} %bitcast.2), calls=%async_computation.1 | async-start | bytes 2097152 | tf_op jit(solution)/shard_map/all_to_all | solution.py:370
  91.6 3.7 %collective-permute-start = (f32[1,32]{1,0:T(1,128)S(1)}, f32[1,32]{1,0:T(1,128)S(1)}, u32[]{:S(2)}, u32[]{:S(2)}) collective-permute-start(f32[1,32]{1,0:T(1,128)S(1)} %copy-done.11), channel_id=1, source_target_pairs={{32,0},{64,32},{96,64},{128,96},{160,128},{192,160},{224,192},{0,2... | collective-permute-start | bytes 392 | tf_op jit(solution)/shard_map/ppermute | solution.py:326
  95.3 4.2 %collective-permute-start.1 = (f32[2,32]{1,0:T(2,128)S(1)}, f32[2,32]{1,0:T(2,128)S(1)}, u32[]{:S(2)}, u32[]{:S(2)}) collective-permute-start(f32[2,32]{1,0:T(2,128)S(1)} %pad_maximum_fusion.3), channel_id=1, source_target_pairs={{64,0},{96,32},{128,64},{160,96},{192,128},{224,160},{0,192},{32,2... | collective-permute-start | bytes 776 | tf_op jit(solution)/shard_map/ppermute | solution.py:326
  99.5 4.5 %collective-permute-start.2 = (f32[4,32]{1,0:T(4,128)S(1)}, f32[4,32]{1,0:T(4,128)S(1)}, u32[]{:S(2)}, u32[]{:S(2)}) collective-permute-start(f32[4,32]{1,0:T(4,128)S(1)} %pad_maximum_fusion.2), channel_id=1, source_target_pairs={{128,0},{160,32},{192,64},{224,96},{0,128},{32,160},{64,192},{96,2... | collective-permute-start | bytes 1544 | tf_op jit(solution)/shard_map/ppermute | solution.py:326

commit v9 on v8

--- a/solution.py
+++ b/solution.py
@@ -181,7 +181,7 @@
         return carry
 
     loads[0].wait()
-    lax.fori_loop(0, 8, last, 0, unroll=4)
+    lax.fori_loop(0, 8, last, 0, unroll=8)
 
     def store(j):
         part = pl.ds(j * 8, 8)
@@ -200,7 +200,7 @@
         return carry
 
     loads[1].wait()
-    lax.fori_loop(0, 4, finish, 0, unroll=2)
+    lax.fori_loop(0, 4, finish, 0, unroll=4)
     for j in range(4):
         store(j).wait()
 

time: 146 us -> 146 us (level)
  no operation moved by 1% of the time
where the time goes in v9:
time: 146 us
  waiting for transfers between devices  67.9 us (47%)
  starting transfers between devices  31 us (21%)
  Pallas kernels  22.6 us (15%)
  blocking collectives  18.4 us (13%)
  other arithmetic  3.34 us (2%)
  local copies, waits for them, and re-layouts  2.18 us (1%)
    all_to_all x1, waiting for transfers between devices, on_device(): lax.all_to_all(send, 'ma', split_axis=0, concat_axis=0, tiled=True)  46.4 us
    all_to_all x1, waiting for transfers between devices, on_device(): lax.all_to_all(source, ('gz', 'ma'), split_axis=0, concat_axis=0, tiled=T...  18.6 us
    all_to_all x1, blocking collectives, on_device(): lax.all_to_all(result, 'gz', split_axis=0, concat_axis=0, tiled=True)  18.4 us
    pallas_call x1, Pallas kernels, kerr_call(): pl.pallas_call(kerr_kernel, name='kerr', out_shape=jax.ShapeDtypeStruct((...  16.6 us
    all_to_all x1, starting transfers between devices, on_device(): lax.all_to_all(send, 'ma', split_axis=0, concat_axis=0, tiled=True)  12.2 us
    all_to_all x1, starting transfers between devices, on_device(): lax.all_to_all(source, ('gz', 'ma'), split_axis=0, concat_axis=0, tiled=T...  11.3 us
    ppermute x3, starting transfers between devices, gathered_loss(): have = jnp.concatenate([have, lax.ppermute(have, 'gz', route)], axis=0)  7.6 us
    pallas_call x1, Pallas kernels, spectral_call(): pl.pallas_call(spectral_kernel, name='spectral', out_shape=jax.ShapeDtype...  3.39 us
  transfers between devices with their start and end apart: 5, of which 4 were waited for; matrix products, arithmetic and copies ran while one was open for 3% of the time, Pallas kernels for 0%

profile of v9, /device:TPU:1, one launch (start us, length us, event | category | flops | bytes accessed | tf_op | source)
XLA Modules:
  0.0 145.7 jit_solution(6213036826976414145)
XLA Ops:
  0.0 2.6 %pack.1 = f32[32,4,32,128]{3,2,1,0:T(8,128)} custom-call(f32[1,2,32,4096]{3,2,1,0:T(8,128)} %f_ref.1, f32[1,2,32,4096]{3,2,1,0:T(8,128)} %c_ref.1), custom_call_target="tpu_custom_call" | custom-call | flops 1048576 | bytes 4194304 | tf_op jit(solution)/shard_map/pack/pallas_call | solution.py:62
  2.6 12.2 %all-to-all-start = ((f32[32,4,32,128]{3,2,1,0:T(8,128)}), f32[32,4,32,128]{3,2,1,0:T(8,128)S(1)}, u32[]{:S(2)}, u32[]{:S(2)}) async-start(f32[32,4,32,128]{3,2,1,0:T(8,128)} %pack.1), calls=%async_computation | async-start | bytes 4194304 | tf_op jit(solution)/shard_map/all_to_all | solution.py:366
  14.9 0.1 select_reduce_fusion
  15.0 0.1 copy.23
  15.1 1.7 %fusion.back_hbm = bf16[1024,1024]{1,0:T(8,128)(2,1)} fusion(s32[1024]{0:T(1024)S(1)} %copy-done), kind=kLoop, calls=%fused_computation.1 | loop fusion | flops 2097152 | bytes 2101248 | tf_op jit(solution)/shard_map/convert_element_type | solution.py:359
  16.8 46.4 %all-to-all-done.x_ref = f32[32,4,32,128]{3,2,1,0:T(8,128)S(1)} async-done(((f32[32,4,32,128]{3,2,1,0:T(8,128)}), f32[32,4,32,128]{3,2,1,0:T(8,128)S(1)}, u32[]{:S(2)}, u32[]{:S(2)}) %all-to-all-start) | async-done | bytes 2097184 | tf_op jit(solution)/shard_map/all_to_all | solution.py:366
  63.3 16.6 %kerr.1 = f32[8,32,8,128]{3,2,1,0:T(8,128)} custom-call(f32[32,4,32,128]{3,2,1,0:T(8,128)S(1)} %all-to-all-done.x_ref, s32[1,1024]{1,0:T(1,128)S(1)} %bitcast.15, bf16[1024,1024]{1,0:T(8,128)(2,1)} %fusion.back_hbm, bf16[256,192]{1,0:T(8,128)(2,1)S(1)} %copy-done.6, bf16[256,192]{1,0:T(8,128)(2,1)S(1)} %copy-done.7, bf16[2,128,512]{2,1,0:T(8,128)(2,1)S(1)} %copy-done.5, ...), custom_call_target="tpu_custom_call" | custom-call | flops 20000000000 | bytes 8388608 | tf_op jit(solution)/shard_map/kerr/pallas_call | solution.py:211
  80.0 11.3 %all-to-all-start.1 = ((f32[256,8,128]{2,1,0:T(8,128)}), f32[256,8,128]{2,1,0:T(8,128)S(1)}, u32[]{:S(2)}, u32[]{:S(2)}) async-start(f32[256,8,128]{2,1,0:T(8,128)} %bitcast.2), calls=%async_computation.1 | async-start | bytes 2097152 | tf_op jit(solution)/shard_map/all_to_all | solution.py:370
  91.2 2.2 %collective-permute-start = (f32[1,32]{1,0:T(1,128)S(1)}, f32[1,32]{1,0:T(1,128)S(1)}, u32[]{:S(2)}, u32[]{:S(2)}) collective-permute-start(f32[1,32]{1,0:T(1,128)S(1)} %copy-done.11), channel_id=1, source_target_pairs={{32,0},{64,32},{96,64},{128,96},{160,128},{192,160},{224,192},{0,2... | collective-permute-start | bytes 392 | tf_op jit(solution)/shard_map/ppermute | solution.py:326
  93.4 1.4 dynamic-slice_cosine_fusion
  94.8 0.1 neg.20
  94.9 3.5 %collective-permute-start.1 = (f32[2,32]{1,0:T(2,128)S(1)}, f32[2,32]{1,0:T(2,128)S(1)}, u32[]{:S(2)}, u32[]{:S(2)}) collective-permute-start(f32[2,32]{1,0:T(2,128)S(1)} %pad_maximum_fusion.3), channel_id=1, source_target_pairs={{64,0},{96,32},{128,64},{160,96},{192,128},{224,160},{0,192},{32,2... | collective-permute-start | bytes 776 | tf_op jit(solution)/shard_map/ppermute | solution.py:326
  98.4 0.1 copy.25
  98.5 0.1 cos.20
  98.6 0.1 copy.24
  98.7 0.4 collective-permute-done.1
  99.1 2.0 %collective-permute-start.2 = (f32[4,32]{1,0:T(4,128)S(1)}, f32[4,32]{1,0:T(4,128)S(1)}, u32[]{:S(2)}, u32[]{:S(2)}) collective-permute-start(f32[4,32]{1,0:T(4,128)S(1)} %pad_maximum_fusion.2), channel_id=1, source_target_pairs={{128,0},{160,32},{192,64},{224,96},{0,128},{32,160},{64,192},{96,2... | collective-permute-start | bytes 1544 | tf_op jit(solution)/shard_map/ppermute | solution.py:326
  101.2 2.5 %collective-permute-done.2 = f32[4,32]{1,0:T(4,128)S(1)} collective-permute-done((f32[4,32]{1,0:T(4,128)S(1)}, f32[4,32]{1,0:T(4,128)S(1)}, u32[]{:S(2)}, u32[]{:S(2)}) %collective-permute-start.2) | collective-permute-done | bytes 544 | tf_op jit(solution)/shard_map/ppermute | solution.py:326
  103.8 0.1 pad_maximum_fusion.1
  103.9 18.6 %all-to-all-done.1 = f32[256,8,128]{2,1,0:T(8,128)S(1)} async-done(((f32[256,8,128]{2,1,0:T(8,128)}), f32[256,8,128]{2,1,0:T(8,128)S(1)}, u32[]{:S(2)}, u32[]{:S(2)}) %all-to-all-start.1) | async-done | bytes 1048608 | tf_op jit(solution)/shard_map/all_to_all | solution.py:370
  122.6 3.4 %spectral.1 = f32[8,256,128]{2,1,0:T(8,128)S(1)} custom-call(f32[8,32,8,128]{3,2,1,0:T(8,128)S(1)} %bitcast.14, f32[8,1,8,128]{3,2,1,0:T(8,128)S(1)} %broadcast_in_dim.5.l_ref, f32[2,128,128]{2,1,0:T(8,128)S(1)} %pad_maximum_fusion.ph_ref, bf16[2,256,256]{2,1,0:T(8,128)(2,1)S(1)} %copy-done.1, bf16[2,256,256]{2,1,0:T(8,128)(2,1)S(1)} %copy-done.2, ...), custom_call_target="tpu_custom_call" | custom-call | flops 3000000000 | bytes 4194304 | tf_op jit(solution)/shard_map/spectral/pallas_call | solution.py:308
  126.0 18.4 %all_to_all.15 = f32[8,256,128]{2,1,0:T(8,128)S(1)} all-to-all(f32[8,256,128]{2,1,0:T(8,128)S(1)} %spectral.1), channel_id=1, replica_groups=mesh['gz'=8,'ma'=32] {'gz'}, dimensions={0} | all-to-all | bytes 2097152 | tf_op jit(solution)/shard_map/all_to_all | solution.py:378
  144.4 0.2 copy.26
  144.6 1.2 reshape.52
  (34 shorter events, 0.3 us)
Async XLA Ops:
  2.6 12.2 %copy-start.10 = (s32[128,128]{1,0:T(8,128)S(1)}, s32[128,128]{1,0:T(8,128)}, u32[]{:S(2)}) copy-start(s32[128,128]{1,0:T(8,128)} %param.19) | copy-start | bytes 196612
  2.6 12.2 %copy-start.12 = (f32[8]{0:T(128)S(1)}, f32[8]{0:T(128)}, u32[]{:S(2)}) copy-start(f32[8]{0:T(128)} %param.20) | copy-start | bytes 100
  2.6 12.5 %copy-start = (s32[1024]{0:T(1024)S(1)}, s32[1024]{0:T(1024)}, u32[]{:S(2)}) copy-start(s32[1024]{0:T(1024)} %param.18) | copy-start | bytes 12292
  2.6 60.6 %all-to-all-start = ((f32[32,4,32,128]{3,2,1,0:T(8,128)}), f32[32,4,32,128]{3,2,1,0:T(8,128)S(1)}, u32[]{:S(2)}, u32[]{:S(2)}) async-start(f32[32,4,32,128]{3,2,1,0:T(8,128)} %pack.1), calls=%async_computation | async-start | bytes 4194304 | tf_op jit(solution)/shard_map/all_to_all | solution.py:366
  14.8 48.5 %copy-start.5 = (bf16[2,128,512]{2,1,0:T(8,128)(2,1)S(1)}, bf16[2,128,512]{2,1,0:T(8,128)(2,1)}, u32[]{:S(2)}) copy-start(bf16[2,128,512]{2,1,0:T(8,128)(2,1)} %constant.53.clone.proj_hbm) | copy-start | bytes 786436
  14.8 48.4 %copy-start.6 = (bf16[256,192]{1,0:T(8,128)(2,1)S(1)}, bf16[256,192]{1,0:T(8,128)(2,1)}, u32[]{:S(2)}) copy-start(bf16[256,192]{1,0:T(8,128)(2,1)} %constant.51.clone.f2_ref) | copy-start | bytes 294916
  14.8 48.4 %copy-start.7 = (bf16[256,192]{1,0:T(8,128)(2,1)S(1)}, bf16[256,192]{1,0:T(8,128)(2,1)}, u32[]{:S(2)}) copy-start(bf16[256,192]{1,0:T(8,128)(2,1)} %constant.52.clone.f3_ref) | copy-start | bytes 294916
  14.9 48.4 %copy-start.9 = (f32[32,128]{1,0:T(8,128)S(1)}, f32[32,128]{1,0:T(8,128)}, u32[]{:S(2)}) copy-start(f32[32,128]{1,0:T(8,128)} %constant.54.clone.tt_ref) | copy-start | bytes 49156
  79.9 11.4 %copy-start.11 = (f32[1,32]{1,0:T(1,128)S(1)}, f32[1,32]{1,0:T(1,128)}, u32[]{:S(2)}) copy-start(f32[1,32]{1,0:T(1,128)} %param.22) | copy-start | bytes 388
  79.9 42.6 %copy-start.1 = (bf16[2,256,256]{2,1,0:T(8,128)(2,1)S(1)}, bf16[2,256,256]{2,1,0:T(8,128)(2,1)}, u32[]{:S(2)}) copy-start(bf16[2,256,256]{2,1,0:T(8,128)(2,1)} %constant.55.clone.w1_ref) | copy-start | bytes 786436
  79.9 42.6 %copy-start.2 = (bf16[2,256,256]{2,1,0:T(8,128)(2,1)S(1)}, bf16[2,256,256]{2,1,0:T(8,128)(2,1)}, u32[]{:S(2)}) copy-start(bf16[2,256,256]{2,1,0:T(8,128)(2,1)} %constant.56.clone.w2_ref) | copy-start | bytes 786436
  79.9 42.6 %copy-start.3 = (bf16[2,256,256]{2,1,0:T(8,128)(2,1)S(1)}, bf16[2,256,256]{2,1,0:T(8,128)(2,1)}, u32[]{:S(2)}) copy-start(bf16[2,256,256]{2,1,0:T(8,128)(2,1)} %constant.57.clone.w3_ref) | copy-start | bytes 786436
  79.9 42.6 %copy-start.4 = (bf16[2,256,256]{2,1,0:T(8,128)(2,1)S(1)}, bf16[2,256,256]{2,1,0:T(8,128)(2,1)}, u32[]{:S(2)}) copy-start(bf16[2,256,256]{2,1,0:T(8,128)(2,1)} %constant.58.clone.w4_ref) | copy-start | bytes 786436
  80.0 42.6 %copy-start.8 = (f32[2,32,128]{2,1,0:T(8,128)S(1)}, f32[2,32,128]{2,1,0:T(8,128)}, u32[]{:S(2)}) copy-start(f32[2,32,128]{2,1,0:T(8,128)} %constant.59.clone.tw_ref) | copy-start | bytes 98308
  80.0 42.5 %all-to-all-start.1 = ((f32[256,8,128]{2,1,0:T(8,128)}), f32[256,8,128]{2,1,0:T(8,128)S(1)}, u32[]{:S(2)}, u32[]{:S(2)}) async-start(f32[256,8,128]{2,1,0:T(8,128)} %bitcast.2), calls=%async_computation.1 | async-start | bytes 2097152 | tf_op jit(solution)/shard_map/all_to_all | solution.py:370
  91.2 3.7 %collective-permute-start = (f32[1,32]{1,0:T(1,128)S(1)}, f32[1,32]{1,0:T(1,128)S(1)}, u32[]{:S(2)}, u32[]{:S(2)}) collective-permute-start(f32[1,32]{1,0:T(1,128)S(1)} %copy-done.11), channel_id=1, source_target_pairs={{32,0},{64,32},{96,64},{128,96},{160,128},{192,160},{224,192},{0,2... | collective-permute-start | bytes 392 | tf_op jit(solution)/shard_map/ppermute | solution.py:326
  94.9 4.2 %collective-permute-start.1 = (f32[2,32]{1,0:T(2,128)S(1)}, f32[2,32]{1,0:T(2,128)S(1)}, u32[]{:S(2)}, u32[]{:S(2)}) collective-permute-start(f32[2,32]{1,0:T(2,128)S(1)} %pad_maximum_fusion.3), channel_id=1, source_target_pairs={{64,0},{96,32},{128,64},{160,96},{192,128},{224,160},{0,192},{32,2... | collective-permute-start | bytes 776 | tf_op jit(solution)/shard_map/ppermute | solution.py:326
  99.1 4.5 %collective-permute-start.2 = (f32[4,32]{1,0:T(4,128)S(1)}, f32[4,32]{1,0:T(4,128)S(1)}, u32[]{:S(2)}, u32[]{:S(2)}) collective-permute-start(f32[4,32]{1,0:T(4,128)S(1)} %pad_maximum_fusion.2), channel_id=1, source_target_pairs={{128,0},{160,32},{192,64},{224,96},{0,128},{32,160},{64,192},{96,2... | collective-permute-start | bytes 1544 | tf_op jit(solution)/shard_map/ppermute | solution.py:326
